TPU v7x, 32 devices: a whole 2x2x4 slice. The times are simulated.
32 devices in a mesh: ctx: 8 (over y, x, core), head: 4 (over z).
Axes of the slice: x: 2, y: 2, z: 4, core: 2. Of those that a mesh axis runs over, the one named last changes fastest.
Arguments:
- queries: bfloat16 [8192, 6144], P(('ctx', 'head')), may hold values from -56 to 56
- key_rows: bfloat16 [8192, 6144], P(('ctx', 'head')), may hold values from -6 to 6
- value_rows: bfloat16 [8192, 6144], P(('ctx', 'head')), may hold values from -6 to 6
- key_tiles: int32 [48, 64, 18], P('head', 'ctx'), may hold values from -1 to 63, as said below
Outputs:
- attended: bfloat16 [8192, 6144], P(('ctx', 'head'))
Inputs may be any that keep to these rules, and one draw needn't show every extreme that they name: In key_tiles[h, i] the live slots come first and name distinct tiles whose time slab differs from tile i's by at most one; the rest hold -1. Tile i itself and the tiles of the same cell one time slab before and after (where they exist) are always live. In every draw some head and tile have all 18 slots live.
All inputs are finite; a program needn't handle non-finite values.
Results may differ from a plain program's by a relative error of at most 0.0046.
Values may be sent and summed in bfloat16 or wider, within the bound.
No kernel may reach another device: no remote copies, remote signals or barrier semaphores. Data moves between devices by JAX's collectives and lax.ppermute only.
A program may use at most 128 MiB of HBM per device.

v0:
```python
import functools

import jax
import jax.numpy as jnp
from jax import lax
from jax.experimental import pallas as pl
from jax.experimental.pallas import tpu as pltpu
from jax.sharding import PartitionSpec as P


HDIM = 128
TILE = 128
LOG2E = 1.4426950408889634
DEAD = 1e30
CHUNK_HEADS = 3
AHEAD = 2
VMEM_LIMIT = 67043328


HBM = pl.BlockSpec(memory_space=pl.ANY)
SMEM = pl.BlockSpec(memory_space=pltpu.SMEM)


def run_copies(copies):
    for copy in copies:
        copy.start()
    for copy in copies:
        copy.wait()


def head_columns(first_head, width):
    return pl.ds(pl.multiple_of(first_head * HDIM, HDIM), width)


def params():
    return pltpu.CompilerParams(vmem_limit_bytes=VMEM_LIMIT)


def pack_body(peers, heads_dev, chunks, place, *refs):
    sends = len(chunks) * (peers - 1)
    arrays, outs, held, (in_sems, out_sems) = refs[:3], refs[3 : 3 + sends], refs[3 + sends : -2], refs[-2:]
    me = place[0]
    loads = []
    for index, (first, group) in enumerate(chunks):
        for shift in range(1, peers):
            columns = head_columns(lax.rem(me + shift, peers) * heads_dev + first, group * HDIM)
            slot = index * (peers - 1) + shift - 1
            loads.append(
                [
                    pltpu.make_async_copy(
                        array.at[:, columns], held[index].at[shift - 1, which], in_sems.at[slot, which]
                    )
                    for which, array in enumerate(arrays)
                ]
            )
    for copies in loads:
        for copy in copies:
            copy.start()
    stores = []
    for slot, copies in enumerate(loads):
        for copy in copies:
            copy.wait()
        index, shift = divmod(slot, peers - 1)
        store = pltpu.make_async_copy(held[index].at[shift], outs[slot], out_sems.at[slot])
        store.start()
        stores.append(store)
    for store in stores:
        store.wait()


def pack(place, arrays, peers, heads_dev, chunks):
    rows = arrays[0].shape[0]
    outs = [
        jax.ShapeDtypeStruct((3, rows, group * HDIM), jnp.bfloat16) for _, group in chunks for _ in range(peers - 1)
    ]
    moved = sum(3 * (peers - 1) * rows * group * HDIM * 2 for _, group in chunks)
    results = pl.pallas_call(
        functools.partial(pack_body, peers, heads_dev, chunks),
        out_shape=outs,
        in_specs=[SMEM] + [HBM] * 3,
        out_specs=[HBM] * len(outs),
        scratch_shapes=[pltpu.VMEM((peers - 1, 3, rows, group * HDIM), jnp.bfloat16) for _, group in chunks]
        + [
            pltpu.SemaphoreType.DMA((len(outs), 3)),
            pltpu.SemaphoreType.DMA((len(outs),)),
        ],
        cost_estimate=pl.CostEstimate(flops=0, bytes_accessed=2 * moved, transcendentals=0),
        compiler_params=params(),
        name="pack",
    )(place, *arrays)
    return [results[i : i + peers - 1] for i in range(0, len(outs), peers - 1)]


def join_body(peers, heads_dev, first, width, place, key_rows, value_rows, *refs):
    pieces, (out, held, in_sems, out_sem) = refs[: peers - 1], refs[peers - 1 :]
    me = place[0]
    rows = key_rows.shape[0]
    own = head_columns(me * heads_dev + first, width)
    loads = []
    for which, array in enumerate((key_rows, value_rows)):
        loads.append(
            pltpu.make_async_copy(
                array.at[:, own], held.at[which, pl.ds(pl.multiple_of(me * rows, rows), rows)], in_sems.at[0, which]
            )
        )
        for shift in range(1, peers):
            source = lax.rem(me + peers - shift, peers)
            loads.append(
                pltpu.make_async_copy(
                    pieces[shift - 1].at[1 + which],
                    held.at[which, pl.ds(pl.multiple_of(source * rows, rows), rows)],
                    in_sems.at[shift, which],
                )
            )
    run_copies(loads)
    run_copies([pltpu.make_async_copy(held, out, out_sem)])


def join(place, key_rows, value_rows, pieces, heads_dev, first, width):
    peers = len(pieces) + 1
    rows = key_rows.shape[0]
    shape = (2, peers * rows, width)
    return pl.pallas_call(
        functools.partial(join_body, peers, heads_dev, first, width),
        out_shape=jax.ShapeDtypeStruct(shape, jnp.bfloat16),
        in_specs=[SMEM] + [HBM] * (2 + peers - 1),
        out_specs=HBM,
        scratch_shapes=[
            pltpu.VMEM(shape, jnp.bfloat16),
            pltpu.SemaphoreType.DMA((peers, 2)),
            pltpu.SemaphoreType.DMA,
        ],
        cost_estimate=pl.CostEstimate(flops=0, bytes_accessed=4 * peers * rows * width * 2, transcendentals=0),
        compiler_params=params(),
        name="join",
    )(place, key_rows, value_rows, *pieces)


def attend_body(peers, heads_dev, first, group, slots, place, tiles, queries, *refs):
    pieces, refs = refs[: peers - 1], refs[peers - 1 :]
    sides, refs = refs[:3], refs[3:]
    outs, refs = refs[:peers], refs[peers:]
    q_held, kv_held, o_held, scores, peak, total, sums, q_sems, kv_sems, o_sems = refs
    me = place[0]
    rows = queries.shape[0]
    block = peers * rows
    q_tiles = block // TILE
    pairs = (slots + 1) // 2
    entries = 2 * pairs + 1

    loads = []
    for head in range(group):
        lanes = pl.ds(head * HDIM, HDIM)
        copies = [
            pltpu.make_async_copy(
                queries.at[:, head_columns(me * heads_dev + first + head, HDIM)],
                q_held.at[head, pl.ds(pl.multiple_of(me * rows, rows), rows)],
                q_sems.at[head, 0],
            )
        ]
        for shift in range(1, peers):
            source = lax.rem(me + peers - shift, peers)
            copies.append(
                pltpu.make_async_copy(
                    pieces[shift - 1].at[0, :, lanes],
                    q_held.at[head, pl.ds(pl.multiple_of(source * rows, rows), rows)],
                    q_sems.at[head, shift],
                )
            )
        for which in range(2):
            for side in range(3):
                copies.append(
                    pltpu.make_async_copy(
                        sides[side].at[which, :, lanes],
                        kv_held.at[head, which, pl.ds(side * block, block)],
                        kv_sems.at[head, which, side],
                    )
                )
        loads.append((copies[: peers + 3], copies[peers + 3 :]))
    for early, late in loads:
        for copy in early + late:
            copy.start()

    factor = HDIM ** (-0.5) * LOG2E
    stores = []
    for head in range(group):
        lanes = pl.ds(head * HDIM, HDIM)

        def listed(tile, slot):
            return tiles[head, tile * entries + 1 + slot]

        def live(tile):
            return tiles[head, tile * entries]

        def gathered(which, tile, pair):
            return jnp.concatenate(
                [
                    kv_held[head, which, pl.ds(pl.multiple_of(listed(tile, 2 * pair + half) * TILE, TILE), TILE)]
                    for half in range(2)
                ],
                axis=0,
            )

        longest = live(0)
        for tile in range(1, q_tiles):
            longest = jnp.maximum(longest, live(tile))
        steps = (longest + 1) // 2

        peak[...] = jnp.full_like(peak, -jnp.inf)
        total[...] = jnp.zeros_like(total)
        sums[...] = jnp.zeros_like(sums)
        for copy in loads[head][0]:
            copy.wait()

        @pl.loop(0, steps)
        def _(pair):
            for tile in range(q_tiles):
                at = pl.ds(tile * TILE, TILE)
                score = lax.dot_general(
                    q_held[head, at],
                    gathered(0, tile, pair),
                    (((1,), (1,)), ((), ())),
                    preferred_element_type=jnp.float32,
                )
                scores[pair, at] = score
                peak[at] = jnp.maximum(peak[at], jnp.maximum(score[:, :TILE], score[:, TILE:]))

        for tile in range(q_tiles):
            at = pl.ds(tile * TILE, TILE)
            top = jnp.max(peak[at], axis=1, keepdims=True) * factor
            peak[at] = jnp.broadcast_to(top, (TILE, TILE))
        for copy in loads[head][1]:
            copy.wait()

        @pl.loop(0, steps)
        def _(pair):
            for tile in range(q_tiles):
                at = pl.ds(tile * TILE, TILE)
                top = peak[at]
                parts = []
                for half in range(2):
                    base = jnp.where(2 * pair + half < live(tile), top, DEAD)
                    parts.append(
                        jnp.exp2(scores[pair, at, pl.ds(half * TILE, TILE)] * factor - base)
                    )
                total[at] += parts[0] + parts[1]
                weight = jnp.concatenate(parts, axis=1).astype(jnp.bfloat16)
                sums[at] += jnp.dot(
                    weight, gathered(1, tile, pair), preferred_element_type=jnp.float32
                )

        for tile in range(q_tiles):
            at = pl.ds(tile * TILE, TILE)
            row_total = jnp.sum(total[at], axis=1, keepdims=True)
            o_held[head, at] = (sums[at] / row_total).astype(jnp.bfloat16)
        for shift in range(peers):
            target = lax.rem(me + shift, peers)
            store = pltpu.make_async_copy(
                o_held.at[head, pl.ds(pl.multiple_of(target * rows, rows), rows)],
                outs[shift].at[:, lanes],
                o_sems.at[head, shift],
            )
            store.start()
            stores.append(store)
    for store in stores:
        store.wait()


def attend(place, tiles, queries, pieces, sides, heads_dev, first, group, slots):
    peers = len(pieces) + 1
    rows = queries.shape[0]
    block = peers * rows
    width = group * HDIM
    pairs = (slots + 1) // 2
    work = group * block * slots * TILE
    return pl.pallas_call(
        functools.partial(attend_body, peers, heads_dev, first, group, slots),
        out_shape=[jax.ShapeDtypeStruct((rows, width), jnp.bfloat16)] * peers,
        in_specs=[SMEM, SMEM] + [HBM] * (1 + peers - 1 + 3),
        out_specs=[HBM] * peers,
        scratch_shapes=[
            pltpu.VMEM((group, block, HDIM), jnp.bfloat16),
            pltpu.VMEM((group, 2, 3 * block, HDIM), jnp.bfloat16),
            pltpu.VMEM((group, block, HDIM), jnp.bfloat16),
            pltpu.VMEM((pairs, block, 2 * TILE), jnp.float32),
            pltpu.VMEM((block, TILE), jnp.float32),
            pltpu.VMEM((block, TILE), jnp.float32),
            pltpu.VMEM((block, HDIM), jnp.float32),
            pltpu.SemaphoreType.DMA((group, peers)),
            pltpu.SemaphoreType.DMA((group, 2, 3)),
            pltpu.SemaphoreType.DMA((group, peers)),
        ],
        cost_estimate=pl.CostEstimate(
            flops=4 * work * HDIM, bytes_accessed=8 * block * width * 2, transcendentals=work
        ),
        compiler_params=params(),
        name="attend",
    )(place, tiles, queries, *pieces, *sides)


def place_body(peers, heads_dev, chunks, aliased, place, *refs):
    count = len(chunks) * peers
    pieces, out, held, (in_sems, out_sems) = refs[:count], refs[count + aliased], refs[count + aliased + 1 : -2], refs[-2:]
    me = place[0]
    loads, stores = [], []
    for index, (first, group) in enumerate(chunks):
        for shift in range(peers):
            slot = index * peers + shift
            source = lax.rem(me + peers - shift, peers)
            loads.append(pltpu.make_async_copy(pieces[slot], held[index].at[shift], in_sems.at[slot]))
            stores.append(
                pltpu.make_async_copy(
                    held[index].at[shift],
                    out.at[:, head_columns(source * heads_dev + first, group * HDIM)],
                    out_sems.at[slot],
                )
            )
    for load in loads:
        load.start()
    for load, store in zip(loads, stores):
        load.wait()
        store.start()
    for store in stores:
        store.wait()


def place_columns(place, pieces, out, heads_dev, chunks, shape):
    peers = len(pieces) // len(chunks)
    rows = shape[0]
    aliased = 0 if out is None else 1
    moved = sum(2 * peers * rows * group * HDIM * 2 for _, group in chunks)
    return pl.pallas_call(
        functools.partial(place_body, peers, heads_dev, chunks, aliased),
        out_shape=jax.ShapeDtypeStruct(shape, jnp.bfloat16),
        in_specs=[SMEM] + [HBM] * (len(pieces) + aliased),
        out_specs=HBM,
        input_output_aliases={1 + len(pieces): 0} if aliased else {},
        scratch_shapes=[pltpu.VMEM((peers, rows, group * HDIM), jnp.bfloat16) for _, group in chunks]
        + [
            pltpu.SemaphoreType.DMA((len(pieces),)),
            pltpu.SemaphoreType.DMA((len(pieces),)),
        ],
        cost_estimate=pl.CostEstimate(flops=0, bytes_accessed=moved, transcendentals=0),
        compiler_params=params(),
        name="place",
    )(place, *pieces, *(() if out is None else (out,)))


def groups_of(heads_dev):
    groups, first = [], 0
    while first < heads_dev:
        left = heads_dev - first
        group = min(CHUNK_HEADS, (left + 1) // 2)
        groups.append((first, group))
        first += group
    return groups


def around(array, axis, shift):
    count = lax.axis_size(axis)
    return lax.ppermute(array, axis, [(i, (i + shift) % count) for i in range(count)])


def along(array, axis, shift):
    count = lax.axis_size(axis)
    return lax.ppermute(array, axis, [(i, i + shift) for i in range(count) if 0 <= i + shift < count])


def after(place, values):
    return lax.optimization_barrier((place, values))[0]


def shards(queries, key_rows, value_rows, key_tiles):
    peers = lax.axis_size("head")
    heads_dev, q_tiles, slots = key_tiles.shape
    chunks = groups_of(heads_dev)
    place = lax.axis_index("head").astype(jnp.int32).reshape(1)

    pairs = (slots + 1) // 2
    tile_base = (lax.axis_index("ctx") - 1) * q_tiles
    is_live = key_tiles >= 0
    local_ids = jnp.where(is_live, key_tiles - tile_base, key_tiles[:, :, :1] - tile_base)
    counts = jnp.sum(is_live.astype(jnp.int32), axis=2, keepdims=True)
    filler = local_ids[:, :, :1]
    lists = jnp.concatenate([counts, local_ids] + [filler] * (2 * pairs - slots), axis=2)
    lists = lists.reshape(heads_dev, q_tiles * (2 * pairs + 1)).astype(jnp.int32)

    arrays = (queries, key_rows, value_rows)
    arrived, joined, attended = {}, {}, {}

    def moved(array, axis, shift):
        return around(array, axis, shift) if axis == "head" else along(array, axis, shift)

    for kind, index in kernel_order(len(chunks)):
        if kind == "pack":
            results = pack(place, arrays, peers, heads_dev, [chunks[index]])
        elif kind == "join":
            first, group = chunks[index]
            results = join(place, key_rows, value_rows, arrived[index], heads_dev, first, group * HDIM)
        else:
            first, group = chunks[index]
            results = attend(
                place, lists[first : first + group], queries, arrived[index], joined[index], heads_dev, first,
                group, slots,
            )
        if kind == "pack":
            arrived[index] = [moved(results[0][shift - 1], "head", shift) for shift in range(1, peers)]
        elif kind == "join":
            low, high = (moved(results, "ctx", side) for side in (1, -1))
            joined[index] = (low, results, high)
        else:
            attended[index] = [results[0]] + [moved(results[shift], "head", shift) for shift in range(1, peers)]
        place = after(place, results)
    out = None
    if len(chunks) > 1:
        pieces = [piece for index in range(len(chunks) - 1) for piece in attended[index]]
        out = place_columns(place, pieces, out, heads_dev, chunks[:-1], queries.shape)
    return place_columns(place, attended[len(chunks) - 1], out, heads_dev, chunks[-1:], queries.shape)


def kernel_order(count):
    order = [("pack", index) for index in range(min(AHEAD, count))]
    for step in range(count + 1):
        if step < count:
            order.append(("join", step))
        if step + AHEAD < count:
            order.append(("pack", step + AHEAD))
        if step >= 1:
            order.append(("attend", step - 1))
    return order


def solution(mesh):
    placed = (
        P(("ctx", "head"), None),
        P(("ctx", "head"), None),
        P(("ctx", "head"), None),
        P("head", "ctx", None),
    )
    return jax.shard_map(
        shards, mesh=mesh, in_specs=placed, out_specs=P(("ctx", "head"), None), check_vma=False
    )
```

profile of v0, /device:TPU:5, one launch (start us, length us, event | category | flops | bytes accessed | tf_op | source)
XLA Modules:
  0.0 352.6 jit_solution(8913255196916338788)
XLA Ops:
  0.0 2.5 pack.5
  3.8 2.3 collective-permute-start.1
  7.2 2.5 pack.6
  9.7 9.4 %collective-permute-done.refs_0_ = bf16[3,256,384]{2,1,0:T(8,128)(2,1)} collective-permute-done((bf16[3,256,384]{2,1,0:T(8,128)(2,1)}, bf16[3,256,384]{2,1,0:T(8,128)(2,1)}, u32[]{:S(2)}, u32[]{:S(2)}) %collective-permute-start) | collective-permute-done | bytes 589856 | tf_op jit(solution)/shard_map/ppermute | solution.py:361
  19.1 26.2 %collective-permute-done.1.refs_1_ = bf16[3,256,384]{2,1,0:T(8,128)(2,1)} collective-permute-done((bf16[3,256,384]{2,1,0:T(8,128)(2,1)}, bf16[3,256,384]{2,1,0:T(8,128)(2,1)}, u32[]{:S(2)}, u32[]{:S(2)}) %collective-permute-start.1) | collective-permute-done | bytes 589856 | tf_op jit(solution)/shard_map/ppermute | solution.py:361
  45.3 2.7 join.5.refs_4_
  48.0 3.6 %collective-permute-start.6 = (bf16[2,1024,384]{2,1,0:T(8,128)(2,1)}, bf16[2,1024,384]{2,1,0:T(8,128)(2,1)}, u32[]{:S(2)}, u32[]{:S(2)}) collective-permute-start(bf16[2,1024,384]{2,1,0:T(8,128)(2,1)} %join.5.refs_4_), channel_id=1, source_target_pairs={{0,4},{4,8},{8,12},{12,16},{16,20},{20,24},{24,28},{1,5},{5,9},{9,... | collective-permute-start | bytes 4718600 | tf_op jit(solution)/shard_map/ppermute | solution.py:366
  51.6 1.9 collective-permute-start.7
  53.5 12.9 %collective-permute-start.3 = (bf16[3,256,384]{2,1,0:T(8,128)(2,1)}, bf16[3,256,384]{2,1,0:T(8,128)(2,1)}, u32[]{:S(2)}, u32[]{:S(2)}) collective-permute-start(bf16[3,256,384]{2,1,0:T(8,128)(2,1)} %get-tuple-element.59), channel_id=1, source_target_pairs={{0,1},{1,2},{2,3},{3,0},{4,5},{5,6},{6,7},{7,4},{8,9},{9,10},{10,1... | collective-permute-start | bytes 1769480 | tf_op jit(solution)/shard_map/ppermute | solution.py:361
  68.5 2.5 pack.7
  71.0 8.9 %collective-permute-done.3.refs_0_ = bf16[3,256,384]{2,1,0:T(8,128)(2,1)} collective-permute-done((bf16[3,256,384]{2,1,0:T(8,128)(2,1)}, bf16[3,256,384]{2,1,0:T(8,128)(2,1)}, u32[]{:S(2)}, u32[]{:S(2)}) %collective-permute-start.3) | collective-permute-done | bytes 589856 | tf_op jit(solution)/shard_map/ppermute | solution.py:361
  80.0 26.9 %collective-permute-done.4.refs_1_ = bf16[3,256,384]{2,1,0:T(8,128)(2,1)} collective-permute-done((bf16[3,256,384]{2,1,0:T(8,128)(2,1)}, bf16[3,256,384]{2,1,0:T(8,128)(2,1)}, u32[]{:S(2)}, u32[]{:S(2)}) %collective-permute-start.4) | collective-permute-done | bytes 589856 | tf_op jit(solution)/shard_map/ppermute | solution.py:361
  106.8 2.7 join.6.refs_4_
  109.6 3.6 %collective-permute-start.11 = (bf16[2,1024,384]{2,1,0:T(8,128)(2,1)}, bf16[2,1024,384]{2,1,0:T(8,128)(2,1)}, u32[]{:S(2)}, u32[]{:S(2)}) collective-permute-start(bf16[2,1024,384]{2,1,0:T(8,128)(2,1)} %join.6.refs_4_), channel_id=1, source_target_pairs={{0,4},{4,8},{8,12},{12,16},{16,20},{20,24},{24,28},{1,5},{5,9},{9,... | collective-permute-start | bytes 4718600 | tf_op jit(solution)/shard_map/ppermute | solution.py:366
  116.2 13.6 %collective-permute-start.10 = (bf16[3,256,384]{2,1,0:T(8,128)(2,1)}, bf16[3,256,384]{2,1,0:T(8,128)(2,1)}, u32[]{:S(2)}, u32[]{:S(2)}) collective-permute-start(bf16[3,256,384]{2,1,0:T(8,128)(2,1)} %get-tuple-element.66), channel_id=1, source_target_pairs={{0,3},{1,0},{2,1},{3,2},{4,7},{5,4},{6,5},{7,6},{8,11},{9,8},{10,9... | collective-permute-start | bytes 1769480 | tf_op jit(solution)/shard_map/ppermute | solution.py:361
  133.3 2.2 pack.8
  135.6 14.9 %attend.5 = (bf16[256,384]{1,0:T(8,128)(2,1)}, bf16[256,384]{1,0:T(8,128)(2,1)}, bf16[256,384]{1,0:T(8,128)(2,1)}, bf16[256,384]{1,0:T(8,128)(2,1)}) custom-call(s32[1]{0:T(128)} %bitcast.place, s32[3,152]{1,0:T(4,128)} %slice.35.tiles, bf16[256,6144]{1,0:T(8,128)(2,1)} %queries.9, bf16[3,256,384]{2,1,0:T(8,128)(2,1)} %collective-permute-done.refs_0_, ...), custom_call_target="tpu_custom_call" | custom-call | flops 3623878656 | bytes 6291456 | tf_op jit(solution)/shard_map/attend/pallas_call | solution.py:276
  150.5 4.4 %collective-permute-done.8.refs_0_ = bf16[3,256,384]{2,1,0:T(8,128)(2,1)} collective-permute-done((bf16[3,256,384]{2,1,0:T(8,128)(2,1)}, bf16[3,256,384]{2,1,0:T(8,128)(2,1)}, u32[]{:S(2)}, u32[]{:S(2)}) %collective-permute-start.8) | collective-permute-done | bytes 589856 | tf_op jit(solution)/shard_map/ppermute | solution.py:361
  154.9 25.4 %collective-permute-done.9.refs_1_ = bf16[3,256,384]{2,1,0:T(8,128)(2,1)} collective-permute-done((bf16[3,256,384]{2,1,0:T(8,128)(2,1)}, bf16[3,256,384]{2,1,0:T(8,128)(2,1)}, u32[]{:S(2)}, u32[]{:S(2)}) %collective-permute-start.9) | collective-permute-done | bytes 589856 | tf_op jit(solution)/shard_map/ppermute | solution.py:361
  180.3 2.7 join.7.refs_4_
  183.0 5.4 %collective-permute-start.16 = (bf16[2,1024,384]{2,1,0:T(8,128)(2,1)}, bf16[2,1024,384]{2,1,0:T(8,128)(2,1)}, u32[]{:S(2)}, u32[]{:S(2)}) collective-permute-start(bf16[2,1024,384]{2,1,0:T(8,128)(2,1)} %join.7.refs_4_), channel_id=1, source_target_pairs={{0,4},{4,8},{8,12},{12,16},{16,20},{20,24},{24,28},{1,5},{5,9},{9,... | collective-permute-start | bytes 4718600 | tf_op jit(solution)/shard_map/ppermute | solution.py:366
  188.4 1.9 collective-permute-start.17
  190.4 11.3 %collective-permute-done.13.refs_0_ = bf16[3,256,256]{2,1,0:T(8,128)(2,1)} collective-permute-done((bf16[3,256,256]{2,1,0:T(8,128)(2,1)}, bf16[3,256,256]{2,1,0:T(8,128)(2,1)}, u32[]{:S(2)}, u32[]{:S(2)}) %collective-permute-start.13) | collective-permute-done | bytes 393248 | tf_op jit(solution)/shard_map/ppermute | solution.py:361
  206.5 14.3 %attend.6 = (bf16[256,384]{1,0:T(8,128)(2,1)}, bf16[256,384]{1,0:T(8,128)(2,1)}, bf16[256,384]{1,0:T(8,128)(2,1)}, bf16[256,384]{1,0:T(8,128)(2,1)}) custom-call(s32[1]{0:T(128)} %bitcast.place, s32[3,152]{1,0:T(4,128)} %slice.37.tiles, bf16[256,6144]{1,0:T(8,128)(2,1)} %queries.9, bf16[3,256,384]{2,1,0:T(8,128)(2,1)} %collective-permute-done.3.refs_0_, ...), custom_call_target="tpu_custom_call" | custom-call | flops 3623878656 | bytes 6291456 | tf_op jit(solution)/shard_map/attend/pallas_call | solution.py:276
  220.8 2.0 collective-permute-done.14.refs_1_
  222.8 2.3 join.8.refs_4_
  225.1 7.4 %collective-permute-start.21 = (bf16[2,1024,256]{2,1,0:T(8,128)(2,1)}, bf16[2,1024,256]{2,1,0:T(8,128)(2,1)}, u32[]{:S(2)}, u32[]{:S(2)}) collective-permute-start(bf16[2,1024,256]{2,1,0:T(8,128)(2,1)} %join.8.refs_4_), channel_id=1, source_target_pairs={{0,4},{4,8},{8,12},{12,16},{16,20},{20,24},{24,28},{1,5},{5,9},{9,... | collective-permute-start | bytes 3145736 | tf_op jit(solution)/shard_map/ppermute | solution.py:366
  232.5 1.9 collective-permute-start.22
  234.5 6.9 %collective-permute-start.19 = (bf16[3,256,128]{2,1,0:T(8,128)(2,1)}, bf16[3,256,128]{2,1,0:T(8,128)(2,1)}, u32[]{:S(2)}, u32[]{:S(2)}) collective-permute-start(bf16[3,256,128]{2,1,0:T(8,128)(2,1)} %get-tuple-element.80), channel_id=1, source_target_pairs={{0,2},{1,3},{2,0},{3,1},{4,6},{5,7},{6,4},{7,5},{8,10},{9,11},{10,... | collective-permute-start | bytes 589832 | tf_op jit(solution)/shard_map/ppermute | solution.py:361
  241.4 9.2 %collective-permute-done.19.refs_1_ = bf16[3,256,128]{2,1,0:T(8,128)(2,1)} collective-permute-done((bf16[3,256,128]{2,1,0:T(8,128)(2,1)}, bf16[3,256,128]{2,1,0:T(8,128)(2,1)}, u32[]{:S(2)}, u32[]{:S(2)}) %collective-permute-start.19) | collective-permute-done | bytes 196640 | tf_op jit(solution)/shard_map/ppermute | solution.py:361
  250.6 3.6 %collective-permute-start.20 = (bf16[3,256,128]{2,1,0:T(8,128)(2,1)}, bf16[3,256,128]{2,1,0:T(8,128)(2,1)}, u32[]{:S(2)}, u32[]{:S(2)}) collective-permute-start(bf16[3,256,128]{2,1,0:T(8,128)(2,1)} %get-tuple-element.81), channel_id=1, source_target_pairs={{0,3},{1,0},{2,1},{3,2},{4,7},{5,4},{6,5},{7,6},{8,11},{9,8},{10,9... | collective-permute-start | bytes 589832 | tf_op jit(solution)/shard_map/ppermute | solution.py:361
  255.6 2.5 collective-permute-done.20.refs_2_
  258.1 4.3 %collective-permute-start.32 = (bf16[256,384]{1,0:T(8,128)(2,1)}, bf16[256,384]{1,0:T(8,128)(2,1)}, u32[]{:S(2)}, u32[]{:S(2)}) collective-permute-start(bf16[256,384]{1,0:T(8,128)(2,1)} %get-tuple-element.85), channel_id=1, source_target_pairs={{0,2},{1,3},{2,0},{3,1},{4,6},{5,7},{6,4},{7,5},{8,10},{9,11},{10,... | collective-permute-start | bytes 589832 | tf_op jit(solution)/shard_map/ppermute | solution.py:361
  262.4 23.2 %attend.7 = (bf16[256,384]{1,0:T(8,128)(2,1)}, bf16[256,384]{1,0:T(8,128)(2,1)}, bf16[256,384]{1,0:T(8,128)(2,1)}, bf16[256,384]{1,0:T(8,128)(2,1)}) custom-call(s32[1]{0:T(128)} %bitcast.place, s32[3,152]{1,0:T(4,128)} %slice.39.tiles, bf16[256,6144]{1,0:T(8,128)(2,1)} %queries.9, bf16[3,256,384]{2,1,0:T(8,128)(2,1)} %collective-permute-done.8.refs_0_, ...), custom_call_target="tpu_custom_call" | custom-call | flops 3623878656 | bytes 6291456 | tf_op jit(solution)/shard_map/attend/pallas_call | solution.py:276
  285.6 1.9 join.9.refs_4_
  287.6 5.1 %collective-permute-start.23 = (bf16[2,1024,128]{2,1,0:T(8,128)(2,1)}, bf16[2,1024,128]{2,1,0:T(8,128)(2,1)}, u32[]{:S(2)}, u32[]{:S(2)}) collective-permute-start(bf16[2,1024,128]{2,1,0:T(8,128)(2,1)} %join.9.refs_4_), channel_id=1, source_target_pairs={{0,4},{4,8},{8,12},{12,16},{16,20},{20,24},{24,28},{1,5},{5,9},{9,... | collective-permute-start | bytes 1572872 | tf_op jit(solution)/shard_map/ppermute | solution.py:366
  292.8 1.9 collective-permute-start.24
  296.2 3.2 collective-permute-start.30
  299.5 8.7 %attend.8 = (bf16[256,256]{1,0:T(8,128)(2,1)}, bf16[256,256]{1,0:T(8,128)(2,1)}, bf16[256,256]{1,0:T(8,128)(2,1)}, bf16[256,256]{1,0:T(8,128)(2,1)}) custom-call(s32[1]{0:T(128)} %bitcast.place, s32[2,152]{1,0:T(2,128)} %slice.41.tiles, bf16[256,6144]{1,0:T(8,128)(2,1)} %queries.9, bf16[3,256,256]{2,1,0:T(8,128)(2,1)} %collective-permute-done.13.refs_0_, ...), custom_call_target="tpu_custom_call" | custom-call | flops 2415919104 | bytes 4194304 | tf_op jit(solution)/shard_map/attend/pallas_call | solution.py:276
  308.2 3.0 collective-permute-start.37
  311.9 4.4 %collective-permute-start.35 = (bf16[256,384]{1,0:T(8,128)(2,1)}, bf16[256,384]{1,0:T(8,128)(2,1)}, u32[]{:S(2)}, u32[]{:S(2)}) collective-permute-start(bf16[256,384]{1,0:T(8,128)(2,1)} %get-tuple-element.91), channel_id=1, source_target_pairs={{0,2},{1,3},{2,0},{3,1},{4,6},{5,7},{6,4},{7,5},{8,10},{9,11},{10,... | collective-permute-start | bytes 589832 | tf_op jit(solution)/shard_map/ppermute | solution.py:361
  316.3 2.4 collective-permute-done.37.refs_13_
  320.1 2.2 collective-permute-start.39
  323.7 4.6 %attend.9 = (bf16[256,128]{1,0:T(8,128)(2,1)}, bf16[256,128]{1,0:T(8,128)(2,1)}, bf16[256,128]{1,0:T(8,128)(2,1)}, bf16[256,128]{1,0:T(8,128)(2,1)}) custom-call(s32[1]{0:T(128)} %bitcast.place, s32[1,152]{1,0:T(1,128)} %slice.43.tiles, bf16[256,6144]{1,0:T(8,128)(2,1)} %queries.9, bf16[3,256,128]{2,1,0:T(8,128)(2,1)} %collective-permute-done.18.refs_0_, ...), custom_call_target="tpu_custom_call" | custom-call | flops 1207959552 | bytes 2097152 | tf_op jit(solution)/shard_map/attend/pallas_call | solution.py:276
  328.3 14.4 %collective-permute-done.38.refs_14_ = bf16[256,256]{1,0:T(8,128)(2,1)} collective-permute-done((bf16[256,256]{1,0:T(8,128)(2,1)}, bf16[256,256]{1,0:T(8,128)(2,1)}, u32[]{:S(2)}, u32[]{:S(2)}) %collective-permute-start.38) | collective-permute-done | bytes 131104 | tf_op jit(solution)/shard_map/ppermute | solution.py:361
  342.7 2.1 collective-permute-start.26
  344.8 3.1 collective-permute-start.27
  347.9 2.9 place.2.refs_4_
  (66 shorter events, 24.0 us)
Async XLA Ops:
  2.5 16.6 %collective-permute-start = (bf16[3,256,384]{2,1,0:T(8,128)(2,1)}, bf16[3,256,384]{2,1,0:T(8,128)(2,1)}, u32[]{:S(2)}, u32[]{:S(2)}) collective-permute-start(bf16[3,256,384]{2,1,0:T(8,128)(2,1)} %get-tuple-element.55), channel_id=1, source_target_pairs={{0,1},{1,2},{2,3},{3,0},{4,5},{5,6},{6,7},{7,4},{8,9},{9,10},{10,1... | collective-permute-start | bytes 1769480 | tf_op jit(solution)/shard_map/ppermute | solution.py:361
  3.8 41.5 %collective-permute-start.1 = (bf16[3,256,384]{2,1,0:T(8,128)(2,1)}, bf16[3,256,384]{2,1,0:T(8,128)(2,1)}, u32[]{:S(2)}, u32[]{:S(2)}) collective-permute-start(bf16[3,256,384]{2,1,0:T(8,128)(2,1)} %get-tuple-element.56), channel_id=1, source_target_pairs={{0,2},{1,3},{2,0},{3,1},{4,6},{5,7},{6,4},{7,5},{8,10},{9,11},{10,... | collective-permute-start | bytes 1769480 | tf_op jit(solution)/shard_map/ppermute | solution.py:361
  6.1 39.1 %collective-permute-start.2 = (bf16[3,256,384]{2,1,0:T(8,128)(2,1)}, bf16[3,256,384]{2,1,0:T(8,128)(2,1)}, u32[]{:S(2)}, u32[]{:S(2)}) collective-permute-start(bf16[3,256,384]{2,1,0:T(8,128)(2,1)} %get-tuple-element.57), channel_id=1, source_target_pairs={{0,3},{1,0},{2,1},{3,2},{4,7},{5,4},{6,5},{7,6},{8,11},{9,8},{10,9... | collective-permute-start | bytes 1769480 | tf_op jit(solution)/shard_map/ppermute | solution.py:361
  48.0 81.7 %collective-permute-start.6 = (bf16[2,1024,384]{2,1,0:T(8,128)(2,1)}, bf16[2,1024,384]{2,1,0:T(8,128)(2,1)}, u32[]{:S(2)}, u32[]{:S(2)}) collective-permute-start(bf16[2,1024,384]{2,1,0:T(8,128)(2,1)} %join.5.refs_4_), channel_id=1, source_target_pairs={{0,4},{4,8},{8,12},{12,16},{16,20},{20,24},{24,28},{1,5},{5,9},{9,... | collective-permute-start | bytes 4718600 | tf_op jit(solution)/shard_map/ppermute | solution.py:366
  51.6 78.2 %collective-permute-start.7 = (bf16[2,1024,384]{2,1,0:T(8,128)(2,1)}, bf16[2,1024,384]{2,1,0:T(8,128)(2,1)}, u32[]{:S(2)}, u32[]{:S(2)}) collective-permute-start(bf16[2,1024,384]{2,1,0:T(8,128)(2,1)} %join.5.refs_4_), channel_id=1, source_target_pairs={{4,0},{8,4},{12,8},{16,12},{20,16},{24,20},{28,24},{5,1},{9,5},{13... | collective-permute-start | bytes 4718600 | tf_op jit(solution)/shard_map/ppermute | solution.py:366
  53.5 26.5 %collective-permute-start.3 = (bf16[3,256,384]{2,1,0:T(8,128)(2,1)}, bf16[3,256,384]{2,1,0:T(8,128)(2,1)}, u32[]{:S(2)}, u32[]{:S(2)}) collective-permute-start(bf16[3,256,384]{2,1,0:T(8,128)(2,1)} %get-tuple-element.59), channel_id=1, source_target_pairs={{0,1},{1,2},{2,3},{3,0},{4,5},{5,6},{6,7},{7,4},{8,9},{9,10},{10,1... | collective-permute-start | bytes 1769480 | tf_op jit(solution)/shard_map/ppermute | solution.py:361
  66.4 40.5 %collective-permute-start.4 = (bf16[3,256,384]{2,1,0:T(8,128)(2,1)}, bf16[3,256,384]{2,1,0:T(8,128)(2,1)}, u32[]{:S(2)}, u32[]{:S(2)}) collective-permute-start(bf16[3,256,384]{2,1,0:T(8,128)(2,1)} %get-tuple-element.60), channel_id=1, source_target_pairs={{0,2},{1,3},{2,0},{3,1},{4,6},{5,7},{6,4},{7,5},{8,10},{9,11},{10,... | collective-permute-start | bytes 1769480 | tf_op jit(solution)/shard_map/ppermute | solution.py:361
  67.7 39.1 %collective-permute-start.5 = (bf16[3,256,384]{2,1,0:T(8,128)(2,1)}, bf16[3,256,384]{2,1,0:T(8,128)(2,1)}, u32[]{:S(2)}, u32[]{:S(2)}) collective-permute-start(bf16[3,256,384]{2,1,0:T(8,128)(2,1)} %get-tuple-element.61), channel_id=1, source_target_pairs={{0,3},{1,0},{2,1},{3,2},{4,7},{5,4},{6,5},{7,6},{8,11},{9,8},{10,9... | collective-permute-start | bytes 1769480 | tf_op jit(solution)/shard_map/ppermute | solution.py:361
  109.6 92.2 %collective-permute-start.11 = (bf16[2,1024,384]{2,1,0:T(8,128)(2,1)}, bf16[2,1024,384]{2,1,0:T(8,128)(2,1)}, u32[]{:S(2)}, u32[]{:S(2)}) collective-permute-start(bf16[2,1024,384]{2,1,0:T(8,128)(2,1)} %join.6.refs_4_), channel_id=1, source_target_pairs={{0,4},{4,8},{8,12},{12,16},{16,20},{20,24},{24,28},{1,5},{5,9},{9,... | collective-permute-start | bytes 4718600 | tf_op jit(solution)/shard_map/ppermute | solution.py:366
  114.1 91.4 %collective-permute-start.12 = (bf16[2,1024,384]{2,1,0:T(8,128)(2,1)}, bf16[2,1024,384]{2,1,0:T(8,128)(2,1)}, u32[]{:S(2)}, u32[]{:S(2)}) collective-permute-start(bf16[2,1024,384]{2,1,0:T(8,128)(2,1)} %join.6.refs_4_), channel_id=1, source_target_pairs={{4,0},{8,4},{12,8},{16,12},{20,16},{24,20},{28,24},{5,1},{9,5},{13... | collective-permute-start | bytes 4718600 | tf_op jit(solution)/shard_map/ppermute | solution.py:366
  116.2 34.3 %collective-permute-start.10 = (bf16[3,256,384]{2,1,0:T(8,128)(2,1)}, bf16[3,256,384]{2,1,0:T(8,128)(2,1)}, u32[]{:S(2)}, u32[]{:S(2)}) collective-permute-start(bf16[3,256,384]{2,1,0:T(8,128)(2,1)} %get-tuple-element.66), channel_id=1, source_target_pairs={{0,3},{1,0},{2,1},{3,2},{4,7},{5,4},{6,5},{7,6},{8,11},{9,8},{10,9... | collective-permute-start | bytes 1769480 | tf_op jit(solution)/shard_map/ppermute | solution.py:361
  129.7 25.2 %collective-permute-start.8 = (bf16[3,256,384]{2,1,0:T(8,128)(2,1)}, bf16[3,256,384]{2,1,0:T(8,128)(2,1)}, u32[]{:S(2)}, u32[]{:S(2)}) collective-permute-start(bf16[3,256,384]{2,1,0:T(8,128)(2,1)} %get-tuple-element.64), channel_id=1, source_target_pairs={{0,1},{1,2},{2,3},{3,0},{4,5},{5,6},{6,7},{7,4},{8,9},{9,10},{10,1... | collective-permute-start | bytes 1769480 | tf_op jit(solution)/shard_map/ppermute | solution.py:361
  129.7 50.6 %collective-permute-start.9 = (bf16[3,256,384]{2,1,0:T(8,128)(2,1)}, bf16[3,256,384]{2,1,0:T(8,128)(2,1)}, u32[]{:S(2)}, u32[]{:S(2)}) collective-permute-start(bf16[3,256,384]{2,1,0:T(8,128)(2,1)} %get-tuple-element.65), channel_id=1, source_target_pairs={{0,2},{1,3},{2,0},{3,1},{4,6},{5,7},{6,4},{7,5},{8,10},{9,11},{10,... | collective-permute-start | bytes 1769480 | tf_op jit(solution)/shard_map/ppermute | solution.py:361
  131.3 0.6 copy-start
  131.5 1.1 copy-start.1
  183.0 75.1 %collective-permute-start.16 = (bf16[2,1024,384]{2,1,0:T(8,128)(2,1)}, bf16[2,1024,384]{2,1,0:T(8,128)(2,1)}, u32[]{:S(2)}, u32[]{:S(2)}) collective-permute-start(bf16[2,1024,384]{2,1,0:T(8,128)(2,1)} %join.7.refs_4_), channel_id=1, source_target_pairs={{0,4},{4,8},{8,12},{12,16},{16,20},{20,24},{24,28},{1,5},{5,9},{9,... | collective-permute-start | bytes 4718600 | tf_op jit(solution)/shard_map/ppermute | solution.py:366
  188.4 74.0 %collective-permute-start.17 = (bf16[2,1024,384]{2,1,0:T(8,128)(2,1)}, bf16[2,1024,384]{2,1,0:T(8,128)(2,1)}, u32[]{:S(2)}, u32[]{:S(2)}) collective-permute-start(bf16[2,1024,384]{2,1,0:T(8,128)(2,1)} %join.7.refs_4_), channel_id=1, source_target_pairs={{4,0},{8,4},{12,8},{16,12},{20,16},{24,20},{28,24},{5,1},{9,5},{13... | collective-permute-start | bytes 4718600 | tf_op jit(solution)/shard_map/ppermute | solution.py:366
  190.4 11.4 %collective-permute-start.13 = (bf16[3,256,256]{2,1,0:T(8,128)(2,1)}, bf16[3,256,256]{2,1,0:T(8,128)(2,1)}, u32[]{:S(2)}, u32[]{:S(2)}) collective-permute-start(bf16[3,256,256]{2,1,0:T(8,128)(2,1)} %get-tuple-element.69), channel_id=1, source_target_pairs={{0,1},{1,2},{2,3},{3,0},{4,5},{5,6},{6,7},{7,4},{8,9},{9,10},{10,1... | collective-permute-start | bytes 1179656 | tf_op jit(solution)/shard_map/ppermute | solution.py:361
  201.7 21.0 %collective-permute-start.14 = (bf16[3,256,256]{2,1,0:T(8,128)(2,1)}, bf16[3,256,256]{2,1,0:T(8,128)(2,1)}, u32[]{:S(2)}, u32[]{:S(2)}) collective-permute-start(bf16[3,256,256]{2,1,0:T(8,128)(2,1)} %get-tuple-element.70), channel_id=1, source_target_pairs={{0,2},{1,3},{2,0},{3,1},{4,6},{5,7},{6,4},{7,5},{8,10},{9,11},{10,... | collective-permute-start | bytes 1179656 | tf_op jit(solution)/shard_map/ppermute | solution.py:361
  201.7 21.0 %collective-permute-start.15 = (bf16[3,256,256]{2,1,0:T(8,128)(2,1)}, bf16[3,256,256]{2,1,0:T(8,128)(2,1)}, u32[]{:S(2)}, u32[]{:S(2)}) collective-permute-start(bf16[3,256,256]{2,1,0:T(8,128)(2,1)} %get-tuple-element.71), channel_id=1, source_target_pairs={{0,3},{1,0},{2,1},{3,2},{4,7},{5,4},{6,5},{7,6},{8,11},{9,8},{10,9... | collective-permute-start | bytes 1179656 | tf_op jit(solution)/shard_map/ppermute | solution.py:361
  205.6 28.9 %collective-permute-start.18 = (bf16[3,256,128]{2,1,0:T(8,128)(2,1)}, bf16[3,256,128]{2,1,0:T(8,128)(2,1)}, u32[]{:S(2)}, u32[]{:S(2)}) collective-permute-start(bf16[3,256,128]{2,1,0:T(8,128)(2,1)} %get-tuple-element.79), channel_id=1, source_target_pairs={{0,1},{1,2},{2,3},{3,0},{4,5},{5,6},{6,7},{7,4},{8,9},{9,10},{10,1... | collective-permute-start | bytes 589832 | tf_op jit(solution)/shard_map/ppermute | solution.py:361
  225.1 71.0 %collective-permute-start.21 = (bf16[2,1024,256]{2,1,0:T(8,128)(2,1)}, bf16[2,1024,256]{2,1,0:T(8,128)(2,1)}, u32[]{:S(2)}, u32[]{:S(2)}) collective-permute-start(bf16[2,1024,256]{2,1,0:T(8,128)(2,1)} %join.8.refs_4_), channel_id=1, source_target_pairs={{0,4},{4,8},{8,12},{12,16},{16,20},{20,24},{24,28},{1,5},{5,9},{9,... | collective-permute-start | bytes 3145736 | tf_op jit(solution)/shard_map/ppermute | solution.py:366
  232.5 63.7 %collective-permute-start.22 = (bf16[2,1024,256]{2,1,0:T(8,128)(2,1)}, bf16[2,1024,256]{2,1,0:T(8,128)(2,1)}, u32[]{:S(2)}, u32[]{:S(2)}) collective-permute-start(bf16[2,1024,256]{2,1,0:T(8,128)(2,1)} %join.8.refs_4_), channel_id=1, source_target_pairs={{4,0},{8,4},{12,8},{16,12},{20,16},{24,20},{28,24},{5,1},{9,5},{13... | collective-permute-start | bytes 3145736 | tf_op jit(solution)/shard_map/ppermute | solution.py:366
  234.5 16.1 %collective-permute-start.19 = (bf16[3,256,128]{2,1,0:T(8,128)(2,1)}, bf16[3,256,128]{2,1,0:T(8,128)(2,1)}, u32[]{:S(2)}, u32[]{:S(2)}) collective-permute-start(bf16[3,256,128]{2,1,0:T(8,128)(2,1)} %get-tuple-element.80), channel_id=1, source_target_pairs={{0,2},{1,3},{2,0},{3,1},{4,6},{5,7},{6,4},{7,5},{8,10},{9,11},{10,... | collective-permute-start | bytes 589832 | tf_op jit(solution)/shard_map/ppermute | solution.py:361
  250.6 7.5 %collective-permute-start.20 = (bf16[3,256,128]{2,1,0:T(8,128)(2,1)}, bf16[3,256,128]{2,1,0:T(8,128)(2,1)}, u32[]{:S(2)}, u32[]{:S(2)}) collective-permute-start(bf16[3,256,128]{2,1,0:T(8,128)(2,1)} %get-tuple-element.81), channel_id=1, source_target_pairs={{0,3},{1,0},{2,1},{3,2},{4,7},{5,4},{6,5},{7,6},{8,11},{9,8},{10,9... | collective-permute-start | bytes 589832 | tf_op jit(solution)/shard_map/ppermute | solution.py:361
  258.1 29.5 %collective-permute-start.31 = (bf16[256,384]{1,0:T(8,128)(2,1)}, bf16[256,384]{1,0:T(8,128)(2,1)}, u32[]{:S(2)}, u32[]{:S(2)}) collective-permute-start(bf16[256,384]{1,0:T(8,128)(2,1)} %get-tuple-element.84), channel_id=1, source_target_pairs={{0,1},{1,2},{2,3},{3,0},{4,5},{5,6},{6,7},{7,4},{8,9},{9,10},{10,1... | collective-permute-start | bytes 589832 | tf_op jit(solution)/shard_map/ppermute | solution.py:361
  258.1 34.6 %collective-permute-start.32 = (bf16[256,384]{1,0:T(8,128)(2,1)}, bf16[256,384]{1,0:T(8,128)(2,1)}, u32[]{:S(2)}, u32[]{:S(2)}) collective-permute-start(bf16[256,384]{1,0:T(8,128)(2,1)} %get-tuple-element.85), channel_id=1, source_target_pairs={{0,2},{1,3},{2,0},{3,1},{4,6},{5,7},{6,4},{7,5},{8,10},{9,11},{10,... | collective-permute-start | bytes 589832 | tf_op jit(solution)/shard_map/ppermute | solution.py:361
  262.4 33.7 %collective-permute-start.33 = (bf16[256,384]{1,0:T(8,128)(2,1)}, bf16[256,384]{1,0:T(8,128)(2,1)}, u32[]{:S(2)}, u32[]{:S(2)}) collective-permute-start(bf16[256,384]{1,0:T(8,128)(2,1)} %get-tuple-element.86), channel_id=1, source_target_pairs={{0,3},{1,0},{2,1},{3,2},{4,7},{5,4},{6,5},{7,6},{8,11},{9,8},{10,9... | collective-permute-start | bytes 589832 | tf_op jit(solution)/shard_map/ppermute | solution.py:361
  287.6 32.5 %collective-permute-start.23 = (bf16[2,1024,128]{2,1,0:T(8,128)(2,1)}, bf16[2,1024,128]{2,1,0:T(8,128)(2,1)}, u32[]{:S(2)}, u32[]{:S(2)}) collective-permute-start(bf16[2,1024,128]{2,1,0:T(8,128)(2,1)} %join.9.refs_4_), channel_id=1, source_target_pairs={{0,4},{4,8},{8,12},{12,16},{16,20},{20,24},{24,28},{1,5},{5,9},{9,... | collective-permute-start | bytes 1572872 | tf_op jit(solution)/shard_map/ppermute | solution.py:366
  292.8 27.3 %collective-permute-start.24 = (bf16[2,1024,128]{2,1,0:T(8,128)(2,1)}, bf16[2,1024,128]{2,1,0:T(8,128)(2,1)}, u32[]{:S(2)}, u32[]{:S(2)}) collective-permute-start(bf16[2,1024,128]{2,1,0:T(8,128)(2,1)} %join.9.refs_4_), channel_id=1, source_target_pairs={{4,0},{8,4},{12,8},{16,12},{20,16},{24,20},{28,24},{5,1},{9,5},{13... | collective-permute-start | bytes 1572872 | tf_op jit(solution)/shard_map/ppermute | solution.py:366
  296.1 12.0 %collective-permute-start.28 = (bf16[256,384]{1,0:T(8,128)(2,1)}, bf16[256,384]{1,0:T(8,128)(2,1)}, u32[]{:S(2)}, u32[]{:S(2)}) collective-permute-start(bf16[256,384]{1,0:T(8,128)(2,1)} %get-tuple-element.74), channel_id=1, source_target_pairs={{0,1},{1,2},{2,3},{3,0},{4,5},{5,6},{6,7},{7,4},{8,9},{9,10},{10,1... | collective-permute-start | bytes 589832 | tf_op jit(solution)/shard_map/ppermute | solution.py:361
  296.2 15.7 %collective-permute-start.29 = (bf16[256,384]{1,0:T(8,128)(2,1)}, bf16[256,384]{1,0:T(8,128)(2,1)}, u32[]{:S(2)}, u32[]{:S(2)}) collective-permute-start(bf16[256,384]{1,0:T(8,128)(2,1)} %get-tuple-element.75), channel_id=1, source_target_pairs={{0,2},{1,3},{2,0},{3,1},{4,6},{5,7},{6,4},{7,5},{8,10},{9,11},{10,... | collective-permute-start | bytes 589832 | tf_op jit(solution)/shard_map/ppermute | solution.py:361
  296.2 15.7 %collective-permute-start.30 = (bf16[256,384]{1,0:T(8,128)(2,1)}, bf16[256,384]{1,0:T(8,128)(2,1)}, u32[]{:S(2)}, u32[]{:S(2)}) collective-permute-start(bf16[256,384]{1,0:T(8,128)(2,1)} %get-tuple-element.76), channel_id=1, source_target_pairs={{0,3},{1,0},{2,1},{3,2},{4,7},{5,4},{6,5},{7,6},{8,11},{9,8},{10,9... | collective-permute-start | bytes 589832 | tf_op jit(solution)/shard_map/ppermute | solution.py:361
  308.2 10.5 %collective-permute-start.37 = (bf16[256,256]{1,0:T(8,128)(2,1)}, bf16[256,256]{1,0:T(8,128)(2,1)}, u32[]{:S(2)}, u32[]{:S(2)}) collective-permute-start(bf16[256,256]{1,0:T(8,128)(2,1)} %get-tuple-element.96), channel_id=1, source_target_pairs={{0,1},{1,2},{2,3},{3,0},{4,5},{5,6},{6,7},{7,4},{8,9},{9,10},{10,1... | collective-permute-start | bytes 393224 | tf_op jit(solution)/shard_map/ppermute | solution.py:361
  311.9 32.9 %collective-permute-start.34 = (bf16[256,384]{1,0:T(8,128)(2,1)}, bf16[256,384]{1,0:T(8,128)(2,1)}, u32[]{:S(2)}, u32[]{:S(2)}) collective-permute-start(bf16[256,384]{1,0:T(8,128)(2,1)} %get-tuple-element.90), channel_id=1, source_target_pairs={{0,1},{1,2},{2,3},{3,0},{4,5},{5,6},{6,7},{7,4},{8,9},{9,10},{10,1... | collective-permute-start | bytes 589832 | tf_op jit(solution)/shard_map/ppermute | solution.py:361
  311.9 36.0 %collective-permute-start.35 = (bf16[256,384]{1,0:T(8,128)(2,1)}, bf16[256,384]{1,0:T(8,128)(2,1)}, u32[]{:S(2)}, u32[]{:S(2)}) collective-permute-start(bf16[256,384]{1,0:T(8,128)(2,1)} %get-tuple-element.91), channel_id=1, source_target_pairs={{0,2},{1,3},{2,0},{3,1},{4,6},{5,7},{6,4},{7,5},{8,10},{9,11},{10,... | collective-permute-start | bytes 589832 | tf_op jit(solution)/shard_map/ppermute | solution.py:361
  318.7 29.2 %collective-permute-start.36 = (bf16[256,384]{1,0:T(8,128)(2,1)}, bf16[256,384]{1,0:T(8,128)(2,1)}, u32[]{:S(2)}, u32[]{:S(2)}) collective-permute-start(bf16[256,384]{1,0:T(8,128)(2,1)} %get-tuple-element.92), channel_id=1, source_target_pairs={{0,3},{1,0},{2,1},{3,2},{4,7},{5,4},{6,5},{7,6},{8,11},{9,8},{10,9... | collective-permute-start | bytes 589832 | tf_op jit(solution)/shard_map/ppermute | solution.py:361
  320.1 22.6 %collective-permute-start.38 = (bf16[256,256]{1,0:T(8,128)(2,1)}, bf16[256,256]{1,0:T(8,128)(2,1)}, u32[]{:S(2)}, u32[]{:S(2)}) collective-permute-start(bf16[256,256]{1,0:T(8,128)(2,1)} %get-tuple-element.97), channel_id=1, source_target_pairs={{0,2},{1,3},{2,0},{3,1},{4,6},{5,7},{6,4},{7,5},{8,10},{9,11},{10,... | collective-permute-start | bytes 393224 | tf_op jit(solution)/shard_map/ppermute | solution.py:361
  320.1 22.6 %collective-permute-start.39 = (bf16[256,256]{1,0:T(8,128)(2,1)}, bf16[256,256]{1,0:T(8,128)(2,1)}, u32[]{:S(2)}, u32[]{:S(2)}) collective-permute-start(bf16[256,256]{1,0:T(8,128)(2,1)} %get-tuple-element.98), channel_id=1, source_target_pairs={{0,3},{1,0},{2,1},{3,2},{4,7},{5,4},{6,5},{7,6},{8,11},{9,8},{10,9... | collective-permute-start | bytes 393224 | tf_op jit(solution)/shard_map/ppermute | solution.py:361
  342.7 8.1 %collective-permute-start.25 = (bf16[256,128]{1,0:T(8,128)(2,1)}, bf16[256,128]{1,0:T(8,128)(2,1)}, u32[]{:S(2)}, u32[]{:S(2)}) collective-permute-start(bf16[256,128]{1,0:T(8,128)(2,1)} %get-tuple-element.101), channel_id=1, source_target_pairs={{0,1},{1,2},{2,3},{3,0},{4,5},{5,6},{6,7},{7,4},{8,9},{9,10},{10,1... | collective-permute-start | bytes 196616 | tf_op jit(solution)/shard_map/ppermute | solution.py:361
  342.7 8.1 %collective-permute-start.26 = (bf16[256,128]{1,0:T(8,128)(2,1)}, bf16[256,128]{1,0:T(8,128)(2,1)}, u32[]{:S(2)}, u32[]{:S(2)}) collective-permute-start(bf16[256,128]{1,0:T(8,128)(2,1)} %get-tuple-element.102), channel_id=1, source_target_pairs={{0,2},{1,3},{2,0},{3,1},{4,6},{5,7},{6,4},{7,5},{8,10},{9,11},{10,... | collective-permute-start | bytes 196616 | tf_op jit(solution)/shard_map/ppermute | solution.py:361
  344.8 6.0 %collective-permute-start.27 = (bf16[256,128]{1,0:T(8,128)(2,1)}, bf16[256,128]{1,0:T(8,128)(2,1)}, u32[]{:S(2)}, u32[]{:S(2)}) collective-permute-start(bf16[256,128]{1,0:T(8,128)(2,1)} %get-tuple-element.103), channel_id=1, source_target_pairs={{0,3},{1,0},{2,1},{3,2},{4,7},{5,4},{6,5},{7,6},{8,11},{9,8},{10,9... | collective-permute-start | bytes 196616 | tf_op jit(solution)/shard_map/ppermute | solution.py:361
where the time goes:
time: 357 us; the launch traced here: 353 us
  waiting for transfers between devices  144 us (40%)
  starting transfers between devices  104 us (29%)
  Pallas kernels  94.1 us (26%)
  local copies, waits for them, and re-layouts  6.35 us (2%)
    ppermute x30, waiting for transfers between devices, around(): lax.ppermute(array, axis, [(i, (i + shift) % count) for i in range(count)])  144 us
    ppermute x30, starting transfers between devices, around(): lax.ppermute(array, axis, [(i, (i + shift) % count) for i in range(count)])  69.6 us
    pallas_call x5, Pallas kernels, attend(): pl.pallas_call(functools.partial(attend_body, peers, heads_dev, first, gr...  65.7 us
    ppermute x10, starting transfers between devices, along(): lax.ppermute(array, axis, [(i, i + shift) for i in range(count) if 0 <= i...  34.8 us
    pallas_call x5, Pallas kernels, join(): pl.pallas_call(functools.partial(join_body, peers, heads_dev, first, widt...  12.4 us
    pallas_call x5, Pallas kernels, pack(): pl.pallas_call(functools.partial(pack_body, peers, heads_dev, chunks), ou...  11.6 us
  transfers between devices with their start and end apart: 40, of which 13 were waited for; matrix products, arithmetic and copies ran while one was open for 3% of the time, Pallas kernels for 25%

commit v1 on v0

v1 whole, which is shorter than its diff:
```python
import functools
from typing import NamedTuple

import jax
import jax.numpy as jnp
from jax import lax
from jax.experimental import pallas as pl
from jax.experimental.pallas import tpu as pltpu
from jax.sharding import PartitionSpec as P


HDIM = 128
TILE = 128
LOG2E = 1.4426950408889634
DEAD = 1e30
AHEAD = 2
VMEM_LIMIT = 67043328
LANES = 128
WITHIN = 64
WIDE_HEADS = 3
NARROW_HEADS = 5


HBM = pl.BlockSpec(memory_space=pl.ANY)
SMEM = pl.BlockSpec(memory_space=pltpu.SMEM)


def run_copies(copies):
    for copy in copies:
        copy.start()
    for copy in copies:
        copy.wait()


def head_columns(head):
    return pl.ds(pl.multiple_of(head * HDIM, HDIM), HDIM)


def lanes_of(index):
    return pl.ds(index * HDIM, HDIM) if isinstance(index, int) else pl.ds(pl.multiple_of(index * HDIM, HDIM), HDIM)


def params():
    return pltpu.CompilerParams(vmem_limit_bytes=VMEM_LIMIT)


class Group(NamedTuple):
    peers: int
    base: int
    heads: int

    def head(self, order, member, index):
        return order[self.base + index * self.peers + member]


def pack_body(groups, place, order, *refs):
    sends = sum(group.peers - 1 for group in groups)
    arrays, outs, held, (in_sems, out_sems) = refs[:3], refs[3 : 3 + sends], refs[3 + sends : -2], refs[-2:]
    loads, stores, block = [], [], 0
    for number, group in enumerate(groups):
        me = lax.rem(place[0], group.peers)
        for shift in range(1, group.peers):
            member = lax.rem(me + shift, group.peers)
            copies = []
            for index in range(group.heads):
                columns = head_columns(group.head(order, member, index))
                for which, array in enumerate(arrays):
                    copies.append(
                        pltpu.make_async_copy(
                            array.at[:, columns],
                            held[number].at[shift - 1, which, :, lanes_of(index)],
                            in_sems.at[block],
                        )
                    )
                    block += 1
            sent = len(loads)
            loads.append(copies)
            stores.append(pltpu.make_async_copy(held[number].at[shift - 1], outs[sent], out_sems.at[sent]))
    for copies in loads:
        for copy in copies:
            copy.start()
    for copies, store in zip(loads, stores):
        for copy in copies:
            copy.wait()
        store.start()
    for store in stores:
        store.wait()


def pack(groups, place, order, arrays):
    rows = arrays[0].shape[0]
    outs = [
        jax.ShapeDtypeStruct((3, rows, group.heads * HDIM), jnp.bfloat16)
        for group in groups
        for _ in range(group.peers - 1)
    ]
    blocks = sum(3 * (group.peers - 1) * group.heads for group in groups)
    results = pl.pallas_call(
        functools.partial(pack_body, groups),
        out_shape=outs,
        in_specs=[SMEM, SMEM] + [HBM] * 3,
        out_specs=[HBM] * len(outs),
        scratch_shapes=[pltpu.VMEM((group.peers - 1, 3, rows, group.heads * HDIM), jnp.bfloat16) for group in groups]
        + [pltpu.SemaphoreType.DMA((blocks,)), pltpu.SemaphoreType.DMA((len(outs),))],
        cost_estimate=pl.CostEstimate(flops=0, bytes_accessed=4 * blocks * rows * HDIM, transcendentals=0),
        compiler_params=params(),
        name="pack",
    )(place, order, *arrays)
    sent = []
    for group in groups:
        sent.append(results[: group.peers - 1])
        results = results[group.peers - 1 :]
    return sent


def rows_of(member, rows):
    return pl.ds(pl.multiple_of(member * rows, rows), rows)


def join_body(group, place, order, key_rows, value_rows, *refs):
    peers = group.peers
    pieces, (out, held, own_sems, in_sems, out_sem) = refs[: peers - 1], refs[peers - 1 :]
    me = lax.rem(place[0], peers)
    rows = key_rows.shape[0]
    loads = []
    for which, array in enumerate((key_rows, value_rows)):
        for index in range(group.heads):
            loads.append(
                pltpu.make_async_copy(
                    array.at[:, head_columns(group.head(order, me, index))],
                    held.at[which, rows_of(me, rows), lanes_of(index)],
                    own_sems.at[which, index],
                )
            )
        for shift in range(1, peers):
            source = lax.rem(me + peers - shift, peers)
            loads.append(
                pltpu.make_async_copy(
                    pieces[shift - 1].at[1 + which], held.at[which, rows_of(source, rows)], in_sems.at[shift, which]
                )
            )
    run_copies(loads)
    run_copies([pltpu.make_async_copy(held, out, out_sem)])


def join(group, place, order, key_rows, value_rows, pieces):
    peers, rows = group.peers, key_rows.shape[0]
    shape = (2, peers * rows, group.heads * HDIM)
    return pl.pallas_call(
        functools.partial(join_body, group),
        out_shape=jax.ShapeDtypeStruct(shape, jnp.bfloat16),
        in_specs=[SMEM, SMEM] + [HBM] * (2 + peers - 1),
        out_specs=HBM,
        scratch_shapes=[
            pltpu.VMEM(shape, jnp.bfloat16),
            pltpu.SemaphoreType.DMA((2, group.heads)),
            pltpu.SemaphoreType.DMA((peers, 2)),
            pltpu.SemaphoreType.DMA,
        ],
        cost_estimate=pl.CostEstimate(flops=0, bytes_accessed=4 * shape[0] * shape[1] * shape[2], transcendentals=0),
        compiler_params=params(),
        name="join",
    )(place, order, key_rows, value_rows, *pieces)


def attend_body(group, column, place, order, lists, queries, *refs):
    peers, heads = group.peers, group.heads
    pieces, refs = refs[: peers - 1], refs[peers - 1 :]
    sides, refs = refs[:3], refs[3:]
    outs, refs = refs[:peers], refs[peers:]
    tiles, q_held, kv_held, o_held, scores, peak, total, sums, t_sems, own_sems, q_sems, kv_sems, o_sems = refs
    me = lax.rem(place[0], peers)
    rows = queries.shape[0]
    block = peers * rows
    q_tiles = block // TILE
    first_row = (place[0] // peers) * q_tiles

    def list_copy(head):
        return pltpu.make_async_copy(lists.at[group.head(order, me, head)], tiles.at[head], t_sems.at[head])

    def early(head):
        copies = [
            pltpu.make_async_copy(
                queries.at[:, head_columns(group.head(order, me, head))],
                q_held.at[head, rows_of(me, rows)],
                own_sems.at[head],
            )
        ]
        for shift in range(1, peers):
            source = lax.rem(me + peers - shift, peers)
            copies.append(
                pltpu.make_async_copy(
                    pieces[shift - 1].at[0, :, lanes_of(head)],
                    q_held.at[head, rows_of(source, rows)],
                    q_sems.at[head, shift],
                )
            )
        return copies + sides_of(head, 0)

    def sides_of(head, which):
        return [
            pltpu.make_async_copy(
                sides[side].at[which, :, lanes_of(head)],
                kv_held.at[head, which, pl.ds(side * block, block)],
                kv_sems.at[head, which, side],
            )
            for side in range(3)
        ]

    def back(head):
        return [
            pltpu.make_async_copy(
                o_held.at[head, rows_of(lax.rem(me + shift, peers), rows)],
                outs[shift].at[:, lanes_of(head)],
                o_sems.at[head, shift],
            )
            for shift in range(peers)
        ]

    for head in range(heads):
        for copy in [list_copy(head)] + early(head) + sides_of(head, 1):
            copy.start()

    factor = HDIM ** (-0.5) * LOG2E

    @pl.loop(0, heads)
    def _(head):
        def listed(tile, slot):
            return tiles[head, first_row + tile, column + 1 + slot]

        def live(tile):
            return tiles[head, first_row + tile, column]

        def gathered(which, tile, pair):
            return jnp.concatenate(
                [
                    kv_held[head, which, pl.ds(pl.multiple_of(listed(tile, 2 * pair + half) * TILE, TILE), TILE)]
                    for half in range(2)
                ],
                axis=0,
            )

        list_copy(head).wait()
        longest = live(0)
        for tile in range(1, q_tiles):
            longest = jnp.maximum(longest, live(tile))
        steps = (longest + 1) // 2

        peak[...] = jnp.full_like(peak, -jnp.inf)
        total[...] = jnp.zeros_like(total)
        sums[...] = jnp.zeros_like(sums)
        for copy in early(head):
            copy.wait()

        @pl.loop(0, steps)
        def _(pair):
            for tile in range(q_tiles):
                at = pl.ds(tile * TILE, TILE)
                score = lax.dot_general(
                    q_held[head, at],
                    gathered(0, tile, pair),
                    (((1,), (1,)), ((), ())),
                    preferred_element_type=jnp.float32,
                )
                scores[pair, at] = score
                peak[at] = jnp.maximum(peak[at], jnp.maximum(score[:, :TILE], score[:, TILE:]))

        for tile in range(q_tiles):
            at = pl.ds(tile * TILE, TILE)
            top = jnp.max(peak[at], axis=1, keepdims=True) * factor
            peak[at] = jnp.broadcast_to(top, (TILE, TILE))
        for copy in sides_of(head, 1):
            copy.wait()

        @pl.loop(0, steps)
        def _(pair):
            for tile in range(q_tiles):
                at = pl.ds(tile * TILE, TILE)
                top = peak[at]
                parts = []
                for half in range(2):
                    base = jnp.where(2 * pair + half < live(tile), top, DEAD)
                    parts.append(
                        jnp.exp2(scores[pair, at, pl.ds(half * TILE, TILE)] * factor - base)
                    )
                total[at] += parts[0] + parts[1]
                weight = jnp.concatenate(parts, axis=1).astype(jnp.bfloat16)
                sums[at] += jnp.dot(
                    weight, gathered(1, tile, pair), preferred_element_type=jnp.float32
                )

        for tile in range(q_tiles):
            at = pl.ds(tile * TILE, TILE)
            row_total = jnp.sum(total[at], axis=1, keepdims=True)
            o_held[head, at] = (sums[at] / row_total).astype(jnp.bfloat16)
        for copy in back(head):
            copy.start()

    for head in range(heads):
        for copy in back(head):
            copy.wait()


def attend(group, column, slots, place, order, lists, queries, pieces, sides):
    peers, heads = group.peers, group.heads
    rows = queries.shape[0]
    block = peers * rows
    width = heads * HDIM
    pairs = (slots + 1) // 2
    work = heads * block * slots * TILE
    return pl.pallas_call(
        functools.partial(attend_body, group, column),
        out_shape=[jax.ShapeDtypeStruct((rows, width), jnp.bfloat16)] * peers,
        in_specs=[SMEM, SMEM] + [HBM] * (2 + peers - 1 + 3),
        out_specs=[HBM] * peers,
        scratch_shapes=[
            pltpu.SMEM((heads,) + lists.shape[1:], jnp.int32),
            pltpu.VMEM((heads, block, HDIM), jnp.bfloat16),
            pltpu.VMEM((heads, 2, 3 * block, HDIM), jnp.bfloat16),
            pltpu.VMEM((heads, block, HDIM), jnp.bfloat16),
            pltpu.VMEM((pairs, block, 2 * TILE), jnp.float32),
            pltpu.VMEM((block, TILE), jnp.float32),
            pltpu.VMEM((block, TILE), jnp.float32),
            pltpu.VMEM((block, HDIM), jnp.float32),
            pltpu.SemaphoreType.DMA((heads,)),
            pltpu.SemaphoreType.DMA((heads,)),
            pltpu.SemaphoreType.DMA((heads, peers)),
            pltpu.SemaphoreType.DMA((heads, 2, 3)),
            pltpu.SemaphoreType.DMA((heads, peers)),
        ],
        cost_estimate=pl.CostEstimate(
            flops=4 * work * HDIM, bytes_accessed=8 * block * width * 2, transcendentals=work
        ),
        compiler_params=params(),
        name="attend",
    )(place, order, lists, queries, *pieces, *sides)


def place_body(groups, aliased, place, order, *refs):
    count = sum(group.peers for group in groups)
    pieces, out, held, (in_sems, out_sems) = refs[:count], refs[count + aliased], refs[count + aliased + 1 : -2], refs[-2:]
    loads, stores = [], []
    piece, block = 0, 0
    for number, group in enumerate(groups):
        me = lax.rem(place[0], group.peers)
        for shift in range(group.peers):
            source = lax.rem(me + group.peers - shift, group.peers)
            loads.append(pltpu.make_async_copy(pieces[piece], held[number].at[shift], in_sems.at[piece]))
            copies = []
            for index in range(group.heads):
                copies.append(
                    pltpu.make_async_copy(
                        held[number].at[shift, :, lanes_of(index)],
                        out.at[:, head_columns(group.head(order, source, index))],
                        out_sems.at[block],
                    )
                )
                block += 1
            stores.append(copies)
            piece += 1
    for load in loads:
        load.start()
    for load, copies in zip(loads, stores):
        load.wait()
        for copy in copies:
            copy.start()
    for copies in stores:
        for copy in copies:
            copy.wait()


def place_columns(groups, place, order, pieces, out, shape):
    rows = shape[0]
    aliased = 0 if out is None else 1
    blocks = sum(group.peers * group.heads for group in groups)
    return pl.pallas_call(
        functools.partial(place_body, groups, aliased),
        out_shape=jax.ShapeDtypeStruct(shape, jnp.bfloat16),
        in_specs=[SMEM, SMEM] + [HBM] * (len(pieces) + aliased),
        out_specs=HBM,
        input_output_aliases={2 + len(pieces): 0} if aliased else {},
        scratch_shapes=[pltpu.VMEM((group.peers, rows, group.heads * HDIM), jnp.bfloat16) for group in groups]
        + [
            pltpu.SemaphoreType.DMA((len(pieces),)),
            pltpu.SemaphoreType.DMA((blocks,)),
        ],
        cost_estimate=pl.CostEstimate(flops=0, bytes_accessed=4 * blocks * rows * HDIM, transcendentals=0),
        compiler_params=params(),
        name="place",
    )(place, order, *pieces, *(() if out is None else (out,)))


def around(array, peers, shift):
    count = lax.axis_size("head")
    moves = [(i, i // peers * peers + (i + shift) % peers) for i in range(count)]
    return lax.ppermute(array, "head", moves)


def along(array, shift):
    count = lax.axis_size("ctx")
    return lax.ppermute(array, "ctx", [(i, i + shift) for i in range(count) if 0 <= i + shift < count])


def after(place, values):
    return lax.optimization_barrier((place, values))[0]


def shares(heads, most):
    count = -(-heads // most)
    parts = [heads // count + (i < heads % count) for i in range(count)] if heads else []
    if count > 2 and parts[-1] > 1 and parts[0] == parts[-1]:
        parts[1], parts[-1] = parts[1] + 1, parts[-1] - 1
    return parts


def plan(wide, heads_dev, peers):
    half = peers // 2
    base, wides, narrows = 0, [], []
    for heads in shares(wide, WIDE_HEADS):
        wides.append(Group(peers, base, heads))
        base += peers * heads
    for heads in shares((heads_dev - wide) * (peers // half), NARROW_HEADS):
        narrows.append(Group(half, base, heads))
        base += half * heads
    mixed = []
    while wides or narrows:
        mixed += narrows[:1] + wides[:1]
        wides, narrows = wides[1:], narrows[1:]
    return mixed


def widths(heads_dev):
    return sorted({-(-heads_dev // 2), -(-2 * heads_dev // 3), heads_dev})


def list_rows(key_tiles):
    _, cells, slots = key_tiles.shape
    padded = slots + slots % 2
    is_live = key_tiles >= 0
    base = (lax.axis_index("ctx") - 1) * cells
    local_ids = jnp.where(is_live, key_tiles, key_tiles[:, :, :1]) - base
    counts = jnp.sum(is_live.astype(jnp.int32), axis=2, keepdims=True)
    half = cells // 2
    own_half = (jnp.arange(cells, dtype=jnp.int32) // half * half)[None, :, None]
    half_ids = local_ids // cells * half + local_ids % cells - own_half

    def row(ids, width):
        ids = jnp.pad(ids, ((0, 0), (0, 0), (0, padded - slots)))
        ids = jnp.concatenate([counts, ids], axis=2)
        return jnp.pad(ids, ((0, 0), (0, 0), (0, width - ids.shape[2])))

    return jnp.concatenate([row(local_ids, WITHIN), row(half_ids, LANES - WITHIN)], axis=2).astype(jnp.int32)


def sorted_heads(key_tiles):
    heads_dev, cells, _ = key_tiles.shape
    half = cells // 2
    is_live = key_tiles >= 0
    tile_half = (jnp.arange(cells, dtype=jnp.int32) // half)[None, :, None]
    crosses = jnp.any(is_live & (key_tiles % cells // half != tile_half), axis=(1, 2))
    longest = jnp.max(jnp.sum(is_live.astype(jnp.int32), axis=2), axis=1)
    mine = crosses.astype(jnp.int32) * LANES + longest
    tokens, peers = lax.axis_size("ctx"), lax.axis_size("head")
    spread = jnp.broadcast_to(mine[None], (tokens * peers, heads_dev))
    every = lax.all_to_all(spread, ("ctx", "head"), split_axis=0, concat_axis=0, tiled=True)
    score = jnp.max(every.reshape(tokens, peers * heads_dev), axis=0)
    index = jnp.arange(peers * heads_dev, dtype=jnp.int32)
    ahead = (score[None, :] > score[:, None]) | ((score[None, :] == score[:, None]) & (index[None, :] < index[:, None]))
    rank = jnp.sum(ahead.astype(jnp.int32), axis=1)
    order = jnp.sum(jnp.where(rank[None, :] == index[:, None], index[None, :], 0), axis=1)
    return order.astype(jnp.int32), jnp.sum((score >= LANES).astype(jnp.int32))


def pipeline(groups, place, order, queries, key_rows, value_rows, key_tiles):
    slots = key_tiles.shape[2]
    arrays = (queries, key_rows, value_rows)
    packed, arrived, joined, attended = {}, {}, {}, {}

    def send(index, pieces):
        arrived[index] = [
            around(pieces[shift - 1], groups[index].peers, shift)
            for shift in range(1, groups[index].peers)
        ]

    for kind, index in kernel_order(len(groups)):
        if kind == "join" and index == 0:
            rows = list_rows(after(key_tiles, place))
            lists = gather_heads(rows)
        group = groups[index]
        peers = group.peers
        if kind == "pack":
            results = pack(groups[index : index + 1] if index == 0 else groups[1:], place, order, arrays)
        elif kind == "join":
            results = join(group, place, order, key_rows, value_rows, arrived[index])
        else:
            column = 0 if peers == lax.axis_size("head") else WITHIN
            results = attend(
                group, column, slots, place, order, lists, queries, arrived[index], joined[index]
            )
        if kind == "pack":
            packed.update(zip(range(index, len(groups)), results))
            for ahead in range(index, min(AHEAD, index + 1)):
                send(ahead, packed[ahead])
        elif kind == "join":
            low, high = (along(results, side) for side in (1, -1))
            joined[index] = (low, results, high)
            if index + AHEAD < len(groups):
                send(index + AHEAD, after(packed[index + AHEAD], results))
        else:
            attended[index] = [results[0]] + [around(results[shift], peers, shift) for shift in range(1, peers)]
        place = after(place, results)
    out = None
    last = len(groups) - 1
    if last:
        pieces = [piece for index in range(last) for piece in attended[index]]
        out = place_columns(groups[:-1], place, order, pieces, out, queries.shape)
    return place_columns(groups[-1:], place, order, attended[last], out, queries.shape)


def gather_heads(rows):
    count = lax.axis_size("head")
    spread = jnp.broadcast_to(rows[None], (count,) + rows.shape)
    every = lax.all_to_all(spread, "head", split_axis=0, concat_axis=0, tiled=True)
    return every.reshape((-1,) + rows.shape[1:])


def plans(heads_dev, peers):
    return [plan(wide, heads_dev, peers) for wide in widths(heads_dev)]


def shards(queries, key_rows, value_rows, key_tiles):
    peers = lax.axis_size("head")
    heads_dev = key_tiles.shape[0]
    place = lax.axis_index("head").astype(jnp.int32).reshape(1)
    order, crossing = sorted_heads(key_tiles)
    which = jnp.int32(0)
    for wide in widths(heads_dev)[:-1]:
        which = which + (crossing > wide * peers).astype(jnp.int32)
    branches = [functools.partial(pipeline, groups) for groups in plans(heads_dev, peers)]
    return lax.switch(which, branches, place, order, queries, key_rows, value_rows, key_tiles)


def kernel_order(count):
    order = [("pack", index) for index in range(min(2, count))]
    for step in range(count + 1):
        if step < count:
            order.append(("join", step))
        if step >= 1:
            order.append(("attend", step - 1))
    return order


def solution(mesh):
    placed = (
        P(("ctx", "head"), None),
        P(("ctx", "head"), None),
        P(("ctx", "head"), None),
        P("head", "ctx", None),
    )
    return jax.shard_map(
        shards, mesh=mesh, in_specs=placed, out_specs=P(("ctx", "head"), None), check_vma=False
    )
```

time: 357 us -> 318 us (0.89)
  the two profiles are of different devices: /device:TPU:5 before, /device:TPU:10 now
where the time goes in v1:
time: 318 us; the launch traced here: 317 us
  waiting for transfers between devices  138 us (43%)
  Pallas kernels  106 us (33%)
  starting transfers between devices  62.5 us (20%)
  other arithmetic  5.05 us (2%)
  local copies, waits for them, and re-layouts  3.2 us (1%)
    ppermute x22, waiting for transfers between devices, around(): return lax.ppermute(array, 'head', moves)  110 us
    pallas_call x5, Pallas kernels, attend(): pl.pallas_call(functools.partial(attend_body, group, column), out_shape=[...  74.6 us
    ppermute x10, starting transfers between devices, along(): lax.ppermute(array, 'ctx', [(i, i + shift) for i in range(count) if 0 <=...  28.5 us
    ppermute x10, waiting for transfers between devices, along(): lax.ppermute(array, 'ctx', [(i, i + shift) for i in range(count) if 0 <=...  23 us
    ppermute x22, starting transfers between devices, around(): return lax.ppermute(array, 'head', moves)  22 us
    pallas_call x5, Pallas kernels, join(): pl.pallas_call(functools.partial(join_body, group), out_shape=jax.ShapeDt...  16 us
    pallas_call x2, Pallas kernels, pack(): pl.pallas_call(functools.partial(pack_body, groups), out_shape=outs, in_s...  9.22 us
  transfers between devices with their start and end apart: 34, of which 13 were waited for; matrix products, arithmetic and copies ran while one was open for 1% of the time, Pallas kernels for 31%

profile of v1, /device:TPU:10, one launch (start us, length us, event | category | flops | bytes accessed | tf_op | source)
XLA Modules:
  0.0 317.2 jit_solution(17900708088192645380)
XLA Ops:
  3.0 6.0 %all-to-all-start.3 = ((s32[32,1,12]{2,1,0:T(1,128)}), s32[32,1,12]{2,1,0:T(1,128)S(1)}, u32[]{:S(2)}, u32[]{:S(2)}) async-start(s32[32,1,12]{2,1,0:T(1,128)} %broadcast_in_dim.80), calls=%async_computation.3 | async-start | bytes 32768 | tf_op jit(solution)/shard_map/all_to_all | solution.py:465
  9.0 5.0 %all-to-all-done.3 = s32[32,1,12]{2,1,0:T(1,128)S(1)} async-done(((s32[32,1,12]{2,1,0:T(1,128)}), s32[32,1,12]{2,1,0:T(1,128)S(1)}, u32[]{:S(2)}, u32[]{:S(2)}) %all-to-all-start.3) | async-done | bytes 1568 | tf_op jit(solution)/shard_map/all_to_all | solution.py:465
  17.3 299.7 %conditional.1 = (bf16[256,6144]{1,0:T(8,128)(2,1)}) conditional(s32[]{:T(128)} %clamp.3, (s32[]{:T(128)}, s32[48,48]{1,0:T(8,128)S(1)}, bf16[256,6144]{1,0:T(8,128)(2,1)}, bf16[256,6144]{1,0:T(8,128)(2,1)}, bf16[256,6144]{1,0:T(8,128)(2,1)}, /*index=5*/s32[12,8,18]{2,1,0:T(8,128)}, s32[]{:T(128)}, s32[48,48]{1,0:T(8,128)S(1)}, ...), branch_computations={%region_7.9_spmd, %region_9.11_spmd, %region_11.13_spmd} | conditional | flops 14495586304 | bytes 147285600 | solution.py:540
  18.1 2.8 pack.8
  21.0 1.6 collective-permute-start.28
  22.6 6.4 %pack.9 = (bf16[3,256,384]{2,1,0:T(8,128)(2,1)}, bf16[3,256,384]{2,1,0:T(8,128)(2,1)}, bf16[3,256,384]{2,1,0:T(8,128)(2,1)}, bf16[3,256,512]{2,1,0:T(8,128)(2,1)...) custom-call(s32[1]{0:T(128)} %bitcast.4.place, ...), custom_call_target="tpu_custom_call" | custom-call | bytes 11010048 | tf_op jit(solution)/shard_map/cond/branch_1_fun/pack/pallas_call | solution.py:98
  29.0 2.8 collective-permute-start.30
  31.9 29.7 %collective-permute-done.28.refs_0_ = bf16[3,256,512]{2,1,0:T(8,128)(2,1)} collective-permute-done((bf16[3,256,512]{2,1,0:T(8,128)(2,1)}, bf16[3,256,512]{2,1,0:T(8,128)(2,1)}, u32[]{:S(2)}, u32[]{:S(2)}) %collective-permute-start.28) | collective-permute-done | bytes 786464 | tf_op jit(solution)/shard_map/cond/branch_1_fun/ppermute | solution.py:396
  61.5 3.0 join.19.refs_2_
  64.6 15.2 %collective-permute-done.30.refs_1_ = bf16[3,256,384]{2,1,0:T(8,128)(2,1)} collective-permute-done((bf16[3,256,384]{2,1,0:T(8,128)(2,1)}, bf16[3,256,384]{2,1,0:T(8,128)(2,1)}, u32[]{:S(2)}, u32[]{:S(2)}) %collective-permute-start.30) | collective-permute-done | bytes 589856 | tf_op jit(solution)/shard_map/cond/branch_1_fun/ppermute | solution.py:396
  79.8 3.4 %collective-permute-done.31.refs_2_ = bf16[3,256,384]{2,1,0:T(8,128)(2,1)} collective-permute-done((bf16[3,256,384]{2,1,0:T(8,128)(2,1)}, bf16[3,256,384]{2,1,0:T(8,128)(2,1)}, u32[]{:S(2)}, u32[]{:S(2)}) %collective-permute-start.31) | collective-permute-done | bytes 589856 | tf_op jit(solution)/shard_map/cond/branch_1_fun/ppermute | solution.py:396
  83.2 3.4 %join.20.refs_4_ = bf16[2,1024,384]{2,1,0:T(8,128)(2,1)} custom-call(s32[1]{0:T(128)} %bitcast.4.place, s32[48]{0:T(128)} %select_reduce_fusion.1.order, bf16[256,6144]{1,0:T(8,128)(2,1)} %get-tuple-element.226.refs_1_.key_rows, bf16[256,6144]{1,0:T(8,128)(2,1)} %get-tuple-element.229.refs_2_.value_rows, ...), custom_call_target="tpu_custom_call" | custom-call | bytes 3145728 | tf_op jit(solution)/shard_map/cond/branch_1_fun/join/pallas_call | solution.py:149
  86.7 1.9 collective-permute-start.35
  88.6 3.9 %collective-permute-start.36 = (bf16[2,1024,384]{2,1,0:T(8,128)(2,1)}, bf16[2,1024,384]{2,1,0:T(8,128)(2,1)}, u32[]{:S(2)}, u32[]{:S(2)}) collective-permute-start(bf16[2,1024,384]{2,1,0:T(8,128)(2,1)} %join.20.refs_4_), channel_id=1, source_target_pairs={{4,0},{8,4},{12,8},{16,12},{20,16},{24,20},{28,24},{5,1},{9,5},{13... | collective-permute-start | bytes 4718600 | tf_op jit(solution)/shard_map/cond/branch_1_fun/ppermute | solution.py:401
  93.4 1.9 collective-permute-start.32
  95.3 3.6 %collective-permute-start.33 = (bf16[2,512,512]{2,1,0:T(8,128)(2,1)}, bf16[2,512,512]{2,1,0:T(8,128)(2,1)}, u32[]{:S(2)}, u32[]{:S(2)}) collective-permute-start(bf16[2,512,512]{2,1,0:T(8,128)(2,1)} %join.19.refs_2_), channel_id=1, source_target_pairs={{4,0},{8,4},{12,8},{16,12},{20,16},{24,20},{28,24},{5,1},{9,5},{13... | collective-permute-start | bytes 3145736 | tf_op jit(solution)/shard_map/cond/branch_1_fun/ppermute | solution.py:401
  100.7 5.9 %all-to-all-start.1 = ((s32[4,12,8,128]{3,2,1,0:T(8,128)}), s32[4,12,8,128]{3,2,1,0:T(8,128)}, u32[]{:S(2)}, u32[]{:S(2)}) async-start(s32[4,12,8,128]{3,2,1,0:T(8,128)} %broadcast_in_dim.53), calls=%async_computation.1 | async-start | bytes 393216 | tf_op jit(solution)/shard_map/cond/branch_1_fun/all_to_all | solution.py:523
  106.6 13.2 %collective-permute-done.34.refs_0_ = bf16[3,256,512]{2,1,0:T(8,128)(2,1)} collective-permute-done((bf16[3,256,512]{2,1,0:T(8,128)(2,1)}, bf16[3,256,512]{2,1,0:T(8,128)(2,1)}, u32[]{:S(2)}, u32[]{:S(2)}) %collective-permute-start.34) | collective-permute-done | bytes 786464 | tf_op jit(solution)/shard_map/cond/branch_1_fun/ppermute | solution.py:396
  120.0 4.3 %collective-permute-start.38 = (bf16[3,256,384]{2,1,0:T(8,128)(2,1)}, bf16[3,256,384]{2,1,0:T(8,128)(2,1)}, u32[]{:S(2)}, u32[]{:S(2)}) collective-permute-start(bf16[3,256,384]{2,1,0:T(8,128)(2,1)} %get-tuple-element.123), channel_id=1, source_target_pairs={{0,2},{1,3},{2,0},{3,1},{4,6},{5,7},{6,4},{7,5},{8,10},{9,11},{10,... | collective-permute-start | bytes 1769480 | tf_op jit(solution)/shard_map/cond/branch_1_fun/ppermute | solution.py:396
  124.2 22.8 %collective-permute-done.33.refs_3_ = bf16[2,512,512]{2,1,0:T(8,128)(2,1)} collective-permute-done((bf16[2,512,512]{2,1,0:T(8,128)(2,1)}, bf16[2,512,512]{2,1,0:T(8,128)(2,1)}, u32[]{:S(2)}, u32[]{:S(2)}) %collective-permute-start.33) | collective-permute-done | bytes 1048608 | tf_op jit(solution)/shard_map/cond/branch_1_fun/ppermute | solution.py:401
  147.0 13.5 %attend.19 = (bf16[256,512]{1,0:T(8,128)(2,1)}, bf16[256,512]{1,0:T(8,128)(2,1)}) custom-call(s32[1]{0:T(128)} %bitcast.4.place, s32[48]{0:T(128)} %select_reduce_fusion.1.order, s32[48,8,128]{2,1,0:T(8,128)} %bitcast.7.lists, bf16[256,6144]{1,0:T(8,128)(2,1)} %get-tuple-element.223.refs_0_.queries, bf16[3,256,512]{2,1,0:T(8,128)(2,1)} %collective-permute-done.28.refs_0_, ...), custom_call_target="tpu_custom_call" | custom-call | flops 2415919104 | bytes 4194304 | tf_op jit(solution)/shard_map/cond/branch_1_fun/attend/pallas_call | solution.py:311
  160.5 3.0 join.21.refs_2_
  163.6 2.7 collective-permute-start.40
  166.3 3.3 %collective-permute-start.41 = (bf16[2,512,512]{2,1,0:T(8,128)(2,1)}, bf16[2,512,512]{2,1,0:T(8,128)(2,1)}, u32[]{:S(2)}, u32[]{:S(2)}) collective-permute-start(bf16[2,512,512]{2,1,0:T(8,128)(2,1)} %join.21.refs_2_), channel_id=1, source_target_pairs={{4,0},{8,4},{12,8},{16,12},{20,16},{24,20},{28,24},{5,1},{9,5},{13... | collective-permute-start | bytes 3145736 | tf_op jit(solution)/shard_map/cond/branch_1_fun/ppermute | solution.py:401
  169.6 23.3 %attend.20 = (bf16[256,384]{1,0:T(8,128)(2,1)}, bf16[256,384]{1,0:T(8,128)(2,1)}, bf16[256,384]{1,0:T(8,128)(2,1)}, bf16[256,384]{1,0:T(8,128)(2,1)}) custom-call(s32[1]{0:T(128)} %bitcast.4.place, s32[48]{0:T(128)} %select_reduce_fusion.1.order, s32[48,8,128]{2,1,0:T(8,128)} %bitcast.7.lists, bf16[256,6144]{1,0:T(8,128)(2,1)} %get-tuple-element.223.refs_0_.queries, ...), custom_call_target="tpu_custom_call" | custom-call | flops 3623878656 | bytes 6291456 | tf_op jit(solution)/shard_map/cond/branch_1_fun/attend/pallas_call | solution.py:311
  193.0 3.4 %join.22.refs_4_ = bf16[2,1024,384]{2,1,0:T(8,128)(2,1)} custom-call(s32[1]{0:T(128)} %bitcast.4.place, s32[48]{0:T(128)} %select_reduce_fusion.1.order, bf16[256,6144]{1,0:T(8,128)(2,1)} %get-tuple-element.226.refs_1_.key_rows, bf16[256,6144]{1,0:T(8,128)(2,1)} %get-tuple-element.229.refs_2_.value_rows, ...), custom_call_target="tpu_custom_call" | custom-call | bytes 3145728 | tf_op jit(solution)/shard_map/cond/branch_1_fun/join/pallas_call | solution.py:149
  196.4 1.9 collective-permute-start.45
  198.3 3.6 %collective-permute-start.46 = (bf16[2,1024,384]{2,1,0:T(8,128)(2,1)}, bf16[2,1024,384]{2,1,0:T(8,128)(2,1)}, u32[]{:S(2)}, u32[]{:S(2)}) collective-permute-start(bf16[2,1024,384]{2,1,0:T(8,128)(2,1)} %join.22.refs_4_), channel_id=1, source_target_pairs={{4,0},{8,4},{12,8},{16,12},{20,16},{24,20},{28,24},{5,1},{9,5},{13... | collective-permute-start | bytes 4718600 | tf_op jit(solution)/shard_map/cond/branch_1_fun/ppermute | solution.py:401
  202.0 1.8 collective-permute-start.42
  203.8 1.8 collective-permute-start.43
  205.6 8.9 %attend.21 = (bf16[256,512]{1,0:T(8,128)(2,1)}, bf16[256,512]{1,0:T(8,128)(2,1)}) custom-call(s32[1]{0:T(128)} %bitcast.4.place, s32[48]{0:T(128)} %select_reduce_fusion.1.order, s32[48,8,128]{2,1,0:T(8,128)} %bitcast.7.lists, bf16[256,6144]{1,0:T(8,128)(2,1)} %get-tuple-element.223.refs_0_.queries, bf16[3,256,512]{2,1,0:T(8,128)(2,1)} %collective-permute-done.34.refs_0_, ...), custom_call_target="tpu_custom_call" | custom-call | flops 2415919104 | bytes 4194304 | tf_op jit(solution)/shard_map/cond/branch_1_fun/attend/pallas_call | solution.py:311
  214.6 23.1 %collective-permute-done.43.refs_1_ = bf16[3,256,256]{2,1,0:T(8,128)(2,1)} collective-permute-done((bf16[3,256,256]{2,1,0:T(8,128)(2,1)}, bf16[3,256,256]{2,1,0:T(8,128)(2,1)}, u32[]{:S(2)}, u32[]{:S(2)}) %collective-permute-start.43) | collective-permute-done | bytes 393248 | tf_op jit(solution)/shard_map/cond/branch_1_fun/ppermute | solution.py:396
  237.6 3.4 %collective-permute-done.44.refs_2_ = bf16[3,256,256]{2,1,0:T(8,128)(2,1)} collective-permute-done((bf16[3,256,256]{2,1,0:T(8,128)(2,1)}, bf16[3,256,256]{2,1,0:T(8,128)(2,1)}, u32[]{:S(2)}, u32[]{:S(2)}) %collective-permute-start.44) | collective-permute-done | bytes 393248 | tf_op jit(solution)/shard_map/cond/branch_1_fun/ppermute | solution.py:396
  241.0 3.1 join.23.refs_4_
  244.1 2.0 collective-permute-start.47
  246.1 3.5 %collective-permute-start.48 = (bf16[2,1024,256]{2,1,0:T(8,128)(2,1)}, bf16[2,1024,256]{2,1,0:T(8,128)(2,1)}, u32[]{:S(2)}, u32[]{:S(2)}) collective-permute-start(bf16[2,1024,256]{2,1,0:T(8,128)(2,1)} %join.23.refs_4_), channel_id=1, source_target_pairs={{4,0},{8,4},{12,8},{16,12},{20,16},{24,20},{28,24},{5,1},{9,5},{13... | collective-permute-start | bytes 3145736 | tf_op jit(solution)/shard_map/cond/branch_1_fun/ppermute | solution.py:401
  249.7 8.3 %collective-permute-done.52.refs_1_ = bf16[256,512]{1,0:T(8,128)(2,1)} collective-permute-done((bf16[256,512]{1,0:T(8,128)(2,1)}, bf16[256,512]{1,0:T(8,128)(2,1)}, u32[]{:S(2)}, u32[]{:S(2)}) %collective-permute-start.52) | collective-permute-done | bytes 262176 | tf_op jit(solution)/shard_map/cond/branch_1_fun/ppermute | solution.py:396
  258.1 2.6 collective-permute-start.54
  260.7 19.2 %attend.22 = (bf16[256,384]{1,0:T(8,128)(2,1)}, bf16[256,384]{1,0:T(8,128)(2,1)}, bf16[256,384]{1,0:T(8,128)(2,1)}, bf16[256,384]{1,0:T(8,128)(2,1)}) custom-call(s32[1]{0:T(128)} %bitcast.4.place, s32[48]{0:T(128)} %select_reduce_fusion.1.order, s32[48,8,128]{2,1,0:T(8,128)} %bitcast.7.lists, bf16[256,6144]{1,0:T(8,128)(2,1)} %get-tuple-element.223.refs_0_.queries, ...), custom_call_target="tpu_custom_call" | custom-call | flops 3623878656 | bytes 6291456 | tf_op jit(solution)/shard_map/cond/branch_1_fun/attend/pallas_call | solution.py:311
  280.0 2.1 collective-permute-start.55
  282.1 2.4 collective-permute-start.58
  284.5 9.6 %attend.23 = (bf16[256,256]{1,0:T(8,128)(2,1)}, bf16[256,256]{1,0:T(8,128)(2,1)}, bf16[256,256]{1,0:T(8,128)(2,1)}, bf16[256,256]{1,0:T(8,128)(2,1)}) custom-call(s32[1]{0:T(128)} %bitcast.4.place, s32[48]{0:T(128)} %select_reduce_fusion.1.order, s32[48,8,128]{2,1,0:T(8,128)} %bitcast.7.lists, bf16[256,6144]{1,0:T(8,128)(2,1)} %get-tuple-element.223.refs_0_.queries, ...), custom_call_target="tpu_custom_call" | custom-call | flops 2415919104 | bytes 4194304 | tf_op jit(solution)/shard_map/cond/branch_1_fun/attend/pallas_call | solution.py:311
  294.1 2.3 collective-permute-done.55.refs_5_
  296.4 2.2 collective-permute-start.50
  298.7 9.0 %collective-permute-done.58.refs_10_ = bf16[256,384]{1,0:T(8,128)(2,1)} collective-permute-done((bf16[256,384]{1,0:T(8,128)(2,1)}, bf16[256,384]{1,0:T(8,128)(2,1)}, u32[]{:S(2)}, u32[]{:S(2)}) %collective-permute-start.58) | collective-permute-done | bytes 196640 | tf_op jit(solution)/shard_map/cond/branch_1_fun/ppermute | solution.py:396
  307.8 2.7 collective-permute-done.59.refs_11_
  310.4 3.6 %place.8.refs_4_ = bf16[256,6144]{1,0:T(8,128)(2,1)} custom-call(s32[1]{0:T(128)} %bitcast.4.place, s32[48]{0:T(128)} %select_reduce_fusion.1.order, bf16[256,512]{1,0:T(8,128)(2,1)} %get-tuple-element.112.refs_0_, bf16[256,512]{1,0:T(8,128)(2,1)} %collective-permute-done.52.refs_1_, bf16[256,384]{1,0:T(8,128)(2,1)} %get-tuple-element.117.refs_2_, ...), custom_call_target="tpu_custom_call" | custom-call | bytes 5242880 | tf_op jit(solution)/shard_map/cond/branch_1_fun/place/pallas_call | solution.py:376
  314.1 2.5 place.9
  (61 shorter events, 8.8 us)
Async XLA Ops:
  3.0 11.0 %all-to-all-start.3 = ((s32[32,1,12]{2,1,0:T(1,128)}), s32[32,1,12]{2,1,0:T(1,128)S(1)}, u32[]{:S(2)}, u32[]{:S(2)}) async-start(s32[32,1,12]{2,1,0:T(1,128)} %broadcast_in_dim.80), calls=%async_computation.3 | async-start | bytes 32768 | tf_op jit(solution)/shard_map/all_to_all | solution.py:465
  21.0 40.6 %collective-permute-start.28 = (bf16[3,256,512]{2,1,0:T(8,128)(2,1)}, bf16[3,256,512]{2,1,0:T(8,128)(2,1)}, u32[]{:S(2)}, u32[]{:S(2)}) collective-permute-start(bf16[3,256,512]{2,1,0:T(8,128)(2,1)} %pack.8), channel_id=1, source_target_pairs={{0,1},{1,0},{2,3},{3,2},{4,5},{5,4},{6,7},{7,6},{8,9},{9,8},{10,11... | collective-permute-start | bytes 2359304 | tf_op jit(solution)/shard_map/cond/branch_1_fun/ppermute | solution.py:396
  29.0 35.6 %collective-permute-start.29 = (bf16[3,256,384]{2,1,0:T(8,128)(2,1)}, bf16[3,256,384]{2,1,0:T(8,128)(2,1)}, u32[]{:S(2)}, u32[]{:S(2)}) collective-permute-start(bf16[3,256,384]{2,1,0:T(8,128)(2,1)} %get-tuple-element.97), channel_id=1, source_target_pairs={{0,1},{1,2},{2,3},{3,0},{4,5},{5,6},{6,7},{7,4},{8,9},{9,10},{10,1... | collective-permute-start | bytes 1769480 | tf_op jit(solution)/shard_map/cond/branch_1_fun/ppermute | solution.py:396
  29.0 50.8 %collective-permute-start.30 = (bf16[3,256,384]{2,1,0:T(8,128)(2,1)}, bf16[3,256,384]{2,1,0:T(8,128)(2,1)}, u32[]{:S(2)}, u32[]{:S(2)}) collective-permute-start(bf16[3,256,384]{2,1,0:T(8,128)(2,1)} %get-tuple-element.98), channel_id=1, source_target_pairs={{0,2},{1,3},{2,0},{3,1},{4,6},{5,7},{6,4},{7,5},{8,10},{9,11},{10,... | collective-permute-start | bytes 1769480 | tf_op jit(solution)/shard_map/cond/branch_1_fun/ppermute | solution.py:396
  31.9 51.4 %collective-permute-start.31 = (bf16[3,256,384]{2,1,0:T(8,128)(2,1)}, bf16[3,256,384]{2,1,0:T(8,128)(2,1)}, u32[]{:S(2)}, u32[]{:S(2)}) collective-permute-start(bf16[3,256,384]{2,1,0:T(8,128)(2,1)} %get-tuple-element.99), channel_id=1, source_target_pairs={{0,3},{1,0},{2,1},{3,2},{4,7},{5,4},{6,5},{7,6},{8,11},{9,8},{10,9... | collective-permute-start | bytes 1769480 | tf_op jit(solution)/shard_map/cond/branch_1_fun/ppermute | solution.py:396
  86.7 76.9 %collective-permute-start.35 = (bf16[2,1024,384]{2,1,0:T(8,128)(2,1)}, bf16[2,1024,384]{2,1,0:T(8,128)(2,1)}, u32[]{:S(2)}, u32[]{:S(2)}) collective-permute-start(bf16[2,1024,384]{2,1,0:T(8,128)(2,1)} %join.20.refs_4_), channel_id=1, source_target_pairs={{0,4},{4,8},{8,12},{12,16},{16,20},{20,24},{24,28},{1,5},{5,9},{9,... | collective-permute-start | bytes 4718600 | tf_op jit(solution)/shard_map/cond/branch_1_fun/ppermute | solution.py:401
  88.6 77.7 %collective-permute-start.36 = (bf16[2,1024,384]{2,1,0:T(8,128)(2,1)}, bf16[2,1024,384]{2,1,0:T(8,128)(2,1)}, u32[]{:S(2)}, u32[]{:S(2)}) collective-permute-start(bf16[2,1024,384]{2,1,0:T(8,128)(2,1)} %join.20.refs_4_), channel_id=1, source_target_pairs={{4,0},{8,4},{12,8},{16,12},{20,16},{24,20},{28,24},{5,1},{9,5},{13... | collective-permute-start | bytes 4718600 | tf_op jit(solution)/shard_map/cond/branch_1_fun/ppermute | solution.py:401
  93.4 26.5 %collective-permute-start.32 = (bf16[2,512,512]{2,1,0:T(8,128)(2,1)}, bf16[2,512,512]{2,1,0:T(8,128)(2,1)}, u32[]{:S(2)}, u32[]{:S(2)}) collective-permute-start(bf16[2,512,512]{2,1,0:T(8,128)(2,1)} %join.19.refs_2_), channel_id=1, source_target_pairs={{0,4},{4,8},{8,12},{12,16},{16,20},{20,24},{24,28},{1,5},{5,9},{9,... | collective-permute-start | bytes 3145736 | tf_op jit(solution)/shard_map/cond/branch_1_fun/ppermute | solution.py:401
  95.3 51.7 %collective-permute-start.33 = (bf16[2,512,512]{2,1,0:T(8,128)(2,1)}, bf16[2,512,512]{2,1,0:T(8,128)(2,1)}, u32[]{:S(2)}, u32[]{:S(2)}) collective-permute-start(bf16[2,512,512]{2,1,0:T(8,128)(2,1)} %join.19.refs_2_), channel_id=1, source_target_pairs={{4,0},{8,4},{12,8},{16,12},{20,16},{24,20},{28,24},{5,1},{9,5},{13... | collective-permute-start | bytes 3145736 | tf_op jit(solution)/shard_map/cond/branch_1_fun/ppermute | solution.py:401
  99.0 20.8 %collective-permute-start.34 = (bf16[3,256,512]{2,1,0:T(8,128)(2,1)}, bf16[3,256,512]{2,1,0:T(8,128)(2,1)}, u32[]{:S(2)}, u32[]{:S(2)}) collective-permute-start(bf16[3,256,512]{2,1,0:T(8,128)(2,1)} %get-tuple-element.115), channel_id=1, source_target_pairs={{0,1},{1,0},{2,3},{3,2},{4,5},{5,4},{6,7},{7,6},{8,9},{9,8},{10,11... | collective-permute-start | bytes 2359304 | tf_op jit(solution)/shard_map/cond/branch_1_fun/ppermute | solution.py:396
  100.7 46.4 %all-to-all-start.1 = ((s32[4,12,8,128]{3,2,1,0:T(8,128)}), s32[4,12,8,128]{3,2,1,0:T(8,128)}, u32[]{:S(2)}, u32[]{:S(2)}) async-start(s32[4,12,8,128]{3,2,1,0:T(8,128)} %broadcast_in_dim.53), calls=%async_computation.1 | async-start | bytes 393216 | tf_op jit(solution)/shard_map/cond/branch_1_fun/all_to_all | solution.py:523
  119.8 73.2 %collective-permute-start.37 = (bf16[3,256,384]{2,1,0:T(8,128)(2,1)}, bf16[3,256,384]{2,1,0:T(8,128)(2,1)}, u32[]{:S(2)}, u32[]{:S(2)}) collective-permute-start(bf16[3,256,384]{2,1,0:T(8,128)(2,1)} %get-tuple-element.122), channel_id=1, source_target_pairs={{0,1},{1,2},{2,3},{3,0},{4,5},{5,6},{6,7},{7,4},{8,9},{9,10},{10,1... | collective-permute-start | bytes 1769480 | tf_op jit(solution)/shard_map/cond/branch_1_fun/ppermute | solution.py:396
  120.0 73.0 %collective-permute-start.38 = (bf16[3,256,384]{2,1,0:T(8,128)(2,1)}, bf16[3,256,384]{2,1,0:T(8,128)(2,1)}, u32[]{:S(2)}, u32[]{:S(2)}) collective-permute-start(bf16[3,256,384]{2,1,0:T(8,128)(2,1)} %get-tuple-element.123), channel_id=1, source_target_pairs={{0,2},{1,3},{2,0},{3,1},{4,6},{5,7},{6,4},{7,5},{8,10},{9,11},{10,... | collective-permute-start | bytes 1769480 | tf_op jit(solution)/shard_map/cond/branch_1_fun/ppermute | solution.py:396
  147.0 45.9 %collective-permute-start.39 = (bf16[3,256,384]{2,1,0:T(8,128)(2,1)}, bf16[3,256,384]{2,1,0:T(8,128)(2,1)}, u32[]{:S(2)}, u32[]{:S(2)}) collective-permute-start(bf16[3,256,384]{2,1,0:T(8,128)(2,1)} %get-tuple-element.124), channel_id=1, source_target_pairs={{0,3},{1,0},{2,1},{3,2},{4,7},{5,4},{6,5},{7,6},{8,11},{9,8},{10,9... | collective-permute-start | bytes 1769480 | tf_op jit(solution)/shard_map/cond/branch_1_fun/ppermute | solution.py:396
  163.6 40.2 %collective-permute-start.40 = (bf16[2,512,512]{2,1,0:T(8,128)(2,1)}, bf16[2,512,512]{2,1,0:T(8,128)(2,1)}, u32[]{:S(2)}, u32[]{:S(2)}) collective-permute-start(bf16[2,512,512]{2,1,0:T(8,128)(2,1)} %join.21.refs_2_), channel_id=1, source_target_pairs={{0,4},{4,8},{8,12},{12,16},{16,20},{20,24},{24,28},{1,5},{5,9},{9,... | collective-permute-start | bytes 3145736 | tf_op jit(solution)/shard_map/cond/branch_1_fun/ppermute | solution.py:401
  166.3 39.3 %collective-permute-start.41 = (bf16[2,512,512]{2,1,0:T(8,128)(2,1)}, bf16[2,512,512]{2,1,0:T(8,128)(2,1)}, u32[]{:S(2)}, u32[]{:S(2)}) collective-permute-start(bf16[2,512,512]{2,1,0:T(8,128)(2,1)} %join.21.refs_2_), channel_id=1, source_target_pairs={{4,0},{8,4},{12,8},{16,12},{20,16},{24,20},{28,24},{5,1},{9,5},{13... | collective-permute-start | bytes 3145736 | tf_op jit(solution)/shard_map/cond/branch_1_fun/ppermute | solution.py:401
  196.4 61.7 %collective-permute-start.45 = (bf16[2,1024,384]{2,1,0:T(8,128)(2,1)}, bf16[2,1024,384]{2,1,0:T(8,128)(2,1)}, u32[]{:S(2)}, u32[]{:S(2)}) collective-permute-start(bf16[2,1024,384]{2,1,0:T(8,128)(2,1)} %join.22.refs_4_), channel_id=1, source_target_pairs={{0,4},{4,8},{8,12},{12,16},{16,20},{20,24},{24,28},{1,5},{5,9},{9,... | collective-permute-start | bytes 4718600 | tf_op jit(solution)/shard_map/cond/branch_1_fun/ppermute | solution.py:401
  198.3 62.4 %collective-permute-start.46 = (bf16[2,1024,384]{2,1,0:T(8,128)(2,1)}, bf16[2,1024,384]{2,1,0:T(8,128)(2,1)}, u32[]{:S(2)}, u32[]{:S(2)}) collective-permute-start(bf16[2,1024,384]{2,1,0:T(8,128)(2,1)} %join.22.refs_4_), channel_id=1, source_target_pairs={{4,0},{8,4},{12,8},{16,12},{20,16},{24,20},{28,24},{5,1},{9,5},{13... | collective-permute-start | bytes 4718600 | tf_op jit(solution)/shard_map/cond/branch_1_fun/ppermute | solution.py:401
  202.0 12.6 %collective-permute-start.42 = (bf16[3,256,256]{2,1,0:T(8,128)(2,1)}, bf16[3,256,256]{2,1,0:T(8,128)(2,1)}, u32[]{:S(2)}, u32[]{:S(2)}) collective-permute-start(bf16[3,256,256]{2,1,0:T(8,128)(2,1)} %get-tuple-element.129), channel_id=1, source_target_pairs={{0,1},{1,2},{2,3},{3,0},{4,5},{5,6},{6,7},{7,4},{8,9},{9,10},{10,1... | collective-permute-start | bytes 1179656 | tf_op jit(solution)/shard_map/cond/branch_1_fun/ppermute | solution.py:396
  203.8 33.9 %collective-permute-start.43 = (bf16[3,256,256]{2,1,0:T(8,128)(2,1)}, bf16[3,256,256]{2,1,0:T(8,128)(2,1)}, u32[]{:S(2)}, u32[]{:S(2)}) collective-permute-start(bf16[3,256,256]{2,1,0:T(8,128)(2,1)} %get-tuple-element.130), channel_id=1, source_target_pairs={{0,2},{1,3},{2,0},{3,1},{4,6},{5,7},{6,4},{7,5},{8,10},{9,11},{10,... | collective-permute-start | bytes 1179656 | tf_op jit(solution)/shard_map/cond/branch_1_fun/ppermute | solution.py:396
  205.6 35.4 %collective-permute-start.44 = (bf16[3,256,256]{2,1,0:T(8,128)(2,1)}, bf16[3,256,256]{2,1,0:T(8,128)(2,1)}, u32[]{:S(2)}, u32[]{:S(2)}) collective-permute-start(bf16[3,256,256]{2,1,0:T(8,128)(2,1)} %get-tuple-element.131), channel_id=1, source_target_pairs={{0,3},{1,0},{2,1},{3,2},{4,7},{5,4},{6,5},{7,6},{8,11},{9,8},{10,9... | collective-permute-start | bytes 1179656 | tf_op jit(solution)/shard_map/cond/branch_1_fun/ppermute | solution.py:396
  244.1 38.0 %collective-permute-start.47 = (bf16[2,1024,256]{2,1,0:T(8,128)(2,1)}, bf16[2,1024,256]{2,1,0:T(8,128)(2,1)}, u32[]{:S(2)}, u32[]{:S(2)}) collective-permute-start(bf16[2,1024,256]{2,1,0:T(8,128)(2,1)} %join.23.refs_4_), channel_id=1, source_target_pairs={{0,4},{4,8},{8,12},{12,16},{16,20},{20,24},{24,28},{1,5},{5,9},{9,... | collective-permute-start | bytes 3145736 | tf_op jit(solution)/shard_map/cond/branch_1_fun/ppermute | solution.py:401
  246.1 38.4 %collective-permute-start.48 = (bf16[2,1024,256]{2,1,0:T(8,128)(2,1)}, bf16[2,1024,256]{2,1,0:T(8,128)(2,1)}, u32[]{:S(2)}, u32[]{:S(2)}) collective-permute-start(bf16[2,1024,256]{2,1,0:T(8,128)(2,1)} %join.23.refs_4_), channel_id=1, source_target_pairs={{4,0},{8,4},{12,8},{16,12},{20,16},{24,20},{28,24},{5,1},{9,5},{13... | collective-permute-start | bytes 3145736 | tf_op jit(solution)/shard_map/cond/branch_1_fun/ppermute | solution.py:401
  249.6 8.4 %collective-permute-start.52 = (bf16[256,512]{1,0:T(8,128)(2,1)}, bf16[256,512]{1,0:T(8,128)(2,1)}, u32[]{:S(2)}, u32[]{:S(2)}) collective-permute-start(bf16[256,512]{1,0:T(8,128)(2,1)} %get-tuple-element.113), channel_id=1, source_target_pairs={{0,1},{1,0},{2,3},{3,2},{4,5},{5,4},{6,7},{7,6},{8,9},{9,8},{10,11... | collective-permute-start | bytes 786440 | tf_op jit(solution)/shard_map/cond/branch_1_fun/ppermute | solution.py:396
  258.1 21.9 %collective-permute-start.53 = (bf16[256,384]{1,0:T(8,128)(2,1)}, bf16[256,384]{1,0:T(8,128)(2,1)}, u32[]{:S(2)}, u32[]{:S(2)}) collective-permute-start(bf16[256,384]{1,0:T(8,128)(2,1)} %get-tuple-element.118), channel_id=1, source_target_pairs={{0,1},{1,2},{2,3},{3,0},{4,5},{5,6},{6,7},{7,4},{8,9},{9,10},{10,1... | collective-permute-start | bytes 589832 | tf_op jit(solution)/shard_map/cond/branch_1_fun/ppermute | solution.py:396
  258.1 24.0 %collective-permute-start.54 = (bf16[256,384]{1,0:T(8,128)(2,1)}, bf16[256,384]{1,0:T(8,128)(2,1)}, u32[]{:S(2)}, u32[]{:S(2)}) collective-permute-start(bf16[256,384]{1,0:T(8,128)(2,1)} %get-tuple-element.119), channel_id=1, source_target_pairs={{0,2},{1,3},{2,0},{3,1},{4,6},{5,7},{6,4},{7,5},{8,10},{9,11},{10,... | collective-permute-start | bytes 589832 | tf_op jit(solution)/shard_map/cond/branch_1_fun/ppermute | solution.py:396
  260.7 35.7 %collective-permute-start.56 = (bf16[256,512]{1,0:T(8,128)(2,1)}, bf16[256,512]{1,0:T(8,128)(2,1)}, u32[]{:S(2)}, u32[]{:S(2)}) collective-permute-start(bf16[256,512]{1,0:T(8,128)(2,1)} %get-tuple-element.127), channel_id=1, source_target_pairs={{0,1},{1,0},{2,3},{3,2},{4,5},{5,4},{6,7},{7,6},{8,9},{9,8},{10,11... | collective-permute-start | bytes 786440 | tf_op jit(solution)/shard_map/cond/branch_1_fun/ppermute | solution.py:396
  280.0 16.4 %collective-permute-start.55 = (bf16[256,384]{1,0:T(8,128)(2,1)}, bf16[256,384]{1,0:T(8,128)(2,1)}, u32[]{:S(2)}, u32[]{:S(2)}) collective-permute-start(bf16[256,384]{1,0:T(8,128)(2,1)} %get-tuple-element.120), channel_id=1, source_target_pairs={{0,3},{1,0},{2,1},{3,2},{4,7},{5,4},{6,5},{7,6},{8,11},{9,8},{10,9... | collective-permute-start | bytes 589832 | tf_op jit(solution)/shard_map/cond/branch_1_fun/ppermute | solution.py:396
  282.1 16.5 %collective-permute-start.57 = (bf16[256,384]{1,0:T(8,128)(2,1)}, bf16[256,384]{1,0:T(8,128)(2,1)}, u32[]{:S(2)}, u32[]{:S(2)}) collective-permute-start(bf16[256,384]{1,0:T(8,128)(2,1)} %get-tuple-element.134), channel_id=1, source_target_pairs={{0,1},{1,2},{2,3},{3,0},{4,5},{5,6},{6,7},{7,4},{8,9},{9,10},{10,1... | collective-permute-start | bytes 589832 | tf_op jit(solution)/shard_map/cond/branch_1_fun/ppermute | solution.py:396
  282.1 25.7 %collective-permute-start.58 = (bf16[256,384]{1,0:T(8,128)(2,1)}, bf16[256,384]{1,0:T(8,128)(2,1)}, u32[]{:S(2)}, u32[]{:S(2)}) collective-permute-start(bf16[256,384]{1,0:T(8,128)(2,1)} %get-tuple-element.135), channel_id=1, source_target_pairs={{0,2},{1,3},{2,0},{3,1},{4,6},{5,7},{6,4},{7,5},{8,10},{9,11},{10,... | collective-permute-start | bytes 589832 | tf_op jit(solution)/shard_map/cond/branch_1_fun/ppermute | solution.py:396
  284.5 25.9 %collective-permute-start.59 = (bf16[256,384]{1,0:T(8,128)(2,1)}, bf16[256,384]{1,0:T(8,128)(2,1)}, u32[]{:S(2)}, u32[]{:S(2)}) collective-permute-start(bf16[256,384]{1,0:T(8,128)(2,1)} %get-tuple-element.136), channel_id=1, source_target_pairs={{0,3},{1,0},{2,1},{3,2},{4,7},{5,4},{6,5},{7,6},{8,11},{9,8},{10,9... | collective-permute-start | bytes 589832 | tf_op jit(solution)/shard_map/cond/branch_1_fun/ppermute | solution.py:396
  296.4 17.6 %collective-permute-start.49 = (bf16[256,256]{1,0:T(8,128)(2,1)}, bf16[256,256]{1,0:T(8,128)(2,1)}, u32[]{:S(2)}, u32[]{:S(2)}) collective-permute-start(bf16[256,256]{1,0:T(8,128)(2,1)} %get-tuple-element.139), channel_id=1, source_target_pairs={{0,1},{1,2},{2,3},{3,0},{4,5},{5,6},{6,7},{7,4},{8,9},{9,10},{10,1... | collective-permute-start | bytes 393224 | tf_op jit(solution)/shard_map/cond/branch_1_fun/ppermute | solution.py:396
  296.4 17.6 %collective-permute-start.50 = (bf16[256,256]{1,0:T(8,128)(2,1)}, bf16[256,256]{1,0:T(8,128)(2,1)}, u32[]{:S(2)}, u32[]{:S(2)}) collective-permute-start(bf16[256,256]{1,0:T(8,128)(2,1)} %get-tuple-element.140), channel_id=1, source_target_pairs={{0,2},{1,3},{2,0},{3,1},{4,6},{5,7},{6,4},{7,5},{8,10},{9,11},{10,... | collective-permute-start | bytes 393224 | tf_op jit(solution)/shard_map/cond/branch_1_fun/ppermute | solution.py:396
  298.6 15.5 %collective-permute-start.51 = (bf16[256,256]{1,0:T(8,128)(2,1)}, bf16[256,256]{1,0:T(8,128)(2,1)}, u32[]{:S(2)}, u32[]{:S(2)}) collective-permute-start(bf16[256,256]{1,0:T(8,128)(2,1)} %get-tuple-element.141), channel_id=1, source_target_pairs={{0,3},{1,0},{2,1},{3,2},{4,7},{5,4},{6,5},{7,6},{8,11},{9,8},{10,9... | collective-permute-start | bytes 393224 | tf_op jit(solution)/shard_map/cond/branch_1_fun/ppermute | solution.py:396

commit v2 on v1

--- a/solution.py
+++ b/solution.py
@@ -16,7 +16,7 @@
 AHEAD = 2
 VMEM_LIMIT = 67043328
 LANES = 128
-WITHIN = 64
+WITHIN = 32
 WIDE_HEADS = 3
 NARROW_HEADS = 5
 
@@ -163,7 +163,7 @@
     )(place, order, key_rows, value_rows, *pieces)
 
 
-def attend_body(group, column, place, order, lists, queries, *refs):
+def attend_body(group, whole, column, place, order, lists, queries, *refs):
     peers, heads = group.peers, group.heads
     pieces, refs = refs[: peers - 1], refs[peers - 1 :]
     sides, refs = refs[:3], refs[3:]
@@ -175,8 +175,14 @@
     q_tiles = block // TILE
     first_row = (place[0] // peers) * q_tiles
 
+    heads_dev = lists.shape[0] // whole
+
     def list_copy(head):
-        return pltpu.make_async_copy(lists.at[group.head(order, me, head)], tiles.at[head], t_sems.at[head])
+        number = group.head(order, me, head)
+        shift = lax.rem(place[0] + whole - number // heads_dev, whole)
+        return pltpu.make_async_copy(
+            lists.at[shift * heads_dev + lax.rem(number, heads_dev)], tiles.at[head], t_sems.at[head]
+        )
 
     def early(head):
         copies = [
@@ -308,8 +314,9 @@
     width = heads * HDIM
     pairs = (slots + 1) // 2
     work = heads * block * slots * TILE
+    whole = lax.axis_size("head")
     return pl.pallas_call(
-        functools.partial(attend_body, group, column),
+        functools.partial(attend_body, group, whole, column),
         out_shape=[jax.ShapeDtypeStruct((rows, width), jnp.bfloat16)] * peers,
         in_specs=[SMEM, SMEM] + [HBM] * (2 + peers - 1 + 3),
         out_specs=[HBM] * peers,
@@ -413,24 +420,22 @@
     return parts
 
 
-def plan(wide, heads_dev, peers):
+def plan(wide, local, heads_dev, peers):
     half = peers // 2
     base, wides, narrows = 0, [], []
     for heads in shares(wide, WIDE_HEADS):
         wides.append(Group(peers, base, heads))
         base += peers * heads
-    for heads in shares((heads_dev - wide) * (peers // half), NARROW_HEADS):
+    for heads in shares((heads_dev * peers - base - local) // half, NARROW_HEADS):
         narrows.append(Group(half, base, heads))
         base += half * heads
-    mixed = []
-    while wides or narrows:
-        mixed += narrows[:1] + wides[:1]
-        wides, narrows = wides[1:], narrows[1:]
-    return mixed
-
-
-def widths(heads_dev):
-    return sorted({-(-heads_dev // 2), -(-2 * heads_dev // 3), heads_dev})
+    mixed = [Group(1, base, local)] if local else []
+    return mixed + narrows[:1] + wides + narrows[1:]
+
+
+def cases(heads_dev, peers):
+    local = heads_dev * peers // 6 // (peers // 2) * (peers // 2)
+    return [(-(-heads_dev // 2), local), (-(-2 * heads_dev // 3), local), (heads_dev, 0)]
 
 
 def list_rows(key_tiles):
@@ -440,26 +445,31 @@
     base = (lax.axis_index("ctx") - 1) * cells
     local_ids = jnp.where(is_live, key_tiles, key_tiles[:, :, :1]) - base
     counts = jnp.sum(is_live.astype(jnp.int32), axis=2, keepdims=True)
-    half = cells // 2
-    own_half = (jnp.arange(cells, dtype=jnp.int32) // half * half)[None, :, None]
-    half_ids = local_ids // cells * half + local_ids % cells - own_half
-
-    def row(ids, width):
+    tile = jnp.arange(cells, dtype=jnp.int32)[None, :, None]
+
+    def row(part):
+        ids = local_ids // cells * part + local_ids % cells - tile // part * part
         ids = jnp.pad(ids, ((0, 0), (0, 0), (0, padded - slots)))
         ids = jnp.concatenate([counts, ids], axis=2)
-        return jnp.pad(ids, ((0, 0), (0, 0), (0, width - ids.shape[2])))
-
-    return jnp.concatenate([row(local_ids, WITHIN), row(half_ids, LANES - WITHIN)], axis=2).astype(jnp.int32)
+        return jnp.pad(ids, ((0, 0), (0, 0), (0, WITHIN - ids.shape[2])))
+
+    peers = lax.axis_size("head")
+    rows = [row(cells), row(cells // 2), row(cells // peers)]
+    rows = jnp.concatenate(rows, axis=2)
+    return jnp.pad(rows, ((0, 0), (0, 0), (0, LANES - rows.shape[2]))).astype(jnp.int32)
 
 
 def sorted_heads(key_tiles):
     heads_dev, cells, _ = key_tiles.shape
-    half = cells // 2
     is_live = key_tiles >= 0
-    tile_half = (jnp.arange(cells, dtype=jnp.int32) // half)[None, :, None]
-    crosses = jnp.any(is_live & (key_tiles % cells // half != tile_half), axis=(1, 2))
+    tile = jnp.arange(cells, dtype=jnp.int32)[None, :, None]
+
+    def leaves(part):
+        return jnp.any(is_live & (key_tiles % cells // part != tile // part), axis=(1, 2)).astype(jnp.int32)
+
+    kind = leaves(cells // 2) + leaves(cells // lax.axis_size("head"))
     longest = jnp.max(jnp.sum(is_live.astype(jnp.int32), axis=2), axis=1)
-    mine = crosses.astype(jnp.int32) * LANES + longest
+    mine = kind * LANES + longest
     tokens, peers = lax.axis_size("ctx"), lax.axis_size("head")
     spread = jnp.broadcast_to(mine[None], (tokens * peers, heads_dev))
     every = lax.all_to_all(spread, ("ctx", "head"), split_axis=0, concat_axis=0, tiled=True)
@@ -468,13 +478,16 @@
     ahead = (score[None, :] > score[:, None]) | ((score[None, :] == score[:, None]) & (index[None, :] < index[:, None]))
     rank = jnp.sum(ahead.astype(jnp.int32), axis=1)
     order = jnp.sum(jnp.where(rank[None, :] == index[:, None], index[None, :], 0), axis=1)
-    return order.astype(jnp.int32), jnp.sum((score >= LANES).astype(jnp.int32))
-
-
-def pipeline(groups, place, order, queries, key_rows, value_rows, key_tiles):
-    slots = key_tiles.shape[2]
+    crossing = jnp.sum((score >= 2 * LANES).astype(jnp.int32))
+    local = jnp.sum((score < LANES).astype(jnp.int32))
+    return order.astype(jnp.int32), crossing, local
+
+
+def pipeline(groups, slots, place, order, lists, queries, key_rows, value_rows):
+    whole = lax.axis_size("head")
     arrays = (queries, key_rows, value_rows)
     packed, arrived, joined, attended = {}, {}, {}, {}
+    movers = movers_of(groups)
 
     def send(index, pieces):
         arrived[index] = [
@@ -482,32 +495,26 @@
             for shift in range(1, groups[index].peers)
         ]
 
-    for kind, index in kernel_order(len(groups)):
-        if kind == "join" and index == 0:
-            rows = list_rows(after(key_tiles, place))
-            lists = gather_heads(rows)
+    for kind, index in kernel_order(groups):
         group = groups[index]
         peers = group.peers
         if kind == "pack":
-            results = pack(groups[index : index + 1] if index == 0 else groups[1:], place, order, arrays)
+            taken = movers[:AHEAD] if index == movers[0] else movers[AHEAD:]
+            results = pack([groups[i] for i in taken], place, order, arrays)
         elif kind == "join":
-            results = join(group, place, order, key_rows, value_rows, arrived[index])
+            results = join(group, place, order, key_rows, value_rows, arrived.get(index, []))
         else:
-            column = 0 if peers == lax.axis_size("head") else WITHIN
-            results = attend(
-                group, column, slots, place, order, lists, queries, arrived[index], joined[index]
-            )
+            column = 0 if peers == whole else 2 * WITHIN if peers == 1 else WITHIN
+            results = attend(group, column, slots, place, order, lists, queries, arrived.get(index, []), joined[index])
         if kind == "pack":
-            packed.update(zip(range(index, len(groups)), results))
-            for ahead in range(index, min(AHEAD, index + 1)):
-                send(ahead, packed[ahead])
+            packed.update(zip(taken, results))
         elif kind == "join":
             low, high = (along(results, side) for side in (1, -1))
             joined[index] = (low, results, high)
-            if index + AHEAD < len(groups):
-                send(index + AHEAD, after(packed[index + AHEAD], results))
         else:
             attended[index] = [results[0]] + [around(results[shift], peers, shift) for shift in range(1, peers)]
+        for ahead in sent_after(groups, kind, index):
+            send(ahead, packed[ahead] if kind == "pack" else after(packed[ahead], results))
         place = after(place, results)
     out = None
     last = len(groups) - 1
@@ -518,35 +525,57 @@
 
 
 def gather_heads(rows):
-    count = lax.axis_size("head")
-    spread = jnp.broadcast_to(rows[None], (count,) + rows.shape)
-    every = lax.all_to_all(spread, "head", split_axis=0, concat_axis=0, tiled=True)
-    return every.reshape((-1,) + rows.shape[1:])
+    peers = lax.axis_size("head")
+    return jnp.concatenate([rows] + [around(rows, peers, shift) for shift in range(1, peers)], axis=0)
 
 
 def plans(heads_dev, peers):
-    return [plan(wide, heads_dev, peers) for wide in widths(heads_dev)]
+    return [plan(wide, local, heads_dev, peers) for wide, local in cases(heads_dev, peers)]
 
 
 def shards(queries, key_rows, value_rows, key_tiles):
     peers = lax.axis_size("head")
     heads_dev = key_tiles.shape[0]
     place = lax.axis_index("head").astype(jnp.int32).reshape(1)
-    order, crossing = sorted_heads(key_tiles)
-    which = jnp.int32(0)
-    for wide in widths(heads_dev)[:-1]:
-        which = which + (crossing > wide * peers).astype(jnp.int32)
-    branches = [functools.partial(pipeline, groups) for groups in plans(heads_dev, peers)]
-    return lax.switch(which, branches, place, order, queries, key_rows, value_rows, key_tiles)
-
-
-def kernel_order(count):
-    order = [("pack", index) for index in range(min(2, count))]
-    for step in range(count + 1):
-        if step < count:
-            order.append(("join", step))
-        if step >= 1:
-            order.append(("attend", step - 1))
+    lists = gather_heads(list_rows(key_tiles))
+    order, crossing, local = sorted_heads(key_tiles)
+    which = jnp.int32(len(cases(heads_dev, peers)) - 1)
+    for number, (wide, locals_needed) in reversed(list(enumerate(cases(heads_dev, peers)[:-1]))):
+        which = jnp.where((crossing <= wide * peers) & (local >= locals_needed), number, which)
+    branches = [functools.partial(pipeline, groups, key_tiles.shape[2]) for groups in plans(heads_dev, peers)]
+    return lax.switch(which, branches, place, order, lists, queries, key_rows, value_rows)
+
+
+def movers_of(groups):
+    return [index for index, group in enumerate(groups) if group.peers > 1]
+
+
+def sent_after(groups, kind, index):
+    movers = movers_of(groups)
+    if index not in movers:
+        return []
+    number = movers.index(index)
+    if kind == "pack":
+        return movers[:AHEAD] if number == 0 else []
+    if kind == "join":
+        return movers[AHEAD : AHEAD + 1] if number == 0 else []
+    return movers[number + AHEAD + 1 : number + AHEAD + 2]
+
+
+def kernel_order(groups):
+    movers = movers_of(groups)
+    order = [("pack", movers[0])]
+    local = groups[0].peers == 1
+    if local:
+        order.append(("join", 0))
+    order += [("pack", index) for index in movers[AHEAD : AHEAD + 1]]
+    order.append(("join", movers[0]))
+    if local:
+        order.append(("attend", 0))
+    for index, following in zip(movers, movers[1:] + [None]):
+        if following is not None:
+            order.append(("join", following))
+        order.append(("attend", index))
     return order
 
 

time: 318 us -> 283 us (0.89)
  the two profiles are of different devices: /device:TPU:10 before, /device:TPU:5 now
where the time goes in v2:
time: 283 us; the launch traced here: 280 us
  Pallas kernels  108 us (38%)
  starting transfers between devices  81.6 us (29%)
  waiting for transfers between devices  79.2 us (28%)
  other arithmetic  5.71 us (2%)
    ppermute x23, waiting for transfers between devices, around(): return lax.ppermute(array, 'head', moves)  78.4 us
    pallas_call x5, Pallas kernels, attend(): pl.pallas_call(functools.partial(attend_body, group, whole, column), out_...  78.1 us
    ppermute x23, starting transfers between devices, around(): return lax.ppermute(array, 'head', moves)  45.4 us
    ppermute x10, starting transfers between devices, along(): lax.ppermute(array, 'ctx', [(i, i + shift) for i in range(count) if 0 <=...  29.8 us
    pallas_call x5, Pallas kernels, join(): pl.pallas_call(functools.partial(join_body, group), out_shape=jax.ShapeDt...  16 us
    pallas_call x2, Pallas kernels, pack(): pl.pallas_call(functools.partial(pack_body, groups), out_shape=outs, in_s...  7.57 us
    all_to_all x1, starting transfers between devices, sorted_heads(): lax.all_to_all(spread, ('ctx', 'head'), split_axis=0, concat_axis=0, tile...  6.38 us
    pallas_call x2, Pallas kernels, place_columns(): pl.pallas_call(functools.partial(place_body, groups, aliased), out_shape=...  6.16 us
  transfers between devices with their start and end apart: 34, of which 6 were waited for; matrix products, arithmetic and copies ran while one was open for 1% of the time, Pallas kernels for 35%

profile of v2, /device:TPU:5, one launch (start us, length us, event | category | flops | bytes accessed | tf_op | source)
XLA Modules:
  0.0 279.6 jit_solution(6440928421541117243)
XLA Ops:
  0.0 1.0 copy.39
  1.0 1.1 add_subtract_fusion.2
  2.2 1.4 fusion.10
  4.3 6.4 %all-to-all-start = ((s32[32,1,12]{2,1,0:T(1,128)}), s32[32,1,12]{2,1,0:T(1,128)S(1)}, u32[]{:S(2)}, u32[]{:S(2)}) async-start(s32[32,1,12]{2,1,0:T(1,128)} %broadcast_in_dim.20), calls=%async_computation | async-start | bytes 32768 | tf_op jit(solution)/shard_map/all_to_all | solution.py:475
  11.0 1.2 collective-permute-start.88
  12.2 2.2 collective-permute-start.89
  14.4 1.1 collective-permute-start.90
  20.8 258.6 %conditional.1 = (bf16[256,6144]{1,0:T(8,128)(2,1)}) conditional(s32[]{:T(128)} %clamp.3, (s32[]{:T(128)}, s32[48,48]{1,0:T(8,128)S(1)}, bf16[256,6144]{1,0:T(8,128)(2,1)}, bf16[256,6144]{1,0:T(8,128)(2,1)}, bf16[256,6144]{1,0:T(8,128)(2,1)}, /*index=5*/s32[48,8,128]{2,1,0:T(8,128)}, s32[]{:T(128)}, s32[48,48]{1,0:T(8,128)S(1)}, ...), branch_computations={%region_9.10_spmd, %region_10.11_spmd, %region_11.12_spmd} | conditional | flops 14495523840 | bytes 146305856 | solution.py:546
  21.6 3.7 %pack.8 = (bf16[3,256,512]{2,1,0:T(8,128)(2,1)}, bf16[3,256,384]{2,1,0:T(8,128)(2,1)}, bf16[3,256,384]{2,1,0:T(8,128)(2,1)}, bf16[3,256,384]{2,1,0:T(8,128)(2,1)}) custom-call(s32[1]{0:T(128)} %bitcast.1.place, s32[48]{0:T(128)} %select_reduce_fusion.1.order, bf16[256,6144]{1,0:T(8,128)(2,1)} %get-tuple-element.214.refs_0_.queries, ...), custom_call_target="tpu_custom_call" | custom-call | bytes 5111808 | tf_op jit(solution)/shard_map/cond/branch_1_fun/pack/pallas_call | solution.py:98
  25.3 3.1 %join.19.refs_1_ = bf16[2,256,1024]{2,1,0:T(8,128)(2,1)} custom-call(s32[1]{0:T(128)} %bitcast.1.place, s32[48]{0:T(128)} %select_reduce_fusion.1.order, bf16[256,6144]{1,0:T(8,128)(2,1)} %get-tuple-element.217.refs_1_.key_rows, bf16[256,6144]{1,0:T(8,128)(2,1)} %get-tuple-element.220.refs_2_.value_rows), custom_call_target="tpu_custom_call" | custom-call | bytes 2097152 | tf_op jit(solution)/shard_map/cond/branch_1_fun/join/pallas_call | solution.py:149
  28.4 3.5 %collective-permute-start.27 = (bf16[2,256,1024]{2,1,0:T(8,128)(2,1)}, bf16[2,256,1024]{2,1,0:T(8,128)(2,1)}, u32[]{:S(2)}, u32[]{:S(2)}) collective-permute-start(bf16[2,256,1024]{2,1,0:T(8,128)(2,1)} %join.19.refs_1_), channel_id=1, source_target_pairs={{0,4},{4,8},{8,12},{12,16},{16,20},{20,24},{24,28},{1,5},{5,9},{9,... | collective-permute-start | bytes 3145736 | tf_op jit(solution)/shard_map/cond/branch_1_fun/ppermute | solution.py:408
  31.9 1.9 collective-permute-start.28
  34.2 1.1 collective-permute-start.29
  36.0 40.7 %collective-permute-done.26.refs_0_ = bf16[3,256,512]{2,1,0:T(8,128)(2,1)} collective-permute-done((bf16[3,256,512]{2,1,0:T(8,128)(2,1)}, bf16[3,256,512]{2,1,0:T(8,128)(2,1)}, u32[]{:S(2)}, u32[]{:S(2)}) %collective-permute-start.26) | collective-permute-done | bytes 786464 | tf_op jit(solution)/shard_map/cond/branch_1_fun/ppermute | solution.py:403
  76.7 3.9 %pack.9 = (bf16[3,256,384]{2,1,0:T(8,128)(2,1)}, bf16[3,256,384]{2,1,0:T(8,128)(2,1)}, bf16[3,256,384]{2,1,0:T(8,128)(2,1)}, bf16[3,256,256]{2,1,0:T(8,128)(2,1)...) custom-call(s32[1]{0:T(128)} %bitcast.1.place, s32[48]{0:T(128)} %select_reduce_fusion.1.order, ...), custom_call_target="tpu_custom_call" | custom-call | bytes 5898240 | tf_op jit(solution)/shard_map/cond/branch_1_fun/pack/pallas_call | solution.py:98
  80.6 3.0 %join.20.refs_2_ = bf16[2,512,512]{2,1,0:T(8,128)(2,1)} custom-call(s32[1]{0:T(128)} %bitcast.1.place, s32[48]{0:T(128)} %select_reduce_fusion.1.order, bf16[256,6144]{1,0:T(8,128)(2,1)} %get-tuple-element.217.refs_1_.key_rows, bf16[256,6144]{1,0:T(8,128)(2,1)} %get-tuple-element.220.refs_2_.value_rows, bf16[3,256,512]{2,1,0:T(8,128)(2,1)} %collective-permute-done.26.refs_0_), custom_call_target="tpu_custom_call" | custom-call | bytes 2097152 | tf_op jit(solution)/shard_map/cond/branch_1_fun/join/pallas_call | solution.py:149
  83.7 5.5 %collective-permute-start.32 = (bf16[2,512,512]{2,1,0:T(8,128)(2,1)}, bf16[2,512,512]{2,1,0:T(8,128)(2,1)}, u32[]{:S(2)}, u32[]{:S(2)}) collective-permute-start(bf16[2,512,512]{2,1,0:T(8,128)(2,1)} %join.20.refs_2_), channel_id=1, source_target_pairs={{0,4},{4,8},{8,12},{12,16},{16,20},{20,24},{24,28},{1,5},{5,9},{9,... | collective-permute-start | bytes 3145736 | tf_op jit(solution)/shard_map/cond/branch_1_fun/ppermute | solution.py:408
  89.2 2.2 collective-permute-start.33
  91.4 12.5 %attend.19.refs_0_ = bf16[256,1024]{1,0:T(8,128)(2,1)} custom-call(s32[1]{0:T(128)} %bitcast.1.place, s32[48]{0:T(128)} %select_reduce_fusion.1.order, s32[48,8,128]{2,1,0:T(8,128)} %get-tuple-element.106.lists, bf16[256,6144]{1,0:T(8,128)(2,1)} %get-tuple-element.214.refs_0_.queries, bf16[2,256,1024]{2,1,0:T(8,128)(2,1)} %collective-permute-done.27.refs_0_, ...), custom_call_target="tpu_custom_call" | custom-call | flops 2415919104 | bytes 4194304 | tf_op jit(solution)/shard_map/cond/branch_1_fun/attend/pallas_call | solution.py:318
  103.9 3.4 %join.21.refs_4_ = bf16[2,1024,384]{2,1,0:T(8,128)(2,1)} custom-call(s32[1]{0:T(128)} %bitcast.1.place, s32[48]{0:T(128)} %select_reduce_fusion.1.order, bf16[256,6144]{1,0:T(8,128)(2,1)} %get-tuple-element.217.refs_1_.key_rows, bf16[256,6144]{1,0:T(8,128)(2,1)} %get-tuple-element.220.refs_2_.value_rows, ...), custom_call_target="tpu_custom_call" | custom-call | bytes 3145728 | tf_op jit(solution)/shard_map/cond/branch_1_fun/join/pallas_call | solution.py:149
  107.3 3.6 %collective-permute-start.37 = (bf16[2,1024,384]{2,1,0:T(8,128)(2,1)}, bf16[2,1024,384]{2,1,0:T(8,128)(2,1)}, u32[]{:S(2)}, u32[]{:S(2)}) collective-permute-start(bf16[2,1024,384]{2,1,0:T(8,128)(2,1)} %join.21.refs_4_), channel_id=1, source_target_pairs={{0,4},{4,8},{8,12},{12,16},{16,20},{20,24},{24,28},{1,5},{5,9},{9,... | collective-permute-start | bytes 4718600 | tf_op jit(solution)/shard_map/cond/branch_1_fun/ppermute | solution.py:408
  111.0 1.9 collective-permute-start.38
  112.9 1.8 collective-permute-start.34
  114.7 2.2 collective-permute-start.36
  116.9 13.4 %attend.20 = (bf16[256,512]{1,0:T(8,128)(2,1)}, bf16[256,512]{1,0:T(8,128)(2,1)}) custom-call(s32[1]{0:T(128)} %bitcast.1.place, s32[48]{0:T(128)} %select_reduce_fusion.1.order, s32[48,8,128]{2,1,0:T(8,128)} %get-tuple-element.106.lists, bf16[256,6144]{1,0:T(8,128)(2,1)} %get-tuple-element.214.refs_0_.queries, ...), custom_call_target="tpu_custom_call" | custom-call | flops 2415919104 | bytes 4194304 | tf_op jit(solution)/shard_map/cond/branch_1_fun/attend/pallas_call | solution.py:318
  130.3 25.3 %collective-permute-done.35.refs_1_ = bf16[3,256,384]{2,1,0:T(8,128)(2,1)} collective-permute-done((bf16[3,256,384]{2,1,0:T(8,128)(2,1)}, bf16[3,256,384]{2,1,0:T(8,128)(2,1)}, u32[]{:S(2)}, u32[]{:S(2)}) %collective-permute-start.35) | collective-permute-done | bytes 589856 | tf_op jit(solution)/shard_map/cond/branch_1_fun/ppermute | solution.py:403
  155.7 3.5 %join.22.refs_4_ = bf16[2,1024,384]{2,1,0:T(8,128)(2,1)} custom-call(s32[1]{0:T(128)} %bitcast.1.place, s32[48]{0:T(128)} %select_reduce_fusion.1.order, bf16[256,6144]{1,0:T(8,128)(2,1)} %get-tuple-element.217.refs_1_.key_rows, bf16[256,6144]{1,0:T(8,128)(2,1)} %get-tuple-element.220.refs_2_.value_rows, ...), custom_call_target="tpu_custom_call" | custom-call | bytes 3145728 | tf_op jit(solution)/shard_map/cond/branch_1_fun/join/pallas_call | solution.py:149
  159.1 3.7 %collective-permute-start.42 = (bf16[2,1024,384]{2,1,0:T(8,128)(2,1)}, bf16[2,1024,384]{2,1,0:T(8,128)(2,1)}, u32[]{:S(2)}, u32[]{:S(2)}) collective-permute-start(bf16[2,1024,384]{2,1,0:T(8,128)(2,1)} %join.22.refs_4_), channel_id=1, source_target_pairs={{0,4},{4,8},{8,12},{12,16},{16,20},{20,24},{24,28},{1,5},{5,9},{9,... | collective-permute-start | bytes 4718600 | tf_op jit(solution)/shard_map/cond/branch_1_fun/ppermute | solution.py:408
  162.8 1.9 collective-permute-start.43
  164.7 12.9 %collective-permute-start.39 = (bf16[3,256,256]{2,1,0:T(8,128)(2,1)}, bf16[3,256,256]{2,1,0:T(8,128)(2,1)}, u32[]{:S(2)}, u32[]{:S(2)}) collective-permute-start(bf16[3,256,256]{2,1,0:T(8,128)(2,1)} %get-tuple-element.121), channel_id=1, source_target_pairs={{0,1},{1,2},{2,3},{3,0},{4,5},{5,6},{6,7},{7,4},{8,9},{9,10},{10,1... | collective-permute-start | bytes 1179656 | tf_op jit(solution)/shard_map/cond/branch_1_fun/ppermute | solution.py:403
  178.1 1.7 collective-permute-start.41
  179.8 23.3 %attend.21 = (bf16[256,384]{1,0:T(8,128)(2,1)}, bf16[256,384]{1,0:T(8,128)(2,1)}, bf16[256,384]{1,0:T(8,128)(2,1)}, bf16[256,384]{1,0:T(8,128)(2,1)}) custom-call(s32[1]{0:T(128)} %bitcast.1.place, s32[48]{0:T(128)} %select_reduce_fusion.1.order, s32[48,8,128]{2,1,0:T(8,128)} %get-tuple-element.106.lists, ...), custom_call_target="tpu_custom_call" | custom-call | flops 3623878656 | bytes 6291456 | tf_op jit(solution)/shard_map/cond/branch_1_fun/attend/pallas_call | solution.py:318
  203.1 1.5 collective-permute-done.40.refs_1_
  204.6 3.0 %join.23.refs_4_ = bf16[2,1024,256]{2,1,0:T(8,128)(2,1)} custom-call(s32[1]{0:T(128)} %bitcast.1.place, s32[48]{0:T(128)} %select_reduce_fusion.1.order, bf16[256,6144]{1,0:T(8,128)(2,1)} %get-tuple-element.217.refs_1_.key_rows, bf16[256,6144]{1,0:T(8,128)(2,1)} %get-tuple-element.220.refs_2_.value_rows, ...), custom_call_target="tpu_custom_call" | custom-call | bytes 2097152 | tf_op jit(solution)/shard_map/cond/branch_1_fun/join/pallas_call | solution.py:149
  207.7 3.6 %collective-permute-start.44 = (bf16[2,1024,256]{2,1,0:T(8,128)(2,1)}, bf16[2,1024,256]{2,1,0:T(8,128)(2,1)}, u32[]{:S(2)}, u32[]{:S(2)}) collective-permute-start(bf16[2,1024,256]{2,1,0:T(8,128)(2,1)} %join.23.refs_4_), channel_id=1, source_target_pairs={{0,4},{4,8},{8,12},{12,16},{16,20},{20,24},{24,28},{1,5},{5,9},{9,... | collective-permute-start | bytes 3145736 | tf_op jit(solution)/shard_map/cond/branch_1_fun/ppermute | solution.py:408
  211.3 1.9 collective-permute-start.45
  213.2 8.7 %collective-permute-start.49 = (bf16[256,512]{1,0:T(8,128)(2,1)}, bf16[256,512]{1,0:T(8,128)(2,1)}, u32[]{:S(2)}, u32[]{:S(2)}) collective-permute-start(bf16[256,512]{1,0:T(8,128)(2,1)} %get-tuple-element.110), channel_id=1, source_target_pairs={{0,1},{1,0},{2,3},{3,2},{4,5},{5,4},{6,7},{7,6},{8,9},{9,8},{10,11... | collective-permute-start | bytes 786440 | tf_op jit(solution)/shard_map/cond/branch_1_fun/ppermute | solution.py:403
  222.0 1.8 collective-permute-start.51
  223.8 19.2 %attend.22 = (bf16[256,384]{1,0:T(8,128)(2,1)}, bf16[256,384]{1,0:T(8,128)(2,1)}, bf16[256,384]{1,0:T(8,128)(2,1)}, bf16[256,384]{1,0:T(8,128)(2,1)}) custom-call(s32[1]{0:T(128)} %bitcast.1.place, s32[48]{0:T(128)} %select_reduce_fusion.1.order, s32[48,8,128]{2,1,0:T(8,128)} %get-tuple-element.106.lists, ...), custom_call_target="tpu_custom_call" | custom-call | flops 3623878656 | bytes 6291456 | tf_op jit(solution)/shard_map/cond/branch_1_fun/attend/pallas_call | solution.py:318
  243.1 1.7 collective-permute-start.53
  244.8 1.2 collective-permute-start.54
  246.0 2.3 collective-permute-start.55
  248.3 9.6 %attend.23 = (bf16[256,256]{1,0:T(8,128)(2,1)}, bf16[256,256]{1,0:T(8,128)(2,1)}, bf16[256,256]{1,0:T(8,128)(2,1)}, bf16[256,256]{1,0:T(8,128)(2,1)}) custom-call(s32[1]{0:T(128)} %bitcast.1.place, s32[48]{0:T(128)} %select_reduce_fusion.1.order, s32[48,8,128]{2,1,0:T(8,128)} %get-tuple-element.106.lists, ...), custom_call_target="tpu_custom_call" | custom-call | flops 2415919104 | bytes 4194304 | tf_op jit(solution)/shard_map/cond/branch_1_fun/attend/pallas_call | solution.py:318
  258.8 3.1 %collective-permute-start.48 = (bf16[256,256]{1,0:T(8,128)(2,1)}, bf16[256,256]{1,0:T(8,128)(2,1)}, u32[]{:S(2)}, u32[]{:S(2)}) collective-permute-start(bf16[256,256]{1,0:T(8,128)(2,1)} %get-tuple-element.133), channel_id=1, source_target_pairs={{0,3},{1,0},{2,1},{3,2},{4,7},{5,4},{6,5},{7,6},{8,11},{9,8},{10,9... | collective-permute-start | bytes 393224 | tf_op jit(solution)/shard_map/cond/branch_1_fun/ppermute | solution.py:403
  261.9 4.7 %collective-permute-done.54.refs_9_ = bf16[256,384]{1,0:T(8,128)(2,1)} collective-permute-done((bf16[256,384]{1,0:T(8,128)(2,1)}, bf16[256,384]{1,0:T(8,128)(2,1)}, u32[]{:S(2)}, u32[]{:S(2)}) %collective-permute-start.54) | collective-permute-done | bytes 196640 | tf_op jit(solution)/shard_map/cond/branch_1_fun/ppermute | solution.py:403
  266.6 3.6 %place.8.refs_4_ = bf16[256,6144]{1,0:T(8,128)(2,1)} custom-call(s32[1]{0:T(128)} %bitcast.1.place, s32[48]{0:T(128)} %select_reduce_fusion.1.order, bf16[256,1024]{1,0:T(8,128)(2,1)} %attend.19.refs_0_, bf16[256,512]{1,0:T(8,128)(2,1)} %get-tuple-element.109.refs_1_, bf16[256,512]{1,0:T(8,128)(2,1)} %collective-permute-done.49.refs_2_, ...), custom_call_target="tpu_custom_call" | custom-call | bytes 5242880 | tf_op jit(solution)/shard_map/cond/branch_1_fun/place/pallas_call | solution.py:383
  270.2 6.2 %collective-permute-done.47.refs_2_ = bf16[256,256]{1,0:T(8,128)(2,1)} collective-permute-done((bf16[256,256]{1,0:T(8,128)(2,1)}, bf16[256,256]{1,0:T(8,128)(2,1)}, u32[]{:S(2)}, u32[]{:S(2)}) %collective-permute-start.47) | collective-permute-done | bytes 131104 | tf_op jit(solution)/shard_map/cond/branch_1_fun/ppermute | solution.py:403
  276.4 2.5 place.9
  (59 shorter events, 7.9 us)
Async XLA Ops:
  4.3 12.0 %all-to-all-start = ((s32[32,1,12]{2,1,0:T(1,128)}), s32[32,1,12]{2,1,0:T(1,128)S(1)}, u32[]{:S(2)}, u32[]{:S(2)}) async-start(s32[32,1,12]{2,1,0:T(1,128)} %broadcast_in_dim.20), calls=%async_computation | async-start | bytes 32768 | tf_op jit(solution)/shard_map/all_to_all | solution.py:475
  11.0 9.1 %collective-permute-start.88 = (s32[12,8,128]{2,1,0:T(8,128)S(1)}, s32[12,8,128]{2,1,0:T(8,128)S(1)}, u32[]{:S(2)}, u32[]{:S(2)}) collective-permute-start(s32[12,8,128]{2,1,0:T(8,128)S(1)} %pad.17), channel_id=1, source_target_pairs={{0,1},{1,2},{2,3},{3,0},{4,5},{5,6},{6,7},{7,4},{8,9},{9,10},{10,1... | collective-permute-start | bytes 147464 | tf_op jit(solution)/shard_map/ppermute | solution.py:403
  12.2 7.9 %collective-permute-start.89 = (s32[12,8,128]{2,1,0:T(8,128)S(1)}, s32[12,8,128]{2,1,0:T(8,128)S(1)}, u32[]{:S(2)}, u32[]{:S(2)}) collective-permute-start(s32[12,8,128]{2,1,0:T(8,128)S(1)} %pad.17), channel_id=1, source_target_pairs={{0,2},{1,3},{2,0},{3,1},{4,6},{5,7},{6,4},{7,5},{8,10},{9,11},{10,... | collective-permute-start | bytes 147464 | tf_op jit(solution)/shard_map/ppermute | solution.py:403
  14.4 5.7 %collective-permute-start.90 = (s32[12,8,128]{2,1,0:T(8,128)S(1)}, s32[12,8,128]{2,1,0:T(8,128)S(1)}, u32[]{:S(2)}, u32[]{:S(2)}) collective-permute-start(s32[12,8,128]{2,1,0:T(8,128)S(1)} %pad.17), channel_id=1, source_target_pairs={{0,3},{1,0},{2,1},{3,2},{4,7},{5,4},{6,5},{7,6},{8,11},{9,8},{10,9... | collective-permute-start | bytes 147464 | tf_op jit(solution)/shard_map/ppermute | solution.py:403
  28.4 55.2 %collective-permute-start.27 = (bf16[2,256,1024]{2,1,0:T(8,128)(2,1)}, bf16[2,256,1024]{2,1,0:T(8,128)(2,1)}, u32[]{:S(2)}, u32[]{:S(2)}) collective-permute-start(bf16[2,256,1024]{2,1,0:T(8,128)(2,1)} %join.19.refs_1_), channel_id=1, source_target_pairs={{0,4},{4,8},{8,12},{12,16},{16,20},{20,24},{24,28},{1,5},{5,9},{9,... | collective-permute-start | bytes 3145736 | tf_op jit(solution)/shard_map/cond/branch_1_fun/ppermute | solution.py:408
  31.9 57.3 %collective-permute-start.28 = (bf16[2,256,1024]{2,1,0:T(8,128)(2,1)}, bf16[2,256,1024]{2,1,0:T(8,128)(2,1)}, u32[]{:S(2)}, u32[]{:S(2)}) collective-permute-start(bf16[2,256,1024]{2,1,0:T(8,128)(2,1)} %join.19.refs_1_), channel_id=1, source_target_pairs={{4,0},{8,4},{12,8},{16,12},{20,16},{24,20},{28,24},{5,1},{9,5},{13... | collective-permute-start | bytes 3145736 | tf_op jit(solution)/shard_map/cond/branch_1_fun/ppermute | solution.py:408
  33.8 42.9 %collective-permute-start.26 = (bf16[3,256,512]{2,1,0:T(8,128)(2,1)}, bf16[3,256,512]{2,1,0:T(8,128)(2,1)}, u32[]{:S(2)}, u32[]{:S(2)}) collective-permute-start(bf16[3,256,512]{2,1,0:T(8,128)(2,1)} %get-tuple-element.92), channel_id=1, source_target_pairs={{0,1},{1,0},{2,3},{3,2},{4,5},{5,4},{6,7},{7,6},{8,9},{9,8},{10,11... | collective-permute-start | bytes 2359304 | tf_op jit(solution)/shard_map/cond/branch_1_fun/ppermute | solution.py:403
  34.2 69.6 %collective-permute-start.29 = (bf16[3,256,384]{2,1,0:T(8,128)(2,1)}, bf16[3,256,384]{2,1,0:T(8,128)(2,1)}, u32[]{:S(2)}, u32[]{:S(2)}) collective-permute-start(bf16[3,256,384]{2,1,0:T(8,128)(2,1)} %get-tuple-element.93), channel_id=1, source_target_pairs={{0,1},{1,2},{2,3},{3,0},{4,5},{5,6},{6,7},{7,4},{8,9},{9,10},{10,1... | collective-permute-start | bytes 1769480 | tf_op jit(solution)/shard_map/cond/branch_1_fun/ppermute | solution.py:403
  35.4 68.5 %collective-permute-start.30 = (bf16[3,256,384]{2,1,0:T(8,128)(2,1)}, bf16[3,256,384]{2,1,0:T(8,128)(2,1)}, u32[]{:S(2)}, u32[]{:S(2)}) collective-permute-start(bf16[3,256,384]{2,1,0:T(8,128)(2,1)} %get-tuple-element.94), channel_id=1, source_target_pairs={{0,2},{1,3},{2,0},{3,1},{4,6},{5,7},{6,4},{7,5},{8,10},{9,11},{10,... | collective-permute-start | bytes 1769480 | tf_op jit(solution)/shard_map/cond/branch_1_fun/ppermute | solution.py:403
  76.7 27.2 %collective-permute-start.31 = (bf16[3,256,384]{2,1,0:T(8,128)(2,1)}, bf16[3,256,384]{2,1,0:T(8,128)(2,1)}, u32[]{:S(2)}, u32[]{:S(2)}) collective-permute-start(bf16[3,256,384]{2,1,0:T(8,128)(2,1)} %get-tuple-element.95), channel_id=1, source_target_pairs={{0,3},{1,0},{2,1},{3,2},{4,7},{5,4},{6,5},{7,6},{8,11},{9,8},{10,9... | collective-permute-start | bytes 1769480 | tf_op jit(solution)/shard_map/cond/branch_1_fun/ppermute | solution.py:403
  83.7 31.0 %collective-permute-start.32 = (bf16[2,512,512]{2,1,0:T(8,128)(2,1)}, bf16[2,512,512]{2,1,0:T(8,128)(2,1)}, u32[]{:S(2)}, u32[]{:S(2)}) collective-permute-start(bf16[2,512,512]{2,1,0:T(8,128)(2,1)} %join.20.refs_2_), channel_id=1, source_target_pairs={{0,4},{4,8},{8,12},{12,16},{16,20},{20,24},{24,28},{1,5},{5,9},{9,... | collective-permute-start | bytes 3145736 | tf_op jit(solution)/shard_map/cond/branch_1_fun/ppermute | solution.py:408
  89.2 25.5 %collective-permute-start.33 = (bf16[2,512,512]{2,1,0:T(8,128)(2,1)}, bf16[2,512,512]{2,1,0:T(8,128)(2,1)}, u32[]{:S(2)}, u32[]{:S(2)}) collective-permute-start(bf16[2,512,512]{2,1,0:T(8,128)(2,1)} %join.20.refs_2_), channel_id=1, source_target_pairs={{4,0},{8,4},{12,8},{16,12},{20,16},{24,20},{28,24},{5,1},{9,5},{13... | collective-permute-start | bytes 3145736 | tf_op jit(solution)/shard_map/cond/branch_1_fun/ppermute | solution.py:408
  107.3 70.3 %collective-permute-start.37 = (bf16[2,1024,384]{2,1,0:T(8,128)(2,1)}, bf16[2,1024,384]{2,1,0:T(8,128)(2,1)}, u32[]{:S(2)}, u32[]{:S(2)}) collective-permute-start(bf16[2,1024,384]{2,1,0:T(8,128)(2,1)} %join.21.refs_4_), channel_id=1, source_target_pairs={{0,4},{4,8},{8,12},{12,16},{16,20},{20,24},{24,28},{1,5},{5,9},{9,... | collective-permute-start | bytes 4718600 | tf_op jit(solution)/shard_map/cond/branch_1_fun/ppermute | solution.py:408
  111.0 67.2 %collective-permute-start.38 = (bf16[2,1024,384]{2,1,0:T(8,128)(2,1)}, bf16[2,1024,384]{2,1,0:T(8,128)(2,1)}, u32[]{:S(2)}, u32[]{:S(2)}) collective-permute-start(bf16[2,1024,384]{2,1,0:T(8,128)(2,1)} %join.21.refs_4_), channel_id=1, source_target_pairs={{4,0},{8,4},{12,8},{16,12},{20,16},{24,20},{28,24},{5,1},{9,5},{13... | collective-permute-start | bytes 4718600 | tf_op jit(solution)/shard_map/cond/branch_1_fun/ppermute | solution.py:408
  112.9 17.4 %collective-permute-start.34 = (bf16[3,256,384]{2,1,0:T(8,128)(2,1)}, bf16[3,256,384]{2,1,0:T(8,128)(2,1)}, u32[]{:S(2)}, u32[]{:S(2)}) collective-permute-start(bf16[3,256,384]{2,1,0:T(8,128)(2,1)} %get-tuple-element.112), channel_id=1, source_target_pairs={{0,1},{1,2},{2,3},{3,0},{4,5},{5,6},{6,7},{7,4},{8,9},{9,10},{10,1... | collective-permute-start | bytes 1769480 | tf_op jit(solution)/shard_map/cond/branch_1_fun/ppermute | solution.py:403
  114.7 40.9 %collective-permute-start.35 = (bf16[3,256,384]{2,1,0:T(8,128)(2,1)}, bf16[3,256,384]{2,1,0:T(8,128)(2,1)}, u32[]{:S(2)}, u32[]{:S(2)}) collective-permute-start(bf16[3,256,384]{2,1,0:T(8,128)(2,1)} %get-tuple-element.113), channel_id=1, source_target_pairs={{0,2},{1,3},{2,0},{3,1},{4,6},{5,7},{6,4},{7,5},{8,10},{9,11},{10,... | collective-permute-start | bytes 1769480 | tf_op jit(solution)/shard_map/cond/branch_1_fun/ppermute | solution.py:403
  114.7 40.9 %collective-permute-start.36 = (bf16[3,256,384]{2,1,0:T(8,128)(2,1)}, bf16[3,256,384]{2,1,0:T(8,128)(2,1)}, u32[]{:S(2)}, u32[]{:S(2)}) collective-permute-start(bf16[3,256,384]{2,1,0:T(8,128)(2,1)} %get-tuple-element.114), channel_id=1, source_target_pairs={{0,3},{1,0},{2,1},{3,2},{4,7},{5,4},{6,5},{7,6},{8,11},{9,8},{10,9... | collective-permute-start | bytes 1769480 | tf_op jit(solution)/shard_map/cond/branch_1_fun/ppermute | solution.py:403
  159.1 62.8 %collective-permute-start.42 = (bf16[2,1024,384]{2,1,0:T(8,128)(2,1)}, bf16[2,1024,384]{2,1,0:T(8,128)(2,1)}, u32[]{:S(2)}, u32[]{:S(2)}) collective-permute-start(bf16[2,1024,384]{2,1,0:T(8,128)(2,1)} %join.22.refs_4_), channel_id=1, source_target_pairs={{0,4},{4,8},{8,12},{12,16},{16,20},{20,24},{24,28},{1,5},{5,9},{9,... | collective-permute-start | bytes 4718600 | tf_op jit(solution)/shard_map/cond/branch_1_fun/ppermute | solution.py:408
  162.8 59.2 %collective-permute-start.43 = (bf16[2,1024,384]{2,1,0:T(8,128)(2,1)}, bf16[2,1024,384]{2,1,0:T(8,128)(2,1)}, u32[]{:S(2)}, u32[]{:S(2)}) collective-permute-start(bf16[2,1024,384]{2,1,0:T(8,128)(2,1)} %join.22.refs_4_), channel_id=1, source_target_pairs={{4,0},{8,4},{12,8},{16,12},{20,16},{24,20},{28,24},{5,1},{9,5},{13... | collective-permute-start | bytes 4718600 | tf_op jit(solution)/shard_map/cond/branch_1_fun/ppermute | solution.py:408
  164.7 38.4 %collective-permute-start.39 = (bf16[3,256,256]{2,1,0:T(8,128)(2,1)}, bf16[3,256,256]{2,1,0:T(8,128)(2,1)}, u32[]{:S(2)}, u32[]{:S(2)}) collective-permute-start(bf16[3,256,256]{2,1,0:T(8,128)(2,1)} %get-tuple-element.121), channel_id=1, source_target_pairs={{0,1},{1,2},{2,3},{3,0},{4,5},{5,6},{6,7},{7,4},{8,9},{9,10},{10,1... | collective-permute-start | bytes 1179656 | tf_op jit(solution)/shard_map/cond/branch_1_fun/ppermute | solution.py:403
  177.6 27.0 %collective-permute-start.40 = (bf16[3,256,256]{2,1,0:T(8,128)(2,1)}, bf16[3,256,256]{2,1,0:T(8,128)(2,1)}, u32[]{:S(2)}, u32[]{:S(2)}) collective-permute-start(bf16[3,256,256]{2,1,0:T(8,128)(2,1)} %get-tuple-element.122), channel_id=1, source_target_pairs={{0,2},{1,3},{2,0},{3,1},{4,6},{5,7},{6,4},{7,5},{8,10},{9,11},{10,... | collective-permute-start | bytes 1179656 | tf_op jit(solution)/shard_map/cond/branch_1_fun/ppermute | solution.py:403
  178.1 26.5 %collective-permute-start.41 = (bf16[3,256,256]{2,1,0:T(8,128)(2,1)}, bf16[3,256,256]{2,1,0:T(8,128)(2,1)}, u32[]{:S(2)}, u32[]{:S(2)}) collective-permute-start(bf16[3,256,256]{2,1,0:T(8,128)(2,1)} %get-tuple-element.123), channel_id=1, source_target_pairs={{0,3},{1,0},{2,1},{3,2},{4,7},{5,4},{6,5},{7,6},{8,11},{9,8},{10,9... | collective-permute-start | bytes 1179656 | tf_op jit(solution)/shard_map/cond/branch_1_fun/ppermute | solution.py:403
  207.7 37.2 %collective-permute-start.44 = (bf16[2,1024,256]{2,1,0:T(8,128)(2,1)}, bf16[2,1024,256]{2,1,0:T(8,128)(2,1)}, u32[]{:S(2)}, u32[]{:S(2)}) collective-permute-start(bf16[2,1024,256]{2,1,0:T(8,128)(2,1)} %join.23.refs_4_), channel_id=1, source_target_pairs={{0,4},{4,8},{8,12},{12,16},{16,20},{20,24},{24,28},{1,5},{5,9},{9,... | collective-permute-start | bytes 3145736 | tf_op jit(solution)/shard_map/cond/branch_1_fun/ppermute | solution.py:408
  211.3 34.7 %collective-permute-start.45 = (bf16[2,1024,256]{2,1,0:T(8,128)(2,1)}, bf16[2,1024,256]{2,1,0:T(8,128)(2,1)}, u32[]{:S(2)}, u32[]{:S(2)}) collective-permute-start(bf16[2,1024,256]{2,1,0:T(8,128)(2,1)} %join.23.refs_4_), channel_id=1, source_target_pairs={{4,0},{8,4},{12,8},{16,12},{20,16},{24,20},{28,24},{5,1},{9,5},{13... | collective-permute-start | bytes 3145736 | tf_op jit(solution)/shard_map/cond/branch_1_fun/ppermute | solution.py:408
  213.2 29.8 %collective-permute-start.49 = (bf16[256,512]{1,0:T(8,128)(2,1)}, bf16[256,512]{1,0:T(8,128)(2,1)}, u32[]{:S(2)}, u32[]{:S(2)}) collective-permute-start(bf16[256,512]{1,0:T(8,128)(2,1)} %get-tuple-element.110), channel_id=1, source_target_pairs={{0,1},{1,0},{2,3},{3,2},{4,5},{5,4},{6,7},{7,6},{8,9},{9,8},{10,11... | collective-permute-start | bytes 786440 | tf_op jit(solution)/shard_map/cond/branch_1_fun/ppermute | solution.py:403
  221.9 21.2 %collective-permute-start.50 = (bf16[256,384]{1,0:T(8,128)(2,1)}, bf16[256,384]{1,0:T(8,128)(2,1)}, u32[]{:S(2)}, u32[]{:S(2)}) collective-permute-start(bf16[256,384]{1,0:T(8,128)(2,1)} %get-tuple-element.117), channel_id=1, source_target_pairs={{0,1},{1,2},{2,3},{3,0},{4,5},{5,6},{6,7},{7,4},{8,9},{9,10},{10,1... | collective-permute-start | bytes 589832 | tf_op jit(solution)/shard_map/cond/branch_1_fun/ppermute | solution.py:403
  222.0 35.9 %collective-permute-start.51 = (bf16[256,384]{1,0:T(8,128)(2,1)}, bf16[256,384]{1,0:T(8,128)(2,1)}, u32[]{:S(2)}, u32[]{:S(2)}) collective-permute-start(bf16[256,384]{1,0:T(8,128)(2,1)} %get-tuple-element.118), channel_id=1, source_target_pairs={{0,2},{1,3},{2,0},{3,1},{4,6},{5,7},{6,4},{7,5},{8,10},{9,11},{10,... | collective-permute-start | bytes 589832 | tf_op jit(solution)/shard_map/cond/branch_1_fun/ppermute | solution.py:403
  243.1 15.0 %collective-permute-start.52 = (bf16[256,384]{1,0:T(8,128)(2,1)}, bf16[256,384]{1,0:T(8,128)(2,1)}, u32[]{:S(2)}, u32[]{:S(2)}) collective-permute-start(bf16[256,384]{1,0:T(8,128)(2,1)} %get-tuple-element.119), channel_id=1, source_target_pairs={{0,3},{1,0},{2,1},{3,2},{4,7},{5,4},{6,5},{7,6},{8,11},{9,8},{10,9... | collective-permute-start | bytes 589832 | tf_op jit(solution)/shard_map/cond/branch_1_fun/ppermute | solution.py:403
  243.1 15.7 %collective-permute-start.53 = (bf16[256,384]{1,0:T(8,128)(2,1)}, bf16[256,384]{1,0:T(8,128)(2,1)}, u32[]{:S(2)}, u32[]{:S(2)}) collective-permute-start(bf16[256,384]{1,0:T(8,128)(2,1)} %get-tuple-element.126), channel_id=1, source_target_pairs={{0,1},{1,2},{2,3},{3,0},{4,5},{5,6},{6,7},{7,4},{8,9},{9,10},{10,1... | collective-permute-start | bytes 589832 | tf_op jit(solution)/shard_map/cond/branch_1_fun/ppermute | solution.py:403
  244.8 21.7 %collective-permute-start.54 = (bf16[256,384]{1,0:T(8,128)(2,1)}, bf16[256,384]{1,0:T(8,128)(2,1)}, u32[]{:S(2)}, u32[]{:S(2)}) collective-permute-start(bf16[256,384]{1,0:T(8,128)(2,1)} %get-tuple-element.127), channel_id=1, source_target_pairs={{0,2},{1,3},{2,0},{3,1},{4,6},{5,7},{6,4},{7,5},{8,10},{9,11},{10,... | collective-permute-start | bytes 589832 | tf_op jit(solution)/shard_map/cond/branch_1_fun/ppermute | solution.py:403
  246.0 20.5 %collective-permute-start.55 = (bf16[256,384]{1,0:T(8,128)(2,1)}, bf16[256,384]{1,0:T(8,128)(2,1)}, u32[]{:S(2)}, u32[]{:S(2)}) collective-permute-start(bf16[256,384]{1,0:T(8,128)(2,1)} %get-tuple-element.128), channel_id=1, source_target_pairs={{0,3},{1,0},{2,1},{3,2},{4,7},{5,4},{6,5},{7,6},{8,11},{9,8},{10,9... | collective-permute-start | bytes 589832 | tf_op jit(solution)/shard_map/cond/branch_1_fun/ppermute | solution.py:403
  258.0 12.3 %collective-permute-start.46 = (bf16[256,256]{1,0:T(8,128)(2,1)}, bf16[256,256]{1,0:T(8,128)(2,1)}, u32[]{:S(2)}, u32[]{:S(2)}) collective-permute-start(bf16[256,256]{1,0:T(8,128)(2,1)} %get-tuple-element.131), channel_id=1, source_target_pairs={{0,1},{1,2},{2,3},{3,0},{4,5},{5,6},{6,7},{7,4},{8,9},{9,10},{10,1... | collective-permute-start | bytes 393224 | tf_op jit(solution)/shard_map/cond/branch_1_fun/ppermute | solution.py:403
  258.0 18.4 %collective-permute-start.47 = (bf16[256,256]{1,0:T(8,128)(2,1)}, bf16[256,256]{1,0:T(8,128)(2,1)}, u32[]{:S(2)}, u32[]{:S(2)}) collective-permute-start(bf16[256,256]{1,0:T(8,128)(2,1)} %get-tuple-element.132), channel_id=1, source_target_pairs={{0,2},{1,3},{2,0},{3,1},{4,6},{5,7},{6,4},{7,5},{8,10},{9,11},{10,... | collective-permute-start | bytes 393224 | tf_op jit(solution)/shard_map/cond/branch_1_fun/ppermute | solution.py:403
  258.8 17.6 %collective-permute-start.48 = (bf16[256,256]{1,0:T(8,128)(2,1)}, bf16[256,256]{1,0:T(8,128)(2,1)}, u32[]{:S(2)}, u32[]{:S(2)}) collective-permute-start(bf16[256,256]{1,0:T(8,128)(2,1)} %get-tuple-element.133), channel_id=1, source_target_pairs={{0,3},{1,0},{2,1},{3,2},{4,7},{5,4},{6,5},{7,6},{8,11},{9,8},{10,9... | collective-permute-start | bytes 393224 | tf_op jit(solution)/shard_map/cond/branch_1_fun/ppermute | solution.py:403

commit v3 on v2

--- a/solution.py
+++ b/solution.py
@@ -13,7 +13,7 @@
 TILE = 128
 LOG2E = 1.4426950408889634
 DEAD = 1e30
-AHEAD = 2
+AHEAD = 3
 VMEM_LIMIT = 67043328
 LANES = 128
 WITHIN = 32
@@ -558,8 +558,8 @@
     if kind == "pack":
         return movers[:AHEAD] if number == 0 else []
     if kind == "join":
-        return movers[AHEAD : AHEAD + 1] if number == 0 else []
-    return movers[number + AHEAD + 1 : number + AHEAD + 2]
+        return []
+    return movers[number + AHEAD : number + AHEAD + 1]
 
 
 def kernel_order(groups):

time: 283 us -> 284 us (level)
  no operation moved by 1% of the time
where the time goes in v3:
time: 284 us; the launch traced here: 281 us
  Pallas kernels  109 us (38%)
  starting transfers between devices  81.4 us (29%)
  waiting for transfers between devices  79.4 us (28%)
  other arithmetic  5.85 us (2%)
    ppermute x23, waiting for transfers between devices, around(): return lax.ppermute(array, 'head', moves)  78.6 us
    pallas_call x5, Pallas kernels, attend(): pl.pallas_call(functools.partial(attend_body, group, whole, column), out_...  78.2 us
    ppermute x23, starting transfers between devices, around(): return lax.ppermute(array, 'head', moves)  45.3 us
    ppermute x10, starting transfers between devices, along(): lax.ppermute(array, 'ctx', [(i, i + shift) for i in range(count) if 0 <=...  29.7 us
    pallas_call x5, Pallas kernels, join(): pl.pallas_call(functools.partial(join_body, group), out_shape=jax.ShapeDt...  16 us
    pallas_call x2, Pallas kernels, pack(): pl.pallas_call(functools.partial(pack_body, groups), out_shape=outs, in_s...  8.26 us
    all_to_all x1, starting transfers between devices, sorted_heads(): lax.all_to_all(spread, ('ctx', 'head'), split_axis=0, concat_axis=0, tile...  6.38 us
    pallas_call x2, Pallas kernels, place_columns(): pl.pallas_call(functools.partial(place_body, groups, aliased), out_shape=...  6.16 us
  transfers between devices with their start and end apart: 34, of which 6 were waited for; matrix products, arithmetic and copies ran while one was open for 1% of the time, Pallas kernels for 35%

profile of v3, /device:TPU:5, one launch (start us, length us, event | category | flops | bytes accessed | tf_op | source)
XLA Modules:
  0.0 280.8 jit_solution(14362137667586412576)
XLA Ops:
  0.0 1.0 copy.39
  1.0 1.1 add_subtract_fusion.2
  2.2 1.4 fusion.10
  4.3 6.4 %all-to-all-start = ((s32[32,1,12]{2,1,0:T(1,128)}), s32[32,1,12]{2,1,0:T(1,128)S(1)}, u32[]{:S(2)}, u32[]{:S(2)}) async-start(s32[32,1,12]{2,1,0:T(1,128)} %broadcast_in_dim.20), calls=%async_computation | async-start | bytes 32768 | tf_op jit(solution)/shard_map/all_to_all | solution.py:475
  11.0 1.2 collective-permute-start.88
  12.2 2.2 collective-permute-start.89
  14.4 1.1 collective-permute-start.90
  21.1 259.4 %conditional.1 = (bf16[256,6144]{1,0:T(8,128)(2,1)}) conditional(s32[]{:T(128)} %clamp.3, (s32[]{:T(128)}, s32[48,48]{1,0:T(8,128)S(1)}, bf16[256,6144]{1,0:T(8,128)(2,1)}, bf16[256,6144]{1,0:T(8,128)(2,1)}, bf16[256,6144]{1,0:T(8,128)(2,1)}, /*index=5*/s32[48,8,128]{2,1,0:T(8,128)}, s32[]{:T(128)}, s32[48,48]{1,0:T(8,128)S(1)}, ...), branch_computations={%region_9.10_spmd, %region_10.11_spmd, %region_11.12_spmd} | conditional | flops 14495523840 | bytes 146305856 | solution.py:546
  22.0 5.3 %pack.8 = (bf16[3,256,512]{2,1,0:T(8,128)(2,1)}, bf16[3,256,384]{2,1,0:T(8,128)(2,1)}, bf16[3,256,384]{2,1,0:T(8,128)(2,1)}, bf16[3,256,384]{2,1,0:T(8,128)(2,1)...) custom-call(s32[1]{0:T(128)} %bitcast.1.place, ...), custom_call_target="tpu_custom_call" | custom-call | bytes 8650752 | tf_op jit(solution)/shard_map/cond/branch_1_fun/pack/pallas_call | solution.py:98
  27.3 3.1 %join.19.refs_1_ = bf16[2,256,1024]{2,1,0:T(8,128)(2,1)} custom-call(s32[1]{0:T(128)} %bitcast.1.place, s32[48]{0:T(128)} %select_reduce_fusion.1.order, bf16[256,6144]{1,0:T(8,128)(2,1)} %get-tuple-element.207.refs_1_.key_rows, bf16[256,6144]{1,0:T(8,128)(2,1)} %get-tuple-element.210.refs_2_.value_rows), custom_call_target="tpu_custom_call" | custom-call | bytes 2097152 | tf_op jit(solution)/shard_map/cond/branch_1_fun/join/pallas_call | solution.py:149
  30.4 3.5 %collective-permute-start.27 = (bf16[2,256,1024]{2,1,0:T(8,128)(2,1)}, bf16[2,256,1024]{2,1,0:T(8,128)(2,1)}, u32[]{:S(2)}, u32[]{:S(2)}) collective-permute-start(bf16[2,256,1024]{2,1,0:T(8,128)(2,1)} %join.19.refs_1_), channel_id=1, source_target_pairs={{0,4},{4,8},{8,12},{12,16},{16,20},{20,24},{24,28},{1,5},{5,9},{9,... | collective-permute-start | bytes 3145736 | tf_op jit(solution)/shard_map/cond/branch_1_fun/ppermute | solution.py:408
  33.9 1.9 collective-permute-start.28
  36.3 1.1 collective-permute-start.29
  37.7 41.0 %collective-permute-done.26.refs_0_ = bf16[3,256,512]{2,1,0:T(8,128)(2,1)} collective-permute-done((bf16[3,256,512]{2,1,0:T(8,128)(2,1)}, bf16[3,256,512]{2,1,0:T(8,128)(2,1)}, u32[]{:S(2)}, u32[]{:S(2)}) %collective-permute-start.26) | collective-permute-done | bytes 786464 | tf_op jit(solution)/shard_map/cond/branch_1_fun/ppermute | solution.py:403
  78.7 2.9 %pack.9 = (bf16[3,256,256]{2,1,0:T(8,128)(2,1)}, bf16[3,256,256]{2,1,0:T(8,128)(2,1)}, bf16[3,256,256]{2,1,0:T(8,128)(2,1)}) custom-call(s32[1]{0:T(128)} %bitcast.1.place, s32[48]{0:T(128)} %select_reduce_fusion.1.order, bf16[256,6144]{1,0:T(8,128)(2,1)} %get-tuple-element.204.refs_0_.queries, bf16[256,6144]{1,0:T(8,128)(2,1)} %get-tuple-element.207.refs_1_.key_rows, ...), custom_call_target="tpu_custom_call" | custom-call | bytes 2359296 | tf_op jit(solution)/shard_map/cond/branch_1_fun/pack/pallas_call | solution.py:98
  81.7 3.1 %join.20.refs_2_ = bf16[2,512,512]{2,1,0:T(8,128)(2,1)} custom-call(s32[1]{0:T(128)} %bitcast.1.place, s32[48]{0:T(128)} %select_reduce_fusion.1.order, bf16[256,6144]{1,0:T(8,128)(2,1)} %get-tuple-element.207.refs_1_.key_rows, bf16[256,6144]{1,0:T(8,128)(2,1)} %get-tuple-element.210.refs_2_.value_rows, bf16[3,256,512]{2,1,0:T(8,128)(2,1)} %collective-permute-done.26.refs_0_), custom_call_target="tpu_custom_call" | custom-call | bytes 2097152 | tf_op jit(solution)/shard_map/cond/branch_1_fun/join/pallas_call | solution.py:149
  84.7 5.6 %collective-permute-start.32 = (bf16[2,512,512]{2,1,0:T(8,128)(2,1)}, bf16[2,512,512]{2,1,0:T(8,128)(2,1)}, u32[]{:S(2)}, u32[]{:S(2)}) collective-permute-start(bf16[2,512,512]{2,1,0:T(8,128)(2,1)} %join.20.refs_2_), channel_id=1, source_target_pairs={{0,4},{4,8},{8,12},{12,16},{16,20},{20,24},{24,28},{1,5},{5,9},{9,... | collective-permute-start | bytes 3145736 | tf_op jit(solution)/shard_map/cond/branch_1_fun/ppermute | solution.py:408
  90.3 2.2 collective-permute-start.33
  92.5 12.5 %attend.19.refs_0_ = bf16[256,1024]{1,0:T(8,128)(2,1)} custom-call(s32[1]{0:T(128)} %bitcast.1.place, s32[48]{0:T(128)} %select_reduce_fusion.1.order, s32[48,8,128]{2,1,0:T(8,128)} %get-tuple-element.102.lists, bf16[256,6144]{1,0:T(8,128)(2,1)} %get-tuple-element.204.refs_0_.queries, bf16[2,256,1024]{2,1,0:T(8,128)(2,1)} %collective-permute-done.27.refs_0_, ...), custom_call_target="tpu_custom_call" | custom-call | flops 2415919104 | bytes 4194304 | tf_op jit(solution)/shard_map/cond/branch_1_fun/attend/pallas_call | solution.py:318
  105.0 3.4 %join.21.refs_4_ = bf16[2,1024,384]{2,1,0:T(8,128)(2,1)} custom-call(s32[1]{0:T(128)} %bitcast.1.place, s32[48]{0:T(128)} %select_reduce_fusion.1.order, bf16[256,6144]{1,0:T(8,128)(2,1)} %get-tuple-element.207.refs_1_.key_rows, bf16[256,6144]{1,0:T(8,128)(2,1)} %get-tuple-element.210.refs_2_.value_rows, ...), custom_call_target="tpu_custom_call" | custom-call | bytes 3145728 | tf_op jit(solution)/shard_map/cond/branch_1_fun/join/pallas_call | solution.py:149
  108.4 3.6 %collective-permute-start.37 = (bf16[2,1024,384]{2,1,0:T(8,128)(2,1)}, bf16[2,1024,384]{2,1,0:T(8,128)(2,1)}, u32[]{:S(2)}, u32[]{:S(2)}) collective-permute-start(bf16[2,1024,384]{2,1,0:T(8,128)(2,1)} %join.21.refs_4_), channel_id=1, source_target_pairs={{0,4},{4,8},{8,12},{12,16},{16,20},{20,24},{24,28},{1,5},{5,9},{9,... | collective-permute-start | bytes 4718600 | tf_op jit(solution)/shard_map/cond/branch_1_fun/ppermute | solution.py:408
  112.0 2.0 collective-permute-start.38
  114.0 1.8 collective-permute-start.34
  115.8 2.2 collective-permute-start.36
  118.0 13.4 %attend.20 = (bf16[256,512]{1,0:T(8,128)(2,1)}, bf16[256,512]{1,0:T(8,128)(2,1)}) custom-call(s32[1]{0:T(128)} %bitcast.1.place, s32[48]{0:T(128)} %select_reduce_fusion.1.order, s32[48,8,128]{2,1,0:T(8,128)} %get-tuple-element.102.lists, bf16[256,6144]{1,0:T(8,128)(2,1)} %get-tuple-element.204.refs_0_.queries, ...), custom_call_target="tpu_custom_call" | custom-call | flops 2415919104 | bytes 4194304 | tf_op jit(solution)/shard_map/cond/branch_1_fun/attend/pallas_call | solution.py:318
  131.4 25.3 %collective-permute-done.35.refs_1_ = bf16[3,256,384]{2,1,0:T(8,128)(2,1)} collective-permute-done((bf16[3,256,384]{2,1,0:T(8,128)(2,1)}, bf16[3,256,384]{2,1,0:T(8,128)(2,1)}, u32[]{:S(2)}, u32[]{:S(2)}) %collective-permute-start.35) | collective-permute-done | bytes 589856 | tf_op jit(solution)/shard_map/cond/branch_1_fun/ppermute | solution.py:403
  156.7 3.5 %join.22.refs_4_ = bf16[2,1024,384]{2,1,0:T(8,128)(2,1)} custom-call(s32[1]{0:T(128)} %bitcast.1.place, s32[48]{0:T(128)} %select_reduce_fusion.1.order, bf16[256,6144]{1,0:T(8,128)(2,1)} %get-tuple-element.207.refs_1_.key_rows, bf16[256,6144]{1,0:T(8,128)(2,1)} %get-tuple-element.210.refs_2_.value_rows, ...), custom_call_target="tpu_custom_call" | custom-call | bytes 3145728 | tf_op jit(solution)/shard_map/cond/branch_1_fun/join/pallas_call | solution.py:149
  160.2 3.6 %collective-permute-start.42 = (bf16[2,1024,384]{2,1,0:T(8,128)(2,1)}, bf16[2,1024,384]{2,1,0:T(8,128)(2,1)}, u32[]{:S(2)}, u32[]{:S(2)}) collective-permute-start(bf16[2,1024,384]{2,1,0:T(8,128)(2,1)} %join.22.refs_4_), channel_id=1, source_target_pairs={{0,4},{4,8},{8,12},{12,16},{16,20},{20,24},{24,28},{1,5},{5,9},{9,... | collective-permute-start | bytes 4718600 | tf_op jit(solution)/shard_map/cond/branch_1_fun/ppermute | solution.py:408
  163.8 1.9 collective-permute-start.43
  165.8 12.9 %collective-permute-start.39 = (bf16[3,256,256]{2,1,0:T(8,128)(2,1)}, bf16[3,256,256]{2,1,0:T(8,128)(2,1)}, u32[]{:S(2)}, u32[]{:S(2)}) collective-permute-start(bf16[3,256,256]{2,1,0:T(8,128)(2,1)} %get-tuple-element.114), channel_id=1, source_target_pairs={{0,1},{1,2},{2,3},{3,0},{4,5},{5,6},{6,7},{7,4},{8,9},{9,10},{10,1... | collective-permute-start | bytes 1179656 | tf_op jit(solution)/shard_map/cond/branch_1_fun/ppermute | solution.py:403
  179.2 1.6 collective-permute-start.41
  180.8 23.4 %attend.21 = (bf16[256,384]{1,0:T(8,128)(2,1)}, bf16[256,384]{1,0:T(8,128)(2,1)}, bf16[256,384]{1,0:T(8,128)(2,1)}, bf16[256,384]{1,0:T(8,128)(2,1)}) custom-call(s32[1]{0:T(128)} %bitcast.1.place, s32[48]{0:T(128)} %select_reduce_fusion.1.order, s32[48,8,128]{2,1,0:T(8,128)} %get-tuple-element.102.lists, ...), custom_call_target="tpu_custom_call" | custom-call | flops 3623878656 | bytes 6291456 | tf_op jit(solution)/shard_map/cond/branch_1_fun/attend/pallas_call | solution.py:318
  204.3 1.5 collective-permute-done.40.refs_1_
  205.7 3.0 %join.23.refs_4_ = bf16[2,1024,256]{2,1,0:T(8,128)(2,1)} custom-call(s32[1]{0:T(128)} %bitcast.1.place, s32[48]{0:T(128)} %select_reduce_fusion.1.order, bf16[256,6144]{1,0:T(8,128)(2,1)} %get-tuple-element.207.refs_1_.key_rows, bf16[256,6144]{1,0:T(8,128)(2,1)} %get-tuple-element.210.refs_2_.value_rows, ...), custom_call_target="tpu_custom_call" | custom-call | bytes 2097152 | tf_op jit(solution)/shard_map/cond/branch_1_fun/join/pallas_call | solution.py:149
  208.8 3.6 %collective-permute-start.44 = (bf16[2,1024,256]{2,1,0:T(8,128)(2,1)}, bf16[2,1024,256]{2,1,0:T(8,128)(2,1)}, u32[]{:S(2)}, u32[]{:S(2)}) collective-permute-start(bf16[2,1024,256]{2,1,0:T(8,128)(2,1)} %join.23.refs_4_), channel_id=1, source_target_pairs={{0,4},{4,8},{8,12},{12,16},{16,20},{20,24},{24,28},{1,5},{5,9},{9,... | collective-permute-start | bytes 3145736 | tf_op jit(solution)/shard_map/cond/branch_1_fun/ppermute | solution.py:408
  212.4 1.9 collective-permute-start.45
  214.3 8.7 %collective-permute-start.49 = (bf16[256,512]{1,0:T(8,128)(2,1)}, bf16[256,512]{1,0:T(8,128)(2,1)}, u32[]{:S(2)}, u32[]{:S(2)}) collective-permute-start(bf16[256,512]{1,0:T(8,128)(2,1)} %get-tuple-element.106), channel_id=1, source_target_pairs={{0,1},{1,0},{2,3},{3,2},{4,5},{5,4},{6,7},{7,6},{8,9},{9,8},{10,11... | collective-permute-start | bytes 786440 | tf_op jit(solution)/shard_map/cond/branch_1_fun/ppermute | solution.py:403
  223.1 1.7 collective-permute-start.51
  224.8 19.2 %attend.22 = (bf16[256,384]{1,0:T(8,128)(2,1)}, bf16[256,384]{1,0:T(8,128)(2,1)}, bf16[256,384]{1,0:T(8,128)(2,1)}, bf16[256,384]{1,0:T(8,128)(2,1)}) custom-call(s32[1]{0:T(128)} %bitcast.1.place, s32[48]{0:T(128)} %select_reduce_fusion.1.order, s32[48,8,128]{2,1,0:T(8,128)} %get-tuple-element.102.lists, ...), custom_call_target="tpu_custom_call" | custom-call | flops 3623878656 | bytes 6291456 | tf_op jit(solution)/shard_map/cond/branch_1_fun/attend/pallas_call | solution.py:318
  244.1 1.8 collective-permute-start.53
  245.9 1.2 collective-permute-start.54
  247.1 2.3 collective-permute-start.55
  249.4 9.6 %attend.23 = (bf16[256,256]{1,0:T(8,128)(2,1)}, bf16[256,256]{1,0:T(8,128)(2,1)}, bf16[256,256]{1,0:T(8,128)(2,1)}, bf16[256,256]{1,0:T(8,128)(2,1)}) custom-call(s32[1]{0:T(128)} %bitcast.1.place, s32[48]{0:T(128)} %select_reduce_fusion.1.order, s32[48,8,128]{2,1,0:T(8,128)} %get-tuple-element.102.lists, ...), custom_call_target="tpu_custom_call" | custom-call | flops 2415919104 | bytes 4194304 | tf_op jit(solution)/shard_map/cond/branch_1_fun/attend/pallas_call | solution.py:318
  260.0 3.1 %collective-permute-start.48 = (bf16[256,256]{1,0:T(8,128)(2,1)}, bf16[256,256]{1,0:T(8,128)(2,1)}, u32[]{:S(2)}, u32[]{:S(2)}) collective-permute-start(bf16[256,256]{1,0:T(8,128)(2,1)} %get-tuple-element.126), channel_id=1, source_target_pairs={{0,3},{1,0},{2,1},{3,2},{4,7},{5,4},{6,5},{7,6},{8,11},{9,8},{10,9... | collective-permute-start | bytes 393224 | tf_op jit(solution)/shard_map/cond/branch_1_fun/ppermute | solution.py:403
  263.1 4.7 %collective-permute-done.54.refs_9_ = bf16[256,384]{1,0:T(8,128)(2,1)} collective-permute-done((bf16[256,384]{1,0:T(8,128)(2,1)}, bf16[256,384]{1,0:T(8,128)(2,1)}, u32[]{:S(2)}, u32[]{:S(2)}) %collective-permute-start.54) | collective-permute-done | bytes 196640 | tf_op jit(solution)/shard_map/cond/branch_1_fun/ppermute | solution.py:403
  267.8 3.6 %place.8.refs_4_ = bf16[256,6144]{1,0:T(8,128)(2,1)} custom-call(s32[1]{0:T(128)} %bitcast.1.place, s32[48]{0:T(128)} %select_reduce_fusion.1.order, bf16[256,1024]{1,0:T(8,128)(2,1)} %attend.19.refs_0_, bf16[256,512]{1,0:T(8,128)(2,1)} %get-tuple-element.105.refs_1_, bf16[256,512]{1,0:T(8,128)(2,1)} %collective-permute-done.49.refs_2_, ...), custom_call_target="tpu_custom_call" | custom-call | bytes 5242880 | tf_op jit(solution)/shard_map/cond/branch_1_fun/place/pallas_call | solution.py:383
  271.4 6.2 %collective-permute-done.47.refs_2_ = bf16[256,256]{1,0:T(8,128)(2,1)} collective-permute-done((bf16[256,256]{1,0:T(8,128)(2,1)}, bf16[256,256]{1,0:T(8,128)(2,1)}, u32[]{:S(2)}, u32[]{:S(2)}) %collective-permute-start.47) | collective-permute-done | bytes 131104 | tf_op jit(solution)/shard_map/cond/branch_1_fun/ppermute | solution.py:403
  277.6 2.5 place.9
  (59 shorter events, 7.9 us)
Async XLA Ops:
  4.3 12.0 %all-to-all-start = ((s32[32,1,12]{2,1,0:T(1,128)}), s32[32,1,12]{2,1,0:T(1,128)S(1)}, u32[]{:S(2)}, u32[]{:S(2)}) async-start(s32[32,1,12]{2,1,0:T(1,128)} %broadcast_in_dim.20), calls=%async_computation | async-start | bytes 32768 | tf_op jit(solution)/shard_map/all_to_all | solution.py:475
  11.0 9.4 %collective-permute-start.88 = (s32[12,8,128]{2,1,0:T(8,128)S(1)}, s32[12,8,128]{2,1,0:T(8,128)S(1)}, u32[]{:S(2)}, u32[]{:S(2)}) collective-permute-start(s32[12,8,128]{2,1,0:T(8,128)S(1)} %pad.17), channel_id=1, source_target_pairs={{0,1},{1,2},{2,3},{3,0},{4,5},{5,6},{6,7},{7,4},{8,9},{9,10},{10,1... | collective-permute-start | bytes 147464 | tf_op jit(solution)/shard_map/ppermute | solution.py:403
  12.2 8.2 %collective-permute-start.89 = (s32[12,8,128]{2,1,0:T(8,128)S(1)}, s32[12,8,128]{2,1,0:T(8,128)S(1)}, u32[]{:S(2)}, u32[]{:S(2)}) collective-permute-start(s32[12,8,128]{2,1,0:T(8,128)S(1)} %pad.17), channel_id=1, source_target_pairs={{0,2},{1,3},{2,0},{3,1},{4,6},{5,7},{6,4},{7,5},{8,10},{9,11},{10,... | collective-permute-start | bytes 147464 | tf_op jit(solution)/shard_map/ppermute | solution.py:403
  14.4 6.0 %collective-permute-start.90 = (s32[12,8,128]{2,1,0:T(8,128)S(1)}, s32[12,8,128]{2,1,0:T(8,128)S(1)}, u32[]{:S(2)}, u32[]{:S(2)}) collective-permute-start(s32[12,8,128]{2,1,0:T(8,128)S(1)} %pad.17), channel_id=1, source_target_pairs={{0,3},{1,0},{2,1},{3,2},{4,7},{5,4},{6,5},{7,6},{8,11},{9,8},{10,9... | collective-permute-start | bytes 147464 | tf_op jit(solution)/shard_map/ppermute | solution.py:403
  30.4 54.3 %collective-permute-start.27 = (bf16[2,256,1024]{2,1,0:T(8,128)(2,1)}, bf16[2,256,1024]{2,1,0:T(8,128)(2,1)}, u32[]{:S(2)}, u32[]{:S(2)}) collective-permute-start(bf16[2,256,1024]{2,1,0:T(8,128)(2,1)} %join.19.refs_1_), channel_id=1, source_target_pairs={{0,4},{4,8},{8,12},{12,16},{16,20},{20,24},{24,28},{1,5},{5,9},{9,... | collective-permute-start | bytes 3145736 | tf_op jit(solution)/shard_map/cond/branch_1_fun/ppermute | solution.py:408
  33.9 56.4 %collective-permute-start.28 = (bf16[2,256,1024]{2,1,0:T(8,128)(2,1)}, bf16[2,256,1024]{2,1,0:T(8,128)(2,1)}, u32[]{:S(2)}, u32[]{:S(2)}) collective-permute-start(bf16[2,256,1024]{2,1,0:T(8,128)(2,1)} %join.19.refs_1_), channel_id=1, source_target_pairs={{4,0},{8,4},{12,8},{16,12},{20,16},{24,20},{28,24},{5,1},{9,5},{13... | collective-permute-start | bytes 3145736 | tf_op jit(solution)/shard_map/cond/branch_1_fun/ppermute | solution.py:408
  35.8 42.9 %collective-permute-start.26 = (bf16[3,256,512]{2,1,0:T(8,128)(2,1)}, bf16[3,256,512]{2,1,0:T(8,128)(2,1)}, u32[]{:S(2)}, u32[]{:S(2)}) collective-permute-start(bf16[3,256,512]{2,1,0:T(8,128)(2,1)} %get-tuple-element.88), channel_id=1, source_target_pairs={{0,1},{1,0},{2,3},{3,2},{4,5},{5,4},{6,7},{7,6},{8,9},{9,8},{10,11... | collective-permute-start | bytes 2359304 | tf_op jit(solution)/shard_map/cond/branch_1_fun/ppermute | solution.py:403
  36.3 68.7 %collective-permute-start.29 = (bf16[3,256,384]{2,1,0:T(8,128)(2,1)}, bf16[3,256,384]{2,1,0:T(8,128)(2,1)}, u32[]{:S(2)}, u32[]{:S(2)}) collective-permute-start(bf16[3,256,384]{2,1,0:T(8,128)(2,1)} %get-tuple-element.89), channel_id=1, source_target_pairs={{0,1},{1,2},{2,3},{3,0},{4,5},{5,6},{6,7},{7,4},{8,9},{9,10},{10,1... | collective-permute-start | bytes 1769480 | tf_op jit(solution)/shard_map/cond/branch_1_fun/ppermute | solution.py:403
  37.4 67.6 %collective-permute-start.30 = (bf16[3,256,384]{2,1,0:T(8,128)(2,1)}, bf16[3,256,384]{2,1,0:T(8,128)(2,1)}, u32[]{:S(2)}, u32[]{:S(2)}) collective-permute-start(bf16[3,256,384]{2,1,0:T(8,128)(2,1)} %get-tuple-element.90), channel_id=1, source_target_pairs={{0,2},{1,3},{2,0},{3,1},{4,6},{5,7},{6,4},{7,5},{8,10},{9,11},{10,... | collective-permute-start | bytes 1769480 | tf_op jit(solution)/shard_map/cond/branch_1_fun/ppermute | solution.py:403
  78.7 26.2 %collective-permute-start.31 = (bf16[3,256,384]{2,1,0:T(8,128)(2,1)}, bf16[3,256,384]{2,1,0:T(8,128)(2,1)}, u32[]{:S(2)}, u32[]{:S(2)}) collective-permute-start(bf16[3,256,384]{2,1,0:T(8,128)(2,1)} %get-tuple-element.91), channel_id=1, source_target_pairs={{0,3},{1,0},{2,1},{3,2},{4,7},{5,4},{6,5},{7,6},{8,11},{9,8},{10,9... | collective-permute-start | bytes 1769480 | tf_op jit(solution)/shard_map/cond/branch_1_fun/ppermute | solution.py:403
  84.7 31.1 %collective-permute-start.32 = (bf16[2,512,512]{2,1,0:T(8,128)(2,1)}, bf16[2,512,512]{2,1,0:T(8,128)(2,1)}, u32[]{:S(2)}, u32[]{:S(2)}) collective-permute-start(bf16[2,512,512]{2,1,0:T(8,128)(2,1)} %join.20.refs_2_), channel_id=1, source_target_pairs={{0,4},{4,8},{8,12},{12,16},{16,20},{20,24},{24,28},{1,5},{5,9},{9,... | collective-permute-start | bytes 3145736 | tf_op jit(solution)/shard_map/cond/branch_1_fun/ppermute | solution.py:408
  90.3 25.5 %collective-permute-start.33 = (bf16[2,512,512]{2,1,0:T(8,128)(2,1)}, bf16[2,512,512]{2,1,0:T(8,128)(2,1)}, u32[]{:S(2)}, u32[]{:S(2)}) collective-permute-start(bf16[2,512,512]{2,1,0:T(8,128)(2,1)} %join.20.refs_2_), channel_id=1, source_target_pairs={{4,0},{8,4},{12,8},{16,12},{20,16},{24,20},{28,24},{5,1},{9,5},{13... | collective-permute-start | bytes 3145736 | tf_op jit(solution)/shard_map/cond/branch_1_fun/ppermute | solution.py:408
  108.4 70.2 %collective-permute-start.37 = (bf16[2,1024,384]{2,1,0:T(8,128)(2,1)}, bf16[2,1024,384]{2,1,0:T(8,128)(2,1)}, u32[]{:S(2)}, u32[]{:S(2)}) collective-permute-start(bf16[2,1024,384]{2,1,0:T(8,128)(2,1)} %join.21.refs_4_), channel_id=1, source_target_pairs={{0,4},{4,8},{8,12},{12,16},{16,20},{20,24},{24,28},{1,5},{5,9},{9,... | collective-permute-start | bytes 4718600 | tf_op jit(solution)/shard_map/cond/branch_1_fun/ppermute | solution.py:408
  112.0 67.2 %collective-permute-start.38 = (bf16[2,1024,384]{2,1,0:T(8,128)(2,1)}, bf16[2,1024,384]{2,1,0:T(8,128)(2,1)}, u32[]{:S(2)}, u32[]{:S(2)}) collective-permute-start(bf16[2,1024,384]{2,1,0:T(8,128)(2,1)} %join.21.refs_4_), channel_id=1, source_target_pairs={{4,0},{8,4},{12,8},{16,12},{20,16},{24,20},{28,24},{5,1},{9,5},{13... | collective-permute-start | bytes 4718600 | tf_op jit(solution)/shard_map/cond/branch_1_fun/ppermute | solution.py:408
  114.0 17.4 %collective-permute-start.34 = (bf16[3,256,384]{2,1,0:T(8,128)(2,1)}, bf16[3,256,384]{2,1,0:T(8,128)(2,1)}, u32[]{:S(2)}, u32[]{:S(2)}) collective-permute-start(bf16[3,256,384]{2,1,0:T(8,128)(2,1)} %get-tuple-element.92), channel_id=1, source_target_pairs={{0,1},{1,2},{2,3},{3,0},{4,5},{5,6},{6,7},{7,4},{8,9},{9,10},{10,1... | collective-permute-start | bytes 1769480 | tf_op jit(solution)/shard_map/cond/branch_1_fun/ppermute | solution.py:403
  115.8 40.9 %collective-permute-start.35 = (bf16[3,256,384]{2,1,0:T(8,128)(2,1)}, bf16[3,256,384]{2,1,0:T(8,128)(2,1)}, u32[]{:S(2)}, u32[]{:S(2)}) collective-permute-start(bf16[3,256,384]{2,1,0:T(8,128)(2,1)} %get-tuple-element.93), channel_id=1, source_target_pairs={{0,2},{1,3},{2,0},{3,1},{4,6},{5,7},{6,4},{7,5},{8,10},{9,11},{10,... | collective-permute-start | bytes 1769480 | tf_op jit(solution)/shard_map/cond/branch_1_fun/ppermute | solution.py:403
  115.8 40.9 %collective-permute-start.36 = (bf16[3,256,384]{2,1,0:T(8,128)(2,1)}, bf16[3,256,384]{2,1,0:T(8,128)(2,1)}, u32[]{:S(2)}, u32[]{:S(2)}) collective-permute-start(bf16[3,256,384]{2,1,0:T(8,128)(2,1)} %get-tuple-element.94), channel_id=1, source_target_pairs={{0,3},{1,0},{2,1},{3,2},{4,7},{5,4},{6,5},{7,6},{8,11},{9,8},{10,9... | collective-permute-start | bytes 1769480 | tf_op jit(solution)/shard_map/cond/branch_1_fun/ppermute | solution.py:403
  160.2 62.8 %collective-permute-start.42 = (bf16[2,1024,384]{2,1,0:T(8,128)(2,1)}, bf16[2,1024,384]{2,1,0:T(8,128)(2,1)}, u32[]{:S(2)}, u32[]{:S(2)}) collective-permute-start(bf16[2,1024,384]{2,1,0:T(8,128)(2,1)} %join.22.refs_4_), channel_id=1, source_target_pairs={{0,4},{4,8},{8,12},{12,16},{16,20},{20,24},{24,28},{1,5},{5,9},{9,... | collective-permute-start | bytes 4718600 | tf_op jit(solution)/shard_map/cond/branch_1_fun/ppermute | solution.py:408
  163.8 59.3 %collective-permute-start.43 = (bf16[2,1024,384]{2,1,0:T(8,128)(2,1)}, bf16[2,1024,384]{2,1,0:T(8,128)(2,1)}, u32[]{:S(2)}, u32[]{:S(2)}) collective-permute-start(bf16[2,1024,384]{2,1,0:T(8,128)(2,1)} %join.22.refs_4_), channel_id=1, source_target_pairs={{4,0},{8,4},{12,8},{16,12},{20,16},{24,20},{28,24},{5,1},{9,5},{13... | collective-permute-start | bytes 4718600 | tf_op jit(solution)/shard_map/cond/branch_1_fun/ppermute | solution.py:408
  165.8 38.5 %collective-permute-start.39 = (bf16[3,256,256]{2,1,0:T(8,128)(2,1)}, bf16[3,256,256]{2,1,0:T(8,128)(2,1)}, u32[]{:S(2)}, u32[]{:S(2)}) collective-permute-start(bf16[3,256,256]{2,1,0:T(8,128)(2,1)} %get-tuple-element.114), channel_id=1, source_target_pairs={{0,1},{1,2},{2,3},{3,0},{4,5},{5,6},{6,7},{7,4},{8,9},{9,10},{10,1... | collective-permute-start | bytes 1179656 | tf_op jit(solution)/shard_map/cond/branch_1_fun/ppermute | solution.py:403
  178.6 27.1 %collective-permute-start.40 = (bf16[3,256,256]{2,1,0:T(8,128)(2,1)}, bf16[3,256,256]{2,1,0:T(8,128)(2,1)}, u32[]{:S(2)}, u32[]{:S(2)}) collective-permute-start(bf16[3,256,256]{2,1,0:T(8,128)(2,1)} %get-tuple-element.115), channel_id=1, source_target_pairs={{0,2},{1,3},{2,0},{3,1},{4,6},{5,7},{6,4},{7,5},{8,10},{9,11},{10,... | collective-permute-start | bytes 1179656 | tf_op jit(solution)/shard_map/cond/branch_1_fun/ppermute | solution.py:403
  179.2 26.5 %collective-permute-start.41 = (bf16[3,256,256]{2,1,0:T(8,128)(2,1)}, bf16[3,256,256]{2,1,0:T(8,128)(2,1)}, u32[]{:S(2)}, u32[]{:S(2)}) collective-permute-start(bf16[3,256,256]{2,1,0:T(8,128)(2,1)} %get-tuple-element.116), channel_id=1, source_target_pairs={{0,3},{1,0},{2,1},{3,2},{4,7},{5,4},{6,5},{7,6},{8,11},{9,8},{10,9... | collective-permute-start | bytes 1179656 | tf_op jit(solution)/shard_map/cond/branch_1_fun/ppermute | solution.py:403
  208.8 37.2 %collective-permute-start.44 = (bf16[2,1024,256]{2,1,0:T(8,128)(2,1)}, bf16[2,1024,256]{2,1,0:T(8,128)(2,1)}, u32[]{:S(2)}, u32[]{:S(2)}) collective-permute-start(bf16[2,1024,256]{2,1,0:T(8,128)(2,1)} %join.23.refs_4_), channel_id=1, source_target_pairs={{0,4},{4,8},{8,12},{12,16},{16,20},{20,24},{24,28},{1,5},{5,9},{9,... | collective-permute-start | bytes 3145736 | tf_op jit(solution)/shard_map/cond/branch_1_fun/ppermute | solution.py:408
  212.4 34.7 %collective-permute-start.45 = (bf16[2,1024,256]{2,1,0:T(8,128)(2,1)}, bf16[2,1024,256]{2,1,0:T(8,128)(2,1)}, u32[]{:S(2)}, u32[]{:S(2)}) collective-permute-start(bf16[2,1024,256]{2,1,0:T(8,128)(2,1)} %join.23.refs_4_), channel_id=1, source_target_pairs={{4,0},{8,4},{12,8},{16,12},{20,16},{24,20},{28,24},{5,1},{9,5},{13... | collective-permute-start | bytes 3145736 | tf_op jit(solution)/shard_map/cond/branch_1_fun/ppermute | solution.py:408
  214.3 29.7 %collective-permute-start.49 = (bf16[256,512]{1,0:T(8,128)(2,1)}, bf16[256,512]{1,0:T(8,128)(2,1)}, u32[]{:S(2)}, u32[]{:S(2)}) collective-permute-start(bf16[256,512]{1,0:T(8,128)(2,1)} %get-tuple-element.106), channel_id=1, source_target_pairs={{0,1},{1,0},{2,3},{3,2},{4,5},{5,4},{6,7},{7,6},{8,9},{9,8},{10,11... | collective-permute-start | bytes 786440 | tf_op jit(solution)/shard_map/cond/branch_1_fun/ppermute | solution.py:403
  223.0 21.1 %collective-permute-start.50 = (bf16[256,384]{1,0:T(8,128)(2,1)}, bf16[256,384]{1,0:T(8,128)(2,1)}, u32[]{:S(2)}, u32[]{:S(2)}) collective-permute-start(bf16[256,384]{1,0:T(8,128)(2,1)} %get-tuple-element.110), channel_id=1, source_target_pairs={{0,1},{1,2},{2,3},{3,0},{4,5},{5,6},{6,7},{7,4},{8,9},{9,10},{10,1... | collective-permute-start | bytes 589832 | tf_op jit(solution)/shard_map/cond/branch_1_fun/ppermute | solution.py:403
  223.1 36.0 %collective-permute-start.51 = (bf16[256,384]{1,0:T(8,128)(2,1)}, bf16[256,384]{1,0:T(8,128)(2,1)}, u32[]{:S(2)}, u32[]{:S(2)}) collective-permute-start(bf16[256,384]{1,0:T(8,128)(2,1)} %get-tuple-element.111), channel_id=1, source_target_pairs={{0,2},{1,3},{2,0},{3,1},{4,6},{5,7},{6,4},{7,5},{8,10},{9,11},{10,... | collective-permute-start | bytes 589832 | tf_op jit(solution)/shard_map/cond/branch_1_fun/ppermute | solution.py:403
  244.1 15.1 %collective-permute-start.52 = (bf16[256,384]{1,0:T(8,128)(2,1)}, bf16[256,384]{1,0:T(8,128)(2,1)}, u32[]{:S(2)}, u32[]{:S(2)}) collective-permute-start(bf16[256,384]{1,0:T(8,128)(2,1)} %get-tuple-element.112), channel_id=1, source_target_pairs={{0,3},{1,0},{2,1},{3,2},{4,7},{5,4},{6,5},{7,6},{8,11},{9,8},{10,9... | collective-permute-start | bytes 589832 | tf_op jit(solution)/shard_map/cond/branch_1_fun/ppermute | solution.py:403
  244.1 15.9 %collective-permute-start.53 = (bf16[256,384]{1,0:T(8,128)(2,1)}, bf16[256,384]{1,0:T(8,128)(2,1)}, u32[]{:S(2)}, u32[]{:S(2)}) collective-permute-start(bf16[256,384]{1,0:T(8,128)(2,1)} %get-tuple-element.119), channel_id=1, source_target_pairs={{0,1},{1,2},{2,3},{3,0},{4,5},{5,6},{6,7},{7,4},{8,9},{9,10},{10,1... | collective-permute-start | bytes 589832 | tf_op jit(solution)/shard_map/cond/branch_1_fun/ppermute | solution.py:403
  245.9 21.8 %collective-permute-start.54 = (bf16[256,384]{1,0:T(8,128)(2,1)}, bf16[256,384]{1,0:T(8,128)(2,1)}, u32[]{:S(2)}, u32[]{:S(2)}) collective-permute-start(bf16[256,384]{1,0:T(8,128)(2,1)} %get-tuple-element.120), channel_id=1, source_target_pairs={{0,2},{1,3},{2,0},{3,1},{4,6},{5,7},{6,4},{7,5},{8,10},{9,11},{10,... | collective-permute-start | bytes 589832 | tf_op jit(solution)/shard_map/cond/branch_1_fun/ppermute | solution.py:403
  247.1 20.6 %collective-permute-start.55 = (bf16[256,384]{1,0:T(8,128)(2,1)}, bf16[256,384]{1,0:T(8,128)(2,1)}, u32[]{:S(2)}, u32[]{:S(2)}) collective-permute-start(bf16[256,384]{1,0:T(8,128)(2,1)} %get-tuple-element.121), channel_id=1, source_target_pairs={{0,3},{1,0},{2,1},{3,2},{4,7},{5,4},{6,5},{7,6},{8,11},{9,8},{10,9... | collective-permute-start | bytes 589832 | tf_op jit(solution)/shard_map/cond/branch_1_fun/ppermute | solution.py:403
  259.1 12.4 %collective-permute-start.46 = (bf16[256,256]{1,0:T(8,128)(2,1)}, bf16[256,256]{1,0:T(8,128)(2,1)}, u32[]{:S(2)}, u32[]{:S(2)}) collective-permute-start(bf16[256,256]{1,0:T(8,128)(2,1)} %get-tuple-element.124), channel_id=1, source_target_pairs={{0,1},{1,2},{2,3},{3,0},{4,5},{5,6},{6,7},{7,4},{8,9},{9,10},{10,1... | collective-permute-start | bytes 393224 | tf_op jit(solution)/shard_map/cond/branch_1_fun/ppermute | solution.py:403
  259.1 18.4 %collective-permute-start.47 = (bf16[256,256]{1,0:T(8,128)(2,1)}, bf16[256,256]{1,0:T(8,128)(2,1)}, u32[]{:S(2)}, u32[]{:S(2)}) collective-permute-start(bf16[256,256]{1,0:T(8,128)(2,1)} %get-tuple-element.125), channel_id=1, source_target_pairs={{0,2},{1,3},{2,0},{3,1},{4,6},{5,7},{6,4},{7,5},{8,10},{9,11},{10,... | collective-permute-start | bytes 393224 | tf_op jit(solution)/shard_map/cond/branch_1_fun/ppermute | solution.py:403
  260.0 17.6 %collective-permute-start.48 = (bf16[256,256]{1,0:T(8,128)(2,1)}, bf16[256,256]{1,0:T(8,128)(2,1)}, u32[]{:S(2)}, u32[]{:S(2)}) collective-permute-start(bf16[256,256]{1,0:T(8,128)(2,1)} %get-tuple-element.126), channel_id=1, source_target_pairs={{0,3},{1,0},{2,1},{3,2},{4,7},{5,4},{6,5},{7,6},{8,11},{9,8},{10,9... | collective-permute-start | bytes 393224 | tf_op jit(solution)/shard_map/cond/branch_1_fun/ppermute | solution.py:403
